TPU v7x, 256 devices: a whole 4x4x8 slice. The times are simulated.
256 devices in a mesh: pool: 8 (over z), expert: 32 (over x, y, core).
Axes of the slice: x: 4, y: 4, z: 8, core: 2. Of those that a mesh axis runs over, the one named last changes fastest.
Arguments:
- residual: bfloat16 [32, 512, 4096], P('expert', 'pool'), may hold values from -36 to 36
- queries: bfloat16 [32, 512, 4096], P('expert', 'pool'), may hold values from -8 to 8
- fresh_kv: bfloat16 [32, 512, 512], P('expert', 'pool'), may hold values from -16 to 16
- pool_cache: bfloat16 [512, 16, 512], P('pool'), may hold values from -16 to 16
- hit_blocks: int32 [32, 16], P('expert'), may hold values from 0 to 511, as said below
- norm_gain: float32 [4096], replicated, may hold values from 0.1 to 1.9
- route_ids: int32 [32, 512, 8], P('expert', 'pool'), may hold values from 0 to 127, all different within a row; in each aligned block of 64 rows (0 to 63, 64 to 127, ..., all dimensions but the last counted through in order) at most 5 rows name the same one
- route_logits: float32 [32, 512, 8], P('expert', 'pool'), may hold values from -310 to 310
- w_gate: bfloat16 [256, 4096, 384], P(('pool', 'expert')), may hold values from -0.25 to 0.25
- w_up: bfloat16 [256, 4096, 384], P(('pool', 'expert')), may hold values from -0.25 to 0.25
- w_down: bfloat16 [256, 384, 4096], P(('pool', 'expert')), may hold values from -0.625 to 0.625
Outputs:
- attended: bfloat16 [32, 512, 4096], P('expert', 'pool')
- layer_out: bfloat16 [32, 512, 4096], P('expert', 'pool')
Inputs may be any that keep to these rules, and one draw needn't show every extreme that they name: `hit_blocks`: each request's 16 block ids are distinct; block b is held by pool index b // 64; one pool index holds exactly 4 of a request's blocks, and the others share the rest as evenly as they can. `route_ids`: among the 64 tokens of one device, each expert is chosen by at most 5 of them; some expert is chosen by exactly 5 of some device's tokens.
All inputs are finite; a program needn't handle non-finite values.
Results may differ from a plain program's by a relative error of at most 0.017.
Values may be sent and summed in bfloat16 or wider, within the bound.
No kernel may reach another device: no remote copies, remote signals or barrier semaphores. Data moves between devices by JAX's collectives and lax.ppermute only.
A program may use at most 192 MiB of HBM per device.

v0:
```python
import jax
import jax.numpy as jnp
from jax import lax
from jax.sharding import PartitionSpec as P

HD = 128
HOT = 4


MASKED = -1e30
EPSILON = 1e-06


def absorb(softmax_state, block_rows, visible, query_heads):
    run_max, run_sum, run_acc = softmax_state
    heads_kv = query_heads.shape[1]
    head_width = query_heads.shape[3]
    key_count = block_rows.shape[0]
    key_mat = block_rows[:, : heads_kv * head_width].reshape(key_count, heads_kv, head_width)
    values = block_rows[:, heads_kv * head_width :].reshape(key_count, heads_kv, head_width)
    scores = jnp.einsum(
        "tkgd,nkd->kgtn", query_heads, key_mat, preferred_element_type=jnp.float32
    ) * head_width ** (-0.5)
    scores = jnp.where(visible[None, None], scores, MASKED)
    newtop = jnp.maximum(run_max, jnp.max(scores, axis=-1))
    rescale = jnp.exp(run_max - newtop)
    weights = jnp.where(visible[None, None], jnp.exp(scores - newtop[..., None]), 0.0)
    run_sum = run_sum * rescale + jnp.sum(weights, axis=-1)
    weighted = jnp.einsum(
        "kgtn,nkd->kgtd", weights.astype(jnp.bfloat16), values, preferred_element_type=jnp.float32
    )
    return (newtop, run_sum, run_acc * rescale[..., None] + weighted)


def shards(
    residual,
    queries,
    fresh_kv,
    pool_cache,
    hit_blocks,
    norm_gain,
    route_ids,
    route_logits,
    w_gate,
    w_up,
    w_down,
):
    pool_count = lax.axis_size("pool")
    expert_count = lax.axis_size("expert")
    pool_rank = lax.axis_index("pool")
    tok_dev = queries.shape[1]
    model_width = residual.shape[2]
    kv_width = pool_cache.shape[2]
    heads_kv = kv_width // (2 * HD)
    group_size = queries.shape[2] // (heads_kv * HD)
    query_heads = queries[0].reshape(tok_dev, heads_kv, group_size, HD)
    state_shape = (heads_kv, group_size, tok_dev)
    softmax_state = (
        jnp.full(state_shape, MASKED, jnp.float32),
        jnp.zeros(state_shape, jnp.float32),
        jnp.zeros(state_shape + (HD,), jnp.float32),
    )
    hit_list = hit_blocks[0]
    per_owner = pool_cache.shape[0]
    block_len = pool_cache.shape[1]
    owners = hit_list // per_owner
    is_owned = owners == pool_rank
    owner_counts = jnp.sum(
        (owners[:, None] == jnp.arange(pool_count, dtype=jnp.int32)[None, :]).astype(jnp.int32),
        axis=0,
    )
    query_pos = pool_rank * tok_dev + jnp.arange(tok_dev, dtype=jnp.int32)
    slot_rank = jnp.cumsum(is_owned.astype(jnp.int32)) - 1
    picked = (slot_rank[None, :] == jnp.arange(HOT, dtype=jnp.int32)[:, None]) & is_owned[None, :]
    local_ids = jnp.sum(jnp.where(picked, hit_list[None, :] % per_owner, 0), axis=1)
    packed = pool_cache[local_ids]
    part_rows = lax.all_gather(packed, "pool", axis=0, tiled=True)
    slot_index = jnp.arange(part_rows.shape[0], dtype=jnp.int32)
    source_owner = slot_index // HOT
    owner_have = jnp.sum(
        jnp.where(
            source_owner[:, None] == jnp.arange(pool_count, dtype=jnp.int32)[None, :],
            owner_counts[None, :],
            0,
        ),
        axis=1,
    )
    is_valid = slot_index % HOT < owner_have
    row_valid = jnp.repeat(is_valid, block_len)
    visible = jnp.broadcast_to(row_valid[None, :], (tok_dev, row_valid.shape[0]))
    result = absorb(softmax_state, part_rows.reshape(-1, kv_width), visible, query_heads)
    part_rows = lax.all_gather(fresh_kv, "pool", axis=1, tiled=True)
    key_pos = jnp.arange(part_rows.shape[1], dtype=jnp.int32)
    visible = key_pos[None, :] <= query_pos[:, None]
    softmax_state = absorb(result, part_rows.reshape(-1, kv_width), visible, query_heads)
    run_max, run_sum, run_acc = softmax_state
    attn_mix = run_acc / run_sum[..., None]
    attended = (
        jnp.transpose(attn_mix, (2, 0, 1, 3))
        .reshape(1, tok_dev, heads_kv * group_size * HD)
        .astype(jnp.bfloat16)
    )
    resid = lax.optimization_barrier(
        (residual[0].astype(jnp.float32) + attended[0].astype(jnp.float32)).astype(jnp.bfloat16)
    )
    resid_wide = resid.astype(jnp.float32)
    inv_rms = lax.rsqrt(jnp.mean(resid_wide * resid_wide, axis=-1, keepdims=True) + EPSILON)
    normed = (resid_wide * inv_rms * norm_gain).astype(jnp.bfloat16)
    top_count = route_ids.shape[2]
    expert_total = pool_count * expert_count // 2
    capacity = max(2, 5 * tok_dev * top_count // (4 * expert_total))
    chosen = route_ids[0].reshape(-1)
    onehot = (chosen[:, None] == jnp.arange(expert_total, dtype=jnp.int32)[None, :]).astype(
        jnp.int32
    )
    ranking = jnp.sum((jnp.cumsum(onehot, axis=0) - 1) * onehot, axis=1)
    slot_pos = chosen * capacity + ranking
    filler = jnp.arange(tok_dev * top_count, dtype=jnp.int32) // top_count + 1
    source_row = jnp.zeros((expert_total * capacity,), jnp.int32).at[slot_pos].set(filler)
    outgoing = jnp.where(
        (source_row > 0)[:, None],
        normed[jnp.maximum(source_row - 1, 0)],
        jnp.zeros((), jnp.bfloat16),
    )
    outgoing = outgoing.reshape(expert_total, capacity, model_width)
    doubled = jnp.repeat(outgoing, 2, axis=0).reshape(
        pool_count, expert_count, capacity, model_width
    )
    arrived = lax.all_to_all(
        lax.all_to_all(doubled, "pool", split_axis=0, concat_axis=0, tiled=True),
        "expert",
        split_axis=1,
        concat_axis=1,
        tiled=True,
    )
    arrived_rows = arrived.reshape(-1, model_width)
    gate_act = jnp.dot(arrived_rows, w_gate[0], preferred_element_type=jnp.float32)
    up_act = jnp.dot(arrived_rows, w_up[0], preferred_element_type=jnp.float32)
    hidden = (jax.nn.silu(gate_act) * up_act).astype(jnp.bfloat16)
    partial_value = jnp.dot(hidden, w_down[0], preferred_element_type=jnp.float32).astype(
        jnp.bfloat16
    )
    partial_value = partial_value.reshape(pool_count, expert_count, capacity, model_width)
    returned = lax.all_to_all(
        lax.all_to_all(partial_value, "pool", split_axis=0, concat_axis=0, tiled=True),
        "expert",
        split_axis=1,
        concat_axis=1,
        tiled=True,
    )
    summed = jnp.sum(
        returned.reshape(expert_total, 2, capacity, model_width).astype(jnp.float32), axis=1
    )
    summed = summed.reshape(expert_total * capacity, model_width)
    route_weight = jax.nn.softmax(route_logits[0], axis=-1)
    pulled = summed[slot_pos].reshape(tok_dev, top_count, model_width)
    expert_mix = jnp.sum(pulled * route_weight[..., None], axis=1)
    layer_out = (resid_wide + expert_mix).astype(jnp.bfloat16).reshape(1, tok_dev, model_width)
    return (attended, layer_out)


def solution(mesh):
    placed = (
        P("expert", "pool", None),
        P("expert", "pool", None),
        P("expert", "pool", None),
        P("pool", None, None),
        P("expert", None),
        P(),
        P("expert", "pool", None),
        P("expert", "pool", None),
        P(("pool", "expert"), None, None),
        P(("pool", "expert"), None, None),
        P(("pool", "expert"), None, None),
    )
    return jax.shard_map(
        shards,
        mesh=mesh,
        in_specs=placed,
        out_specs=(P("expert", "pool", None), P("expert", "pool", None)),
        check_vma=False,
    )
```

profile of v0, /device:TPU:12, one launch (start us, length us, event | category | flops | bytes accessed | tf_op | source)
XLA Modules:
  0.0 1160.7 jit_solution(5845299903642644287)
XLA Ops:
  11.3 29.1 %all-gather = bf16[32,16,512]{2,1,0:T(8,128)(2,1)S(1)} all-gather(bf16[4,16,512]{2,1,0:T(8,128)(2,1)S(1)} %gather_fusion), channel_id=2, replica_groups=mesh['pool'=8,'expert'=32] {'pool'}, dimensions={0}, use_global_device_ids=true | all-gather | bytes 589824 | tf_op jit(solution)/shard_map/all_gather | solution.py:77
  46.1 27.5 %all_gather.7 = bf16[1,512,512]{2,1,0:T(8,128)(2,1)} all-gather(bf16[1,64,512]{2,1,0:T(8,128)(2,1)S(1)} %copy-done.11), channel_id=1, replica_groups=mesh['pool'=8,'expert'=32] {'pool'}, dimensions={1}, use_global_device_ids=true | all-gather | bytes 589824 | tf_op jit(solution)/shard_map/all_gather | solution.py:92
  91.2 12.8 %gather_fusion.1 = bf16[640,4096]{1,0:T(8,128)(2,1)} fusion(bf16[64,4096]{1,0:T(8,128)(2,1)} %fusion.46, s32[1024]{0:T(1024)S(1)} %pad_clamp_fusion.1), kind=kCustom, calls=%fused_computation.1 | custom fusion | bytes 10488320 | tf_op jit(solution)/shard_map/gather | solution.py:122
  126.8 10.9 broadcast_in_dim.136
  137.7 16.0 %reshape_reshape.3 = bf16[8,32,5,4096]{3,1,0,2:T(8,128)(2,1)} reshape(bf16[128,2,5,4096]{3,1,0,2:T(2,128)(2,1)} %broadcast_in_dim.136) | data formatting | bytes 20971520 | tf_op jit(solution)/shard_map/reshape;reshape | solution.py:126
  153.7 9.5 copy.143
  163.2 225.3 %all_to_all.20 = bf16[8,32,5,4096]{3,1,2,0:T(8,128)(2,1)} all-to-all(bf16[8,32,5,4096]{3,1,2,0:T(8,128)(2,1)} %copy.143), channel_id=1, replica_groups=mesh['pool'=8,'expert'=32] {'pool'}, dimensions={0} | all-to-all | bytes 20971520 | tf_op jit(solution)/shard_map/all_to_all | solution.py:130
  388.5 13.5 %copy.144 = bf16[8,32,5,4096]{3,0,2,1:T(8,128)(2,1)} copy(bf16[8,32,5,4096]{3,1,2,0:T(8,128)(2,1)} %all_to_all.20) | data formatting | bytes 20971520 | tf_op jit(solution)/shard_map/all_to_all | solution.py:130
  402.0 122.8 %all_to_all.21 = bf16[8,32,5,4096]{3,0,2,1:T(8,128)(2,1)S(1)} all-to-all(bf16[8,32,5,4096]{3,0,2,1:T(8,128)(2,1)} %copy.144), channel_id=1, replica_groups=mesh['pool'=8,'expert'=32] {'expert'}, dimensions={1} | all-to-all | bytes 20971520 | tf_op jit(solution)/shard_map/all_to_all | solution.py:129
  524.9 21.3 %copy.145 = bf16[8,32,5,4096]{3,2,1,0:T(8,128)(2,1)} copy(bf16[8,32,5,4096]{3,0,2,1:T(8,128)(2,1)S(1)} %all_to_all.21) | data formatting | bytes 20971520 | tf_op jit(solution)/shard_map/all_to_all | solution.py:129
  546.1 16.8 %reshape.314 = bf16[1280,4096]{1,0:T(8,128)(2,1)} reshape(bf16[8,32,5,4096]{3,2,1,0:T(8,128)(2,1)} %copy.145) | data formatting | bytes 20971520 | tf_op jit(solution)/shard_map/reshape | solution.py:136
  563.0 10.2 fusion.6
  573.1 17.3 %convolution_convert_fusion = bf16[1280,4096]{1,0:T(8,128)(2,1)} fusion(bf16[1,384,4096]{2,1,0:T(8,128)(2,1)S(1)} %copy-done, bf16[1280,4096]{1,0:T(8,128)(2,1)} %reshape.314, bf16[1,4096,384]{2,1,0:T(8,128)(2,1)} %param.20, f32[1280,384]{1,0:T(8,128)} %fusion.6), kind=kOutput, calls=%fused_computation.4 | convolution fusion | flops 8061255680 | bytes 29229056 | tf_op jit(solution)/shard_map/dot_general | solution.py:140
  590.5 15.5 %reshape.315 = bf16[8,32,5,4096]{3,2,1,0:T(8,128)(2,1)} reshape(bf16[1280,4096]{1,0:T(8,128)(2,1)} %convolution_convert_fusion) | data formatting | bytes 20971520 | tf_op jit(solution)/shard_map/reshape | solution.py:143
  606.0 8.9 copy.146
  614.9 235.2 %all_to_all.22 = bf16[8,32,5,4096]{3,1,2,0:T(8,128)(2,1)} all-to-all(bf16[8,32,5,4096]{3,1,2,0:T(8,128)(2,1)S(1)} %copy.146), channel_id=1, replica_groups=mesh['pool'=8,'expert'=32] {'pool'}, dimensions={0} | all-to-all | bytes 20971520 | tf_op jit(solution)/shard_map/all_to_all | solution.py:145
  850.1 13.7 %copy.147 = bf16[8,32,5,4096]{3,0,2,1:T(8,128)(2,1)} copy(bf16[8,32,5,4096]{3,1,2,0:T(8,128)(2,1)} %all_to_all.22) | data formatting | bytes 20971520 | tf_op jit(solution)/shard_map/all_to_all | solution.py:145
  874.2 163.7 %all-to-all-done.3 = bf16[8,32,5,4096]{3,0,2,1:T(8,128)(2,1)} async-done(((bf16[8,32,5,4096]{3,0,2,1:T(8,128)(2,1)}), bf16[8,32,5,4096]{3,0,2,1:T(8,128)(2,1)}, u32[]{:S(2)}, u32[]{:S(2)}) %all-to-all-start.3) | async-done | bytes 10485792 | tf_op jit(solution)/shard_map/all_to_all | solution.py:144
  1037.9 17.2 %copy.148 = f32[8,32,5,4096]{3,1,0,2:T(8,128)} copy(bf16[8,32,5,4096]{3,0,2,1:T(8,128)(2,1)} %all-to-all-done.3) | data formatting | bytes 31457280 | tf_op jit(solution)/shard_map/convert_element_type | solution.py:152
  1055.1 24.8 %reshape.322 = f32[128,2,5,4096]{3,1,0,2:T(2,128)} reshape(f32[8,32,5,4096]{3,1,0,2:T(8,128)} %copy.148) | data formatting | bytes 41943040 | tf_op jit(solution)/shard_map/convert_element_type | solution.py:152
  1079.8 31.5 %reduce_sum.109 = f32[128,5,4096]{2,0,1:T(8,128)} reduce(f32[128,2,5,4096]{3,1,0,2:T(2,128)} %reshape.322, f32[]{:T(128)} %constant.115.clone.1), dimensions={1}, to_apply=%region_13.14 | reduce | flops 2621440 | bytes 31457284 | tf_op jit(solution)/shard_map/reduce_sum | solution.py:151
  1111.4 16.2 %copy.149 = f32[128,5,4096]{2,1,0:T(8,128)} copy(f32[128,5,4096]{2,0,1:T(8,128)} %reduce_sum.109) | data formatting | bytes 20971520 | tf_op jit(solution)/shard_map/reduce_sum | solution.py:151
  1127.5 12.0 %reshape.316 = f32[640,4096]{1,0:T(8,128)} reshape(f32[128,5,4096]{2,1,0:T(8,128)} %copy.149) | data formatting | bytes 20971520 | tf_op jit(solution)/shard_map/reshape | solution.py:154
  1139.6 13.2 %gather_fusion.2 = f32[512,4096]{1,0:T(8,128)} fusion(f32[640,4096]{1,0:T(8,128)} %reshape.316, s32[1024]{0:T(1024)S(1)} %pad_clamp_fusion), kind=kCustom, calls=%fused_computation.2 | custom fusion | bytes 16779264 | tf_op jit(solution)/shard_map/gather | solution.py:156
  (99 shorter events, 74.2 us)
Async XLA Ops:
  0.6 572.5 %copy-start = (bf16[1,384,4096]{2,1,0:T(8,128)(2,1)S(1)}, bf16[1,384,4096]{2,1,0:T(8,128)(2,1)}, u32[]{:S(2)}) copy-start(bf16[1,384,4096]{2,1,0:T(8,128)(2,1)} %param.21) | copy-start | bytes 9437188
  0.6 45.4 %copy-start.11 = (bf16[1,64,512]{2,1,0:T(8,128)(2,1)S(1)}, bf16[1,64,512]{2,1,0:T(8,128)(2,1)}, u32[]{:S(2)}) copy-start(bf16[1,64,512]{2,1,0:T(8,128)(2,1)} %param.13) | copy-start | bytes 196612
  79.3 2.0 copy-start.4
  79.3 2.0 copy-start.7
  79.3 3.0 copy-start.10
  83.4 2.9 copy-start.9
  86.3 2.4 copy-start.8
  88.3 1.1 copy-start.5
  88.3 1.9 copy-start.13
  89.4 0.8 copy-start.2
  863.8 8.8 copy-start.6
  863.8 9.2 copy-start.12
  863.8 174.0 %all-to-all-start.3 = ((bf16[8,32,5,4096]{3,0,2,1:T(8,128)(2,1)}), bf16[8,32,5,4096]{3,0,2,1:T(8,128)(2,1)}, u32[]{:S(2)}, u32[]{:S(2)}) async-start(bf16[8,32,5,4096]{3,0,2,1:T(8,128)(2,1)} %copy.147), calls=%async_computation.3 | async-start | bytes 20971520 | tf_op jit(solution)/shard_map/all_to_all | solution.py:144
  1139.6 20.6 %copy-start.1 = (bf16[1,384,4096]{2,1,0:T(8,128)(2,1)S(1)}, bf16[1,384,4096]{2,1,0:T(8,128)(2,1)}, u32[]{:S(2)}) copy-start(bf16[1,384,4096]{2,1,0:T(8,128)(2,1)} %param.21) | copy-start | bytes 9437188
  1152.8 6.5 copy-start.3
where the time goes:
time: 1170 us; the launch traced here: 1160 us
  blocking collectives  640 us (55%)
  local copies, waits for them, and re-layouts  255 us (22%)
  waiting for transfers between devices  164 us (14%)
  other arithmetic  57.7 us (5%)
  matrix products  33.7 us (3%)
    all_to_all x1, blocking collectives, shards(): lax.all_to_all(partial_value, 'pool', split_axis=0, concat_axis=0, tiled=...  235 us
    all_to_all x1, blocking collectives, shards(): lax.all_to_all(doubled, 'pool', split_axis=0, concat_axis=0, tiled=True)  225 us
    all_to_all x1, waiting for transfers between devices, shards(): lax.all_to_all(lax.all_to_all(partial_value, 'pool', split_axis=0, concat...  164 us
    all_to_all x1, blocking collectives, shards(): lax.all_to_all(lax.all_to_all(doubled, 'pool', split_axis=0, concat_axis=...  123 us
    convert_element_type x2, local copies, waits for them, and re-layouts, shards(): returned.reshape(expert_total, 2, capacity, model_width).astype(jnp.float32)  42 us
    reduce_sum x1, other arithmetic, shards(): jnp.sum(returned.reshape(expert_total, 2, capacity, model_width).astype(j...  31.5 us
    all_gather x1, blocking collectives, shards(): part_rows = lax.all_gather(packed, 'pool', axis=0, tiled=True)  29.1 us
    all_gather x1, blocking collectives, shards(): part_rows = lax.all_gather(fresh_kv, 'pool', axis=1, tiled=True)  27.5 us
  transfers between devices with their start and end apart: 1, of which 1 were waited for; matrix products, arithmetic and copies ran while one was open for 0% of the time, Pallas kernels for 0%

commit v1 on v0

v1 whole, which is shorter than its diff:
```python
import jax
import jax.numpy as jnp
from jax import lax
from jax.experimental import pallas as pl
from jax.experimental.pallas import tpu as pltpu
from jax.sharding import Mesh, PartitionSpec as P

HD = 128
HOT = 4
MOST = 5
META = 128
MASKED = -1e30
EPSILON = 1e-06
F32 = jnp.float32
BF16 = jnp.bfloat16
VMEM_LIMIT = 56 * 1024 * 1024

SMEM = pl.BlockSpec(memory_space=pltpu.SMEM)
VMEM = pl.BlockSpec(memory_space=pltpu.VMEM)


def params(**kw):
    return pltpu.CompilerParams(vmem_limit_bytes=VMEM_LIMIT, **kw)


def gather_kernel(rank_ref, hit_ref, cache_ref, fresh_ref, ids_ref, logit_ref, out_ref):
    rank = rank_ref[0]
    held, block, width = cache_ref.shape
    out_ref[:, :width] = jnp.zeros((out_ref.shape[0], width), BF16)
    out_ref[:, width : 2 * width] = fresh_ref[...]
    count = jnp.int32(0)
    for i in range(hit_ref.shape[1]):
        hit = hit_ref[0, i]
        mine = lax.div(hit, held) == rank
        row = pl.multiple_of(jnp.minimum(count, HOT - 1) * block, block)
        local = lax.rem(hit, held)

        @pl.when(mine)
        def _():
            out_ref[pl.ds(row, block), :width] = cache_ref[local]

        count = count + mine.astype(jnp.int32)
    ids = ids_ref[...].astype(F32)
    logits = logit_ref[...]
    grown = jnp.exp(logits - jnp.max(logits, axis=-1, keepdims=True))
    weight = grown / jnp.sum(grown, axis=-1, keepdims=True)
    high = weight.astype(BF16).astype(F32)
    low = weight - high
    tok, top = ids.shape
    lane = lax.broadcasted_iota(jnp.int32, (tok, META), 1)
    meta = jnp.zeros((tok, META), F32)
    for part, values in enumerate((ids, high, low)):
        for j in range(top):
            meta = jnp.where(lane == part * top + j, values[:, j : j + 1], meta)
    out_ref[:, 2 * width :] = meta.astype(BF16)


def place_ring(rank, pools, tok, pieces, store):
    store(rank * tok, pieces[0][...])
    half = pools // 2
    for s in range(1, half):
        store(lax.rem(rank + pools - s, pools) * tok, pieces[2 * s - 1][...])
        store(lax.rem(rank + s, pools) * tok, pieces[2 * s][...])
    far = lax.rem(rank + half, pools) * tok
    store(far, pieces[2 * half - 1][...])
    store(far + tok // 2, pieces[2 * half][...])


def attend_kernel(rank_ref, hit_ref, gain_ref, query_ref, residual_ref, *refs, pools, held):
    pieces = refs[: pools + 1]
    attended_ref, resid_ref, normed_ref, meta_ref, part_ref, kv_ref, bias_ref = refs[pools + 1 :]
    rank = rank_ref[0]
    tok, model = query_ref.shape
    hits = hit_ref.shape[1]
    width = kv_ref.shape[1]
    block = tok // HOT

    def store(row, value):
        part_ref[pl.ds(pl.multiple_of(row, tok // 2), value.shape[0]), :] = value

    place_ring(rank, pools, tok, pieces, store)
    meta_ref[...] = part_ref[:, 2 * width :]
    owners = [lax.div(hit_ref[0, i], held) for i in range(hits)]
    for i in range(hits):
        slot = jnp.int32(0)
        for earlier in range(i):
            slot = slot + (owners[earlier] == owners[i]).astype(jnp.int32)
        row = pl.multiple_of(owners[i] * tok + jnp.minimum(slot, HOT - 1) * block, block)
        kv_ref[i * block : (i + 1) * block, :] = part_ref[pl.ds(row, block), :width]
    prefix = hits * block
    kv_ref[prefix:, :] = part_ref[:, width : 2 * width]
    heads_kv = width // (2 * HD)
    group = model // (heads_kv * HD)
    rows, keys = bias_ref.shape
    stack = rows // tok
    col = lax.broadcasted_iota(jnp.int32, (rows, keys), 1)
    position = lax.rem(lax.broadcasted_iota(jnp.int32, (rows, keys), 0), tok) + rank * tok
    bias_ref[...] = jnp.where(col - prefix <= position, 0.0, MASKED)
    squares = jnp.zeros((tok, HD), F32)
    for g in range(heads_kv):
        key_mat = kv_ref[:, g * HD : (g + 1) * HD]
        values = kv_ref[:, (heads_kv + g) * HD : (heads_kv + g + 1) * HD]
        for first in range(g * group, (g + 1) * group, stack):
            query = jnp.concatenate(
                [query_ref[:, h * HD : (h + 1) * HD] for h in range(first, first + stack)], axis=0
            )
            scores = lax.dot_general(
                query, key_mat, (((1,), (1,)), ((), ())), preferred_element_type=F32
            )
            scores = scores * HD ** (-0.5) + bias_ref[...]
            weights = jnp.exp(scores - jnp.max(scores, axis=-1, keepdims=True))
            row_sum = jnp.sum(weights, axis=-1, keepdims=True)
            mixed = jnp.dot(weights.astype(BF16), values, preferred_element_type=F32) / row_sum
            mixed = mixed.astype(BF16)
            for s in range(stack):
                cols = slice((first + s) * HD, (first + s + 1) * HD)
                part = mixed[s * tok : (s + 1) * tok]
                attended_ref[:, cols] = part
                resid = (residual_ref[:, cols].astype(F32) + part.astype(F32)).astype(BF16)
                resid_ref[:, cols] = resid
                wide = resid.astype(F32)
                squares = squares + wide * wide
    inv_rms = lax.rsqrt(jnp.sum(squares, axis=-1, keepdims=True) / model + EPSILON)
    normed_ref[...] = (resid_ref[...].astype(F32) * inv_rms * gain_ref[...]).astype(BF16)


def route_kernel(rank_ref, meta_ref, take_ref, high_ref, low_ref, *, pools, top):
    tokens = meta_ref.shape[0]
    slots = take_ref.shape[0]
    tok = tokens // pools
    per = pools * MOST
    first = rank_ref[0] * (slots // per)
    slot = lax.broadcasted_iota(jnp.int32, (tok, slots), 1)
    expert = (lax.div(slot, per) + first).astype(F32)
    inner = lax.rem(slot, per)
    of_block = lax.div(inner, MOST)
    place = lax.rem(inner, MOST).astype(F32)
    before = (
        lax.broadcasted_iota(jnp.int32, (tok, tok), 1)
        < lax.broadcasted_iota(jnp.int32, (tok, tok), 0)
    ).astype(F32)
    for b in range(pools):
        meta = meta_ref[b * tok : (b + 1) * tok, :].astype(F32)
        named = jnp.zeros((tok, slots), F32)
        high = jnp.zeros((tok, slots), F32)
        low = jnp.zeros((tok, slots), F32)
        for j in range(top):
            same = meta[:, j : j + 1] == expert
            named = jnp.where(same, 1.0, named)
            high = jnp.where(same, meta[:, top + j : top + j + 1], high)
            low = jnp.where(same, meta[:, 2 * top + j : 2 * top + j + 1], low)
        rank = jnp.dot(before.astype(BF16), named.astype(BF16), preferred_element_type=F32)
        chosen = (named > 0.5) & (rank == place) & (of_block == b)
        take_ref[:, b * tok : (b + 1) * tok] = jnp.where(chosen, 1.0, 0.0).T.astype(BF16)
        high_ref[b * tok : (b + 1) * tok, :] = jnp.where(chosen, high, 0.0).astype(BF16)
        low_ref[b * tok : (b + 1) * tok, :] = jnp.where(chosen, low, 0.0).astype(BF16)


def pack_kernel(rank_ref, take_ref, *refs, pools):
    pieces = refs[: pools + 1]
    out_ref, rows_ref = refs[pools + 1 :]
    tok = pieces[0].shape[0]

    def store(row, value):
        rows_ref[pl.ds(pl.multiple_of(row, tok // 2), value.shape[0]), :] = value

    place_ring(rank_ref[0], pools, tok, pieces, store)
    out_ref[...] = jnp.dot(
        take_ref[...], rows_ref[...], preferred_element_type=F32
    ).astype(BF16)


def expert_kernel(x_ref, g0, g1, u0, u1, d0, d1, out_ref, hidden_ref, *, steps, wide):
    i = pl.program_id(0)
    half = hidden_ref.shape[1] // 2

    def grow(gate_ref, up_ref, at):
        x = x_ref[...]
        gate = jnp.dot(x, gate_ref[...], preferred_element_type=F32)
        up = jnp.dot(x, up_ref[...], preferred_element_type=F32)
        hidden = gate / (1.0 + jnp.exp(-gate)) * up
        hidden_ref[:, at : at + wide] = hidden.astype(BF16)

    for s in range(steps):

        @pl.when(i == s)
        def _():
            grow(g0, u0, s * wide)

        @pl.when(i == steps + s)
        def _():
            grow(g1, u1, half + s * wide)

    @pl.when(i >= 2 * steps)
    def _():
        out_ref[...] = (
            jnp.dot(hidden_ref[:, :half], d0[...], preferred_element_type=F32)
            + jnp.dot(hidden_ref[:, half:], d1[...], preferred_element_type=F32)
        ).astype(BF16)


def mix_kernel(high_ref, low_ref, y_ref, out_ref):
    y = y_ref[...]
    out_ref[...] = (
        jnp.dot(high_ref[...], y, preferred_element_type=F32)
        + jnp.dot(low_ref[...], y, preferred_element_type=F32)
    ).astype(BF16)


def ring(block, pools):
    right = [(k, (k + 1) % pools) for k in range(pools)]
    left = [(k, (k - 1) % pools) for k in range(pools)]
    pieces = [block]
    from_left = from_right = block
    for _ in range(1, pools // 2):
        from_left = lax.ppermute(from_left, "pool", right)
        from_right = lax.ppermute(from_right, "pool", left)
        pieces += [from_left, from_right]
    half = block.shape[0] // 2
    pieces += [
        lax.ppermute(from_left[:half], "pool", right),
        lax.ppermute(from_right[half:], "pool", left),
    ]
    return pieces


def shards(
    residual,
    queries,
    fresh_kv,
    pool_cache,
    hit_blocks,
    norm_gain,
    route_ids,
    route_logits,
    w_gate,
    w_up,
    w_down,
):
    pools = lax.axis_size("pool")
    plane = lax.axis_size("xy")
    rank = lax.axis_index("pool").astype(jnp.int32)[None]
    _, tok, model = queries.shape
    held, block, width = pool_cache.shape
    hits = hit_blocks.shape[1]
    top = route_ids.shape[2]
    half = w_gate.shape[2]
    shape = jax.ShapeDtypeStruct

    swap = [(0, 1), (1, 0)]
    own = (w_gate[0], w_up[0], w_down[0])
    peer = tuple(lax.ppermute(w, "core", swap) for w in own)

    packed = pl.pallas_call(
        gather_kernel,
        in_specs=[SMEM, SMEM, VMEM, VMEM, VMEM, VMEM],
        out_specs=VMEM,
        out_shape=shape((tok, 2 * width + META), BF16),
        compiler_params=params(),
        name="gather_block",
    )(rank, hit_blocks, pool_cache, fresh_kv[0], route_ids[0], route_logits[0])
    pieces = ring(packed, pools)

    stack = 4
    keys = hits * block + pools * tok
    attended, resid, normed, meta = pl.pallas_call(
        lambda *refs: attend_kernel(*refs, pools=pools, held=held),
        in_specs=[SMEM, SMEM] + [VMEM] * (3 + pools + 1),
        out_specs=[VMEM] * 4,
        out_shape=[shape((tok, model), BF16)] * 3 + [shape((pools * tok, META), BF16)],
        scratch_shapes=[
            pltpu.VMEM((pools * tok, 2 * width + META), BF16),
            pltpu.VMEM((keys, width), BF16),
            pltpu.VMEM((stack * tok, keys), F32),
        ],
        compiler_params=params(),
        name="attend",
    )(rank, hit_blocks, norm_gain[None], queries[0], residual[0], *pieces)

    slots = plane * pools * MOST
    take, high, low = pl.pallas_call(
        lambda *refs: route_kernel(*refs, pools=pools, top=top),
        in_specs=[SMEM, VMEM],
        out_specs=[VMEM] * 3,
        out_shape=[shape((slots, pools * tok), BF16)] + [shape((pools * tok, slots), BF16)] * 2,
        compiler_params=params(),
        name="route",
    )(rank, meta)

    rows = ring(normed, pools)
    chunk = min(1024, model)
    outgoing = pl.pallas_call(
        lambda *refs: pack_kernel(*refs, pools=pools),
        grid=(model // chunk,),
        in_specs=[SMEM, pl.BlockSpec((slots, pools * tok), lambda i: (0, 0))]
        + [pl.BlockSpec((r.shape[0], chunk), lambda i: (0, i)) for r in rows],
        out_specs=pl.BlockSpec((slots, chunk), lambda i: (0, i)),
        out_shape=shape((slots, model), BF16),
        scratch_shapes=[pltpu.VMEM((pools * tok, chunk), BF16)],
        compiler_params=params(),
        name="pack",
    )(rank, take, *rows)
    per = slots // plane
    arrived = lax.all_to_all(
        outgoing.reshape(plane, per, model), "xy", split_axis=0, concat_axis=0, tiled=True
    ).reshape(slots, model)

    wide = min(128, half)
    steps = half // wide
    cols = min(1024, model)
    downs = model // cols
    y = pl.pallas_call(
        lambda *refs: expert_kernel(*refs, steps=steps, wide=wide),
        grid=(2 * steps + downs,),
        in_specs=[pl.BlockSpec((slots, model), lambda i: (0, 0))]
        + [
            pl.BlockSpec((model, wide), lambda i: (0, jnp.clip(i, 0, steps - 1))),
            pl.BlockSpec((model, wide), lambda i: (0, jnp.clip(i - steps, 0, steps - 1))),
        ]
        * 2
        + [pl.BlockSpec((half, cols), lambda i: (0, jnp.clip(i - 2 * steps, 0, downs - 1)))] * 2,
        out_specs=pl.BlockSpec((slots, cols), lambda i: (0, jnp.clip(i - 2 * steps, 0, downs - 1))),
        out_shape=shape((slots, model), BF16),
        scratch_shapes=[pltpu.VMEM((slots, 2 * half), BF16)],
        compiler_params=params(),
        name="expert",
    )(arrived, own[0], peer[0], own[1], peer[1], own[2], peer[2])

    returned = lax.all_to_all(
        y.reshape(plane, per, model), "xy", split_axis=0, concat_axis=0, tiled=True
    ).reshape(slots, model)
    mixed = pl.pallas_call(
        mix_kernel,
        grid=(model // chunk,),
        in_specs=[pl.BlockSpec((pools * tok, slots), lambda i: (0, 0))] * 2
        + [pl.BlockSpec((slots, chunk), lambda i: (0, i))],
        out_specs=pl.BlockSpec((pools * tok, chunk), lambda i: (0, i)),
        out_shape=shape((pools * tok, model), BF16),
        compiler_params=params(),
        name="mix",
    )(high, low, returned)
    mix = lax.psum_scatter(mixed, "pool", scatter_dimension=0, tiled=True)
    layer_out = (resid.astype(F32) + mix.astype(F32)).astype(BF16)
    return (attended[None], layer_out[None])


def solution(mesh):
    pools, experts = mesh.devices.shape
    fine = Mesh(mesh.devices.reshape(pools, experts // 2, 2), ("pool", "xy", "core"))
    ex = ("xy", "core")
    tokens = P(ex, "pool", None)
    slab = P(("pool", "xy", "core"), None, None)
    placed = (
        tokens,
        tokens,
        tokens,
        P("pool", None, None),
        P(ex, None),
        P(),
        tokens,
        tokens,
        slab,
        slab,
        slab,
    )
    return jax.shard_map(
        shards, mesh=fine, in_specs=placed, out_specs=(tokens, tokens), check_vma=False
    )
```

time: 1170 us -> 335 us (0.29)
  blocking collectives: 640 us -> 58 us
  local copies, waits for them, and re-layouts: 255 us -> 7.44 us
  Pallas kernels: 0 us -> 62.5 us
  other arithmetic: 57.7 us -> 1.96 us
  matrix products: 33.7 us -> 0 us
  starting transfers between devices: 8.8 us -> 33.4 us
  between operations: 1.49 us -> 14.2 us
    all_to_all x3 -> x1, blocking collectives: 583 us -> 58 us  [shards(): lax.all_to_all(y.reshape(plane, per, model), 'xy', split_axis=0, concat_a...]
    all_to_all x1, waiting for transfers between devices: 164 us -> 44.3 us  [shards(): lax.all_to_all(outgoing.reshape(plane, per, model), 'xy', split_axis=0, c...]
    pallas_call x0 -> x6, Pallas kernels: none -> 62.5 us  [the longest x1 29.9 us: shards(): pl.pallas_call(lambda *refs: expert_kernel(*refs, steps=steps, wide=wide)...]
    ppermute x0 -> x19, waiting for transfers between devices: none -> 59.1 us  [the longest x6 40.8 us: ring(): from_right = lax.ppermute(from_right, 'pool', left)]
    all_gather x2 -> x0, blocking collectives: 56.6 us -> none  [the longest x1 29.1 us: shards(): part_rows = lax.all_gather(packed, 'pool', axis=0, tiled=True)]
    reshape x4 -> x0, local copies, waits for them, and re-layouts: 53.3 us -> none  [the longest x2 24.4 us: shards(): partial_value.reshape(pool_count, expert_count, capacity, model_width)]
    reduce_scatter x0 -> x1, waiting for transfers between devices: none -> 52.1 us  [shards(): mix = lax.psum_scatter(mixed, 'pool', scatter_dimension=0, tiled=True)]
    all_to_all x3 -> x0, local copies, waits for them, and re-layouts: 48.5 us -> none  [the longest x1 21.3 us: shards(): lax.all_to_all(lax.all_to_all(doubled, 'pool', split_axis=0, concat_axis=...]
  transfers between devices with their start and end apart: 1 -> 21, of which waited for: 1 -> 14; matrix products, arithmetic and copies ran while one was open for 0% -> 0% of each run, Pallas kernels for 0% -> 2%
where the time goes in v1:
time: 335 us; the launch traced here: 333 us
  waiting for transfers between devices  156 us (47%)
  Pallas kernels  62.5 us (19%)
  blocking collectives  58 us (17%)
  starting transfers between devices  33.4 us (10%)
  between operations  14.2 us (4%)
  local copies, waits for them, and re-layouts  7.44 us (2%)
    all_to_all x1, blocking collectives, shards(): lax.all_to_all(y.reshape(plane, per, model), 'xy', split_axis=0, concat_a...  58 us
    reduce_scatter x1, waiting for transfers between devices, shards(): mix = lax.psum_scatter(mixed, 'pool', scatter_dimension=0, tiled=True)  52.1 us
    all_to_all x1, waiting for transfers between devices, shards(): lax.all_to_all(outgoing.reshape(plane, per, model), 'xy', split_axis=0, c...  44.3 us
    ppermute x6, waiting for transfers between devices, ring(): from_right = lax.ppermute(from_right, 'pool', left)  40.8 us
    pallas_call x1, Pallas kernels, shards(): pl.pallas_call(lambda *refs: expert_kernel(*refs, steps=steps, wide=wide)...  29.9 us
    ppermute x6, starting transfers between devices, ring(): from_right = lax.ppermute(from_right, 'pool', left)  13.1 us
    ppermute x3, waiting for transfers between devices, shards(): peer = tuple((lax.ppermute(w, 'core', swap) for w in own))  12.2 us
    pallas_call x1, Pallas kernels, shards(): pl.pallas_call(mix_kernel, grid=(model // chunk,), in_specs=[pl.BlockSpec...  9.95 us
  transfers between devices with their start and end apart: 21, of which 14 were waited for; matrix products, arithmetic and copies ran while one was open for 0% of the time, Pallas kernels for 2%

profile of v1, /device:TPU:12, one launch (start us, length us, event | category | flops | bytes accessed | tf_op | source)
XLA Modules:
  0.0 333.0 jit_solution(8384832070951623123)
XLA Ops:
  9.9 2.5 gather_block.1.refs_5_
  12.4 5.9 %collective-permute-start.1 = (bf16[64,1152]{1,0:T(8,128)(2,1)}, bf16[64,1152]{1,0:T(8,128)(2,1)S(1)}, u32[]{:S(2)}, u32[]{:S(2)}) collective-permute-start(bf16[64,1152]{1,0:T(8,128)(2,1)} %gather_block.1.refs_5_), channel_id=1, source_target_pairs={{0,224},{32,0},{64,32},{96,64},{128,96},{160,128},{192,160},{224,1... | collective-permute-start | bytes 442376 | tf_op jit(solution)/shard_map/ppermute | solution.py:217
  18.3 3.4 %collective-permute-done.1.refs_7_ = bf16[64,1152]{1,0:T(8,128)(2,1)S(1)} collective-permute-done((bf16[64,1152]{1,0:T(8,128)(2,1)}, bf16[64,1152]{1,0:T(8,128)(2,1)S(1)}, u32[]{:S(2)}, u32[]{:S(2)}) %collective-permute-start.1) | collective-permute-done | bytes 147488 | tf_op jit(solution)/shard_map/ppermute | solution.py:217
  21.7 3.6 %collective-permute-start.3 = (bf16[64,1152]{1,0:T(8,128)(2,1)S(1)}, bf16[64,1152]{1,0:T(8,128)(2,1)S(1)}, u32[]{:S(2)}, u32[]{:S(2)}) collective-permute-start(bf16[64,1152]{1,0:T(8,128)(2,1)S(1)} %collective-permute-done.1.refs_7_), channel_id=1, source_target_pairs={{0,224},{32,0},{64,32},{96,64},{128,96},{160,128},{192,160},{224,1... | collective-permute-start | bytes 442376 | tf_op jit(solution)/shard_map/ppermute | solution.py:217
  25.3 2.7 collective-permute-done.3.refs_9_
  27.9 3.7 %collective-permute-start.5 = (bf16[64,1152]{1,0:T(8,128)(2,1)S(1)}, bf16[64,1152]{1,0:T(8,128)(2,1)S(1)}, u32[]{:S(2)}, u32[]{:S(2)}) collective-permute-start(bf16[64,1152]{1,0:T(8,128)(2,1)S(1)} %collective-permute-done.3.refs_9_), channel_id=1, source_target_pairs={{0,224},{32,0},{64,32},{96,64},{128,96},{160,128},{192,160},{224,1... | collective-permute-start | bytes 442376 | tf_op jit(solution)/shard_map/ppermute | solution.py:217
  31.6 2.7 collective-permute-done.5.refs_11_
  34.3 3.8 %collective-permute-start.7 = (bf16[32,1152]{1,0:T(8,128)(2,1)S(1)}, bf16[32,1152]{1,0:T(8,128)(2,1)S(1)}, u32[]{:S(2)}, u32[]{:S(2)}) collective-permute-start(bf16[32,1152]{1,0:T(8,128)(2,1)S(1)} %slice.17), channel_id=1, source_target_pairs={{0,224},{32,0},{64,32},{96,64},{128,96},{160,128},{192,160},{224,1... | collective-permute-start | bytes 221192 | tf_op jit(solution)/shard_map/ppermute | solution.py:222
  40.1 3.7 %collective-permute-done.6.refs_12_ = bf16[32,1152]{1,0:T(8,128)(2,1)S(1)} collective-permute-done((bf16[32,1152]{1,0:T(8,128)(2,1)S(1)}, bf16[32,1152]{1,0:T(8,128)(2,1)S(1)}, u32[]{:S(2)}, u32[]{:S(2)}) %collective-permute-start.6) | collective-permute-done | bytes 73760 | tf_op jit(solution)/shard_map/ppermute | solution.py:221
  44.4 6.5 %attend.1 = (bf16[64,4096]{1,0:T(8,128)(2,1)}, bf16[64,4096]{1,0:T(8,128)(2,1)}, bf16[64,4096]{1,0:T(8,128)(2,1)}, bf16[512,128]{1,0:T(8,128)(2,1)}) custom-call(s32[1]{0:T(128)} %bitcast.rank_ref.refs_0_, s32[1,16]{1,0:T(1,128)} %refs_1_.1, f32[1,4096]{1,0:T(1,128)} %bitcast.31, bf16[64,4096]{1,0:T(8,128)(2,1)} %bitcast.26, bf16[64,4096]{1,0:T(8,128)(2,1)} %bitcast.27, ...), custom_call_target="tpu_custom_call" | custom-call | tf_op jit(solution)/shard_map/attend/pallas_call | solution.py:266
  50.8 2.0 collective-permute-start.8
  52.9 10.6 %collective-permute-done.9.refs_4_ = bf16[64,4096]{1,0:T(8,128)(2,1)S(1)} collective-permute-done((bf16[64,4096]{1,0:T(8,128)(2,1)}, bf16[64,4096]{1,0:T(8,128)(2,1)S(1)}, u32[]{:S(2)}, u32[]{:S(2)}) %collective-permute-start.9) | collective-permute-done | bytes 524320 | tf_op jit(solution)/shard_map/ppermute | solution.py:217
  65.5 11.5 %collective-permute-done.11.refs_6_ = bf16[64,4096]{1,0:T(8,128)(2,1)S(1)} collective-permute-done((bf16[64,4096]{1,0:T(8,128)(2,1)S(1)}, bf16[64,4096]{1,0:T(8,128)(2,1)S(1)}, u32[]{:S(2)}, u32[]{:S(2)}) %collective-permute-start.11) | collective-permute-done | bytes 524320 | tf_op jit(solution)/shard_map/ppermute | solution.py:217
  79.1 10.0 %collective-permute-done.13.refs_8_ = bf16[64,4096]{1,0:T(8,128)(2,1)S(1)} collective-permute-done((bf16[64,4096]{1,0:T(8,128)(2,1)S(1)}, bf16[64,4096]{1,0:T(8,128)(2,1)S(1)}, u32[]{:S(2)}, u32[]{:S(2)}) %collective-permute-start.13) | collective-permute-done | bytes 524320 | tf_op jit(solution)/shard_map/ppermute | solution.py:217
  91.3 6.4 %route.1 = (bf16[640,512]{1,0:T(8,128)(2,1)}, bf16[512,640]{1,0:T(8,128)(2,1)}, bf16[512,640]{1,0:T(8,128)(2,1)}) custom-call(s32[1]{0:T(128)} %bitcast.rank_ref.refs_0_, bf16[512,128]{1,0:T(8,128)(2,1)} %get-tuple-element.11.refs_1_), custom_call_target="tpu_custom_call" | custom-call | tf_op jit(solution)/shard_map/route/pallas_call | solution.py:281
  98.7 7.4 %pack.1 = bf16[640,4096]{1,0:T(8,128)(2,1)} custom-call(s32[1]{0:T(128)} %bitcast.rank_ref.refs_0_, bf16[640,512]{1,0:T(8,128)(2,1)} %get-tuple-element.14.refs_1_, bf16[64,4096]{1,0:T(8,128)(2,1)} %get-tuple-element.15.refs_2_, bf16[64,4096]{1,0:T(8,128)(2,1)} %copy-done.7, bf16[64,4096]{1,0:T(8,128)(2,1)} %copy-done.6, bf16[64,4096]{1,0:T(8,128)(2,1)} %copy-done.9, ...), custom_call_target="tpu_custom_call" | custom-call | tf_op jit(solution)/shard_map/pack/pallas_call | solution.py:292
  106.1 7.6 %all-to-all-start = ((bf16[16,40,4096]{2,1,0:T(8,128)(2,1)}), bf16[16,40,4096]{2,1,0:T(8,128)(2,1)}, u32[]{:S(2)}, u32[]{:S(2)}) async-start(bf16[16,40,4096]{2,1,0:T(8,128)(2,1)} %bitcast.18), calls=%async_computation | async-start | bytes 10485760 | tf_op jit(solution)/shard_map/all_to_all | solution.py:304
  114.5 8.5 %collective-permute-done.16.refs_2_ = bf16[4096,384]{1,0:T(8,128)(2,1)S(1)} collective-permute-done((bf16[4096,384]{1,0:T(8,128)(2,1)S(1)}, bf16[4096,384]{1,0:T(8,128)(2,1)S(1)}, u32[]{:S(2)}, u32[]{:S(2)}) %collective-permute-start.16) | collective-permute-done | bytes 3145760 | tf_op jit(solution)/shard_map/ppermute | solution.py:252
  124.8 3.6 %collective-permute-done.17.refs_4_ = bf16[4096,384]{1,0:T(8,128)(2,1)S(1)} collective-permute-done((bf16[4096,384]{1,0:T(8,128)(2,1)}, bf16[4096,384]{1,0:T(8,128)(2,1)S(1)}, u32[]{:S(2)}, u32[]{:S(2)}) %collective-permute-start.17) | collective-permute-done | bytes 3145760 | tf_op jit(solution)/shard_map/ppermute | solution.py:252
  130.0 44.3 %all-to-all-done = bf16[16,40,4096]{2,1,0:T(8,128)(2,1)} async-done(((bf16[16,40,4096]{2,1,0:T(8,128)(2,1)}), bf16[16,40,4096]{2,1,0:T(8,128)(2,1)}, u32[]{:S(2)}, u32[]{:S(2)}) %all-to-all-start) | async-done | bytes 5242912 | tf_op jit(solution)/shard_map/all_to_all | solution.py:304
  174.3 29.9 %expert.1 = bf16[640,4096]{1,0:T(8,128)(2,1)} custom-call(bf16[640,4096]{1,0:T(8,128)(2,1)} %bitcast.9.refs_0_, bf16[4096,384]{1,0:T(8,128)(2,1)} %bitcast.20, bf16[4096,384]{1,0:T(8,128)(2,1)} %copy-done.1, bf16[4096,384]{1,0:T(8,128)(2,1)} %bitcast.23, bf16[4096,384]{1,0:T(8,128)(2,1)} %copy-done.2, bf16[384,4096]{1,0:T(8,128)(2,1)} %bitcast.25, ...), custom_call_target="tpu_custom_call" | custom-call | tf_op jit(solution)/shard_map/expert/pallas_call | solution.py:312
  204.2 58.0 %all_to_all.10 = bf16[16,40,4096]{2,1,0:T(8,128)(2,1)} all-to-all(bf16[16,40,4096]{2,1,0:T(8,128)(2,1)} %bitcast.17), channel_id=1, replica_groups=mesh['pool'=8,'xy'=16,'core'=2] {'xy'}, dimensions={0} | all-to-all | bytes 10485760 | tf_op jit(solution)/shard_map/all_to_all | solution.py:329
  262.2 9.9 %mix.1 = bf16[512,4096]{1,0:T(8,128)(2,1)} custom-call(bf16[512,640]{1,0:T(8,128)(2,1)} %get-tuple-element.12.high_ref, bf16[512,640]{1,0:T(8,128)(2,1)} %get-tuple-element.13.low_ref, bf16[640,4096]{1,0:T(8,128)(2,1)} %bitcast.19), custom_call_target="tpu_custom_call" | custom-call | tf_op jit(solution)/shard_map/mix/pallas_call | solution.py:332
  272.2 52.1 %reduce-scatter.2.cloned.1.call-done = bf16[64,4096]{1,0:T(8,128)(2,1)} async-done(((bf16[512,4096]{1,0:T(8,128)(2,1)}), bf16[64,4096]{1,0:T(8,128)(2,1)}) %reduce-scatter.2.cloned.1.call-update) | async-done | bytes 524304 | tf_op jit(solution)/shard_map/reduce_scatter | solution.py:342
  (73 shorter events, 18.8 us)
Async XLA Ops:
  12.4 9.3 %collective-permute-start.1 = (bf16[64,1152]{1,0:T(8,128)(2,1)}, bf16[64,1152]{1,0:T(8,128)(2,1)S(1)}, u32[]{:S(2)}, u32[]{:S(2)}) collective-permute-start(bf16[64,1152]{1,0:T(8,128)(2,1)} %gather_block.1.refs_5_), channel_id=1, source_target_pairs={{0,224},{32,0},{64,32},{96,64},{128,96},{160,128},{192,160},{224,1... | collective-permute-start | bytes 442376 | tf_op jit(solution)/shard_map/ppermute | solution.py:217
  18.3 7.0 %collective-permute-start = (bf16[64,1152]{1,0:T(8,128)(2,1)}, bf16[64,1152]{1,0:T(8,128)(2,1)S(1)}, u32[]{:S(2)}, u32[]{:S(2)}) collective-permute-start(bf16[64,1152]{1,0:T(8,128)(2,1)} %gather_block.1.refs_5_), channel_id=1, source_target_pairs={{0,32},{32,64},{64,96},{96,128},{128,160},{160,192},{192,224},{224... | collective-permute-start | bytes 442376 | tf_op jit(solution)/shard_map/ppermute | solution.py:216
  21.7 6.3 %collective-permute-start.3 = (bf16[64,1152]{1,0:T(8,128)(2,1)S(1)}, bf16[64,1152]{1,0:T(8,128)(2,1)S(1)}, u32[]{:S(2)}, u32[]{:S(2)}) collective-permute-start(bf16[64,1152]{1,0:T(8,128)(2,1)S(1)} %collective-permute-done.1.refs_7_), channel_id=1, source_target_pairs={{0,224},{32,0},{64,32},{96,64},{128,96},{160,128},{192,160},{224,1... | collective-permute-start | bytes 442376 | tf_op jit(solution)/shard_map/ppermute | solution.py:217
  25.3 6.4 %collective-permute-start.2 = (bf16[64,1152]{1,0:T(8,128)(2,1)S(1)}, bf16[64,1152]{1,0:T(8,128)(2,1)S(1)}, u32[]{:S(2)}, u32[]{:S(2)}) collective-permute-start(bf16[64,1152]{1,0:T(8,128)(2,1)S(1)} %collective-permute-done.refs_6_), channel_id=1, source_target_pairs={{0,32},{32,64},{64,96},{96,128},{128,160},{160,192},{192,224},{224... | collective-permute-start | bytes 442376 | tf_op jit(solution)/shard_map/ppermute | solution.py:216
  27.9 6.4 %collective-permute-start.5 = (bf16[64,1152]{1,0:T(8,128)(2,1)S(1)}, bf16[64,1152]{1,0:T(8,128)(2,1)S(1)}, u32[]{:S(2)}, u32[]{:S(2)}) collective-permute-start(bf16[64,1152]{1,0:T(8,128)(2,1)S(1)} %collective-permute-done.3.refs_9_), channel_id=1, source_target_pairs={{0,224},{32,0},{64,32},{96,64},{128,96},{160,128},{192,160},{224,1... | collective-permute-start | bytes 442376 | tf_op jit(solution)/shard_map/ppermute | solution.py:217
  31.6 6.4 %collective-permute-start.4 = (bf16[64,1152]{1,0:T(8,128)(2,1)S(1)}, bf16[64,1152]{1,0:T(8,128)(2,1)S(1)}, u32[]{:S(2)}, u32[]{:S(2)}) collective-permute-start(bf16[64,1152]{1,0:T(8,128)(2,1)S(1)} %collective-permute-done.2.refs_8_), channel_id=1, source_target_pairs={{0,32},{32,64},{64,96},{96,128},{128,160},{160,192},{192,224},{224... | collective-permute-start | bytes 442376 | tf_op jit(solution)/shard_map/ppermute | solution.py:216
  34.3 5.7 %collective-permute-start.7 = (bf16[32,1152]{1,0:T(8,128)(2,1)S(1)}, bf16[32,1152]{1,0:T(8,128)(2,1)S(1)}, u32[]{:S(2)}, u32[]{:S(2)}) collective-permute-start(bf16[32,1152]{1,0:T(8,128)(2,1)S(1)} %slice.17), channel_id=1, source_target_pairs={{0,224},{32,0},{64,32},{96,64},{128,96},{160,128},{192,160},{224,1... | collective-permute-start | bytes 221192 | tf_op jit(solution)/shard_map/ppermute | solution.py:222
  38.1 5.6 %collective-permute-start.6 = (bf16[32,1152]{1,0:T(8,128)(2,1)S(1)}, bf16[32,1152]{1,0:T(8,128)(2,1)S(1)}, u32[]{:S(2)}, u32[]{:S(2)}) collective-permute-start(bf16[32,1152]{1,0:T(8,128)(2,1)S(1)} %slice.16), channel_id=1, source_target_pairs={{0,32},{32,64},{64,96},{96,128},{128,160},{160,192},{192,224},{224... | collective-permute-start | bytes 221192 | tf_op jit(solution)/shard_map/ppermute | solution.py:221
  50.8 12.6 %collective-permute-start.9 = (bf16[64,4096]{1,0:T(8,128)(2,1)}, bf16[64,4096]{1,0:T(8,128)(2,1)S(1)}, u32[]{:S(2)}, u32[]{:S(2)}) collective-permute-start(bf16[64,4096]{1,0:T(8,128)(2,1)} %get-tuple-element.15.refs_2_), channel_id=1, source_target_pairs={{0,224},{32,0},{64,32},{96,64},{128,96},{160,128},{192,160},{224,1... | collective-permute-start | bytes 1572872 | tf_op jit(solution)/shard_map/ppermute | solution.py:217
  50.8 12.8 %collective-permute-start.8 = (bf16[64,4096]{1,0:T(8,128)(2,1)}, bf16[64,4096]{1,0:T(8,128)(2,1)S(1)}, u32[]{:S(2)}, u32[]{:S(2)}) collective-permute-start(bf16[64,4096]{1,0:T(8,128)(2,1)} %get-tuple-element.15.refs_2_), channel_id=1, source_target_pairs={{0,32},{32,64},{64,96},{96,128},{128,160},{160,192},{192,224},{224... | collective-permute-start | bytes 1572872 | tf_op jit(solution)/shard_map/ppermute | solution.py:216
  63.5 34.6 %copy-start.6 = (bf16[64,4096]{1,0:T(8,128)(2,1)}, bf16[64,4096]{1,0:T(8,128)(2,1)S(1)}, u32[]{:S(2)}) copy-start(bf16[64,4096]{1,0:T(8,128)(2,1)S(1)} %collective-permute-done.9.refs_4_) | copy-start | bytes 1572868
  63.5 13.6 %collective-permute-start.11 = (bf16[64,4096]{1,0:T(8,128)(2,1)S(1)}, bf16[64,4096]{1,0:T(8,128)(2,1)S(1)}, u32[]{:S(2)}, u32[]{:S(2)}) collective-permute-start(bf16[64,4096]{1,0:T(8,128)(2,1)S(1)} %collective-permute-done.9.refs_4_), channel_id=1, source_target_pairs={{0,224},{32,0},{64,32},{96,64},{128,96},{160,128},{192,160},{224,1... | collective-permute-start | bytes 1572872 | tf_op jit(solution)/shard_map/ppermute | solution.py:217
  63.6 34.4 %copy-start.7 = (bf16[64,4096]{1,0:T(8,128)(2,1)}, bf16[64,4096]{1,0:T(8,128)(2,1)S(1)}, u32[]{:S(2)}) copy-start(bf16[64,4096]{1,0:T(8,128)(2,1)S(1)} %collective-permute-done.8.refs_3_) | copy-start | bytes 1572868
  63.6 13.4 %collective-permute-start.10 = (bf16[64,4096]{1,0:T(8,128)(2,1)S(1)}, bf16[64,4096]{1,0:T(8,128)(2,1)S(1)}, u32[]{:S(2)}, u32[]{:S(2)}) collective-permute-start(bf16[64,4096]{1,0:T(8,128)(2,1)S(1)} %collective-permute-done.8.refs_3_), channel_id=1, source_target_pairs={{0,32},{32,64},{64,96},{96,128},{128,160},{160,192},{192,224},{224... | collective-permute-start | bytes 1572872 | tf_op jit(solution)/shard_map/ppermute | solution.py:216
  77.0 12.0 %collective-permute-start.13 = (bf16[64,4096]{1,0:T(8,128)(2,1)S(1)}, bf16[64,4096]{1,0:T(8,128)(2,1)S(1)}, u32[]{:S(2)}, u32[]{:S(2)}) collective-permute-start(bf16[64,4096]{1,0:T(8,128)(2,1)S(1)} %collective-permute-done.11.refs_6_), channel_id=1, source_target_pairs={{0,224},{32,0},{64,32},{96,64},{128,96},{160,128},{192,160},{224,1... | collective-permute-start | bytes 1572872 | tf_op jit(solution)/shard_map/ppermute | solution.py:217
  77.1 13.3 %collective-permute-start.12 = (bf16[64,4096]{1,0:T(8,128)(2,1)S(1)}, bf16[64,4096]{1,0:T(8,128)(2,1)S(1)}, u32[]{:S(2)}, u32[]{:S(2)}) collective-permute-start(bf16[64,4096]{1,0:T(8,128)(2,1)S(1)} %collective-permute-done.10.refs_5_), channel_id=1, source_target_pairs={{0,32},{32,64},{64,96},{96,128},{128,160},{160,192},{192,224},{224... | collective-permute-start | bytes 1572872 | tf_op jit(solution)/shard_map/ppermute | solution.py:216
  89.1 8.6 %collective-permute-start.15 = (bf16[32,4096]{1,0:T(8,128)(2,1)S(1)}, bf16[32,4096]{1,0:T(8,128)(2,1)S(1)}, u32[]{:S(2)}, u32[]{:S(2)}) collective-permute-start(bf16[32,4096]{1,0:T(8,128)(2,1)S(1)} %slice.19), channel_id=1, source_target_pairs={{0,224},{32,0},{64,32},{96,64},{128,96},{160,128},{192,160},{224,1... | collective-permute-start | bytes 786440 | tf_op jit(solution)/shard_map/ppermute | solution.py:222
  90.4 7.7 %collective-permute-start.14 = (bf16[32,4096]{1,0:T(8,128)(2,1)S(1)}, bf16[32,4096]{1,0:T(8,128)(2,1)S(1)}, u32[]{:S(2)}, u32[]{:S(2)}) collective-permute-start(bf16[32,4096]{1,0:T(8,128)(2,1)S(1)} %slice.18), channel_id=1, source_target_pairs={{0,32},{32,64},{64,96},{96,128},{128,160},{160,192},{192,224},{224... | collective-permute-start | bytes 786440 | tf_op jit(solution)/shard_map/ppermute | solution.py:221
  106.1 68.2 %all-to-all-start = ((bf16[16,40,4096]{2,1,0:T(8,128)(2,1)}), bf16[16,40,4096]{2,1,0:T(8,128)(2,1)}, u32[]{:S(2)}, u32[]{:S(2)}) async-start(bf16[16,40,4096]{2,1,0:T(8,128)(2,1)} %bitcast.18), calls=%async_computation | async-start | bytes 10485760 | tf_op jit(solution)/shard_map/all_to_all | solution.py:304
  113.7 210.5 %reduce-scatter.2.cloned.1.call-start = ((), (), s32[]{:S(2)}) async-start(), calls=%async_computation.3 | async-start | bytes 4718592 | tf_op jit(solution)/shard_map/reduce_scatter | solution.py:342
  113.8 9.2 %collective-permute-start.16 = (bf16[4096,384]{1,0:T(8,128)(2,1)S(1)}, bf16[4096,384]{1,0:T(8,128)(2,1)S(1)}, u32[]{:S(2)}, u32[]{:S(2)}) collective-permute-start(bf16[4096,384]{1,0:T(8,128)(2,1)S(1)} %bitcast.21), channel_id=1, source_target_pairs={{0,1},{1,0},{2,3},{3,2},{4,5},{5,4},{6,7},{7,6},{8,9},{9,8},{10,11... | collective-permute-start | bytes 9437192 | tf_op jit(solution)/shard_map/ppermute | solution.py:252
  113.9 14.5 %collective-permute-start.17 = (bf16[4096,384]{1,0:T(8,128)(2,1)}, bf16[4096,384]{1,0:T(8,128)(2,1)S(1)}, u32[]{:S(2)}, u32[]{:S(2)}) collective-permute-start(bf16[4096,384]{1,0:T(8,128)(2,1)} %bitcast.22), channel_id=1, source_target_pairs={{0,1},{1,0},{2,3},{3,2},{4,5},{5,4},{6,7},{7,6},{8,9},{9,8},{10,11... | collective-permute-start | bytes 9437192 | tf_op jit(solution)/shard_map/ppermute | solution.py:252
  114.4 15.6 %collective-permute-start.18 = (bf16[384,4096]{1,0:T(8,128)(2,1)}, bf16[384,4096]{1,0:T(8,128)(2,1)}, u32[]{:S(2)}, u32[]{:S(2)}) collective-permute-start(bf16[384,4096]{1,0:T(8,128)(2,1)} %bitcast.24), channel_id=1, source_target_pairs={{0,1},{1,0},{2,3},{3,2},{4,5},{5,4},{6,7},{7,6},{8,9},{9,8},{10,11... | collective-permute-start | bytes 9437192 | tf_op jit(solution)/shard_map/ppermute | solution.py:252
  272.1 52.1 %copy-start.5 = (bf16[64,4096]{1,0:T(8,128)(2,1)S(1)}, bf16[64,4096]{1,0:T(8,128)(2,1)}, u32[]{:S(2)}) copy-start(bf16[64,4096]{1,0:T(8,128)(2,1)} %get-tuple-element.10) | copy-start | bytes 1572868
  (17 other events, 159.0 us)
Sparse Core Ops, SparseCore 0:
  272.3 51.9 reduce-scatter.1

commit v2 on v1

v2 whole, which is shorter than its diff:
```python
import jax
import jax.numpy as jnp
from jax import lax
from jax.experimental import pallas as pl
from jax.experimental.pallas import tpu as pltpu
from jax.sharding import Mesh, PartitionSpec as P

HD = 128
HOT = 4
MOST = 5
META = 128
NEAR = 5
NEAR_SLOTS = 24
FAR_SLOTS = 16
MASKED = -1e30
EPSILON = 1e-06
F32 = jnp.float32
BF16 = jnp.bfloat16
COLS = 1024

SMEM = pl.BlockSpec(memory_space=pltpu.SMEM)
VMEM = pl.BlockSpec(memory_space=pltpu.VMEM)
ANY = pl.BlockSpec(memory_space=pl.ANY)


class Fetched(tuple):
    pass


def in_hbm(x):
    return (pltpu.with_memory_space_constraint(x, pltpu.HBM),)


def held_call(kernel, name, outs, args, scalars=0, near=(), far=(), scratch=(), limit=56):
    given = list(args[:scalars])
    specs = [SMEM] * scalars
    for arg in args[scalars:]:
        if isinstance(arg, tuple):
            given.append(arg[0])
            specs.append(VMEM if isinstance(arg, Fetched) else ANY)
        else:
            given.append(pltpu.with_memory_space_constraint(arg, pltpu.VMEM))
            specs.append(VMEM)
    return pl.pallas_call(
        kernel,
        in_specs=specs,
        out_specs=[ANY if n in far else VMEM for n in range(len(outs))],
        out_shape=[
            pltpu.VMEM(o.shape, o.dtype) if n in near else o for n, o in enumerate(outs)
        ],
        scratch_shapes=list(scratch),
        compiler_params=pltpu.CompilerParams(vmem_limit_bytes=limit * 1024 * 1024),
        name=name,
    )(*given)


def gather_kernel(rank_ref, hit_ref, cache_ref, fresh_ref, ids_ref, logit_ref, out_ref, sem):
    rank = rank_ref[0]
    held, block, width = cache_ref.shape
    count = jnp.int32(0)
    local = [jnp.int32(0)] * HOT
    for i in range(hit_ref.shape[1]):
        hit = hit_ref[0, i]
        mine = lax.div(hit, held) == rank
        for slot in range(HOT):
            local[slot] = jnp.where(mine & (count == slot), lax.rem(hit, held), local[slot])
        count = count + mine.astype(jnp.int32)
    copies = [
        pltpu.make_async_copy(
            cache_ref.at[local[slot]],
            out_ref.at[slot * block : (slot + 1) * block, :width],
            sem.at[slot],
        )
        for slot in range(HOT)
    ]
    for copy in copies:
        copy.start()
    out_ref[:, width : 2 * width] = fresh_ref[...]
    ids = ids_ref[...].astype(F32).T
    logits = logit_ref[...].T
    grown = jnp.exp(logits - jnp.max(logits, axis=-1, keepdims=True))
    weight = grown / jnp.sum(grown, axis=-1, keepdims=True)
    high = weight.astype(BF16).astype(F32)
    low = weight - high
    tok, top = ids.shape
    lane = lax.broadcasted_iota(jnp.int32, (tok, META), 1)
    meta = jnp.zeros((tok, META), F32)
    for part, values in enumerate((ids, high, low)):
        for j in range(top):
            meta = jnp.where(lane == part * top + j, values[:, j : j + 1], meta)
    out_ref[:, 2 * width :] = meta.astype(BF16)
    for copy in copies:
        copy.wait()


def place_ring(rank, pools, tok, pieces, store):
    store(rank * tok, pieces[0][...])
    half = pools // 2
    for s in range(1, half):
        store(lax.rem(rank + pools - s, pools) * tok, pieces[2 * s - 1][...])
        store(lax.rem(rank + s, pools) * tok, pieces[2 * s][...])
    far = lax.rem(rank + half, pools) * tok
    store(far, pieces[2 * half - 1][...])
    store(far + tok // 2, pieces[2 * half][...])


def attend_kernel(rank_ref, hit_ref, gain_ref, query_ref, residual_ref, *refs, pools, held):
    pieces = refs[: pools + 1]
    attended_ref, resid_ref, normed_ref, meta_ref, part_ref, kv_ref, bias_ref = refs[pools + 1 :]
    rank = rank_ref[0]
    tok, model = query_ref.shape
    hits = hit_ref.shape[1]
    width = kv_ref.shape[1]
    block = tok // HOT

    def store(row, value):
        part_ref[pl.ds(pl.multiple_of(row, tok // 2), value.shape[0]), :] = value

    place_ring(rank, pools, tok, pieces, store)
    meta_ref[...] = part_ref[:, 2 * width :]
    owners = [lax.div(hit_ref[0, i], held) for i in range(hits)]
    for i in range(hits):
        slot = jnp.int32(0)
        for earlier in range(i):
            slot = slot + (owners[earlier] == owners[i]).astype(jnp.int32)
        row = pl.multiple_of(owners[i] * tok + jnp.minimum(slot, HOT - 1) * block, block)
        kv_ref[i * block : (i + 1) * block, :] = part_ref[pl.ds(row, block), :width]
    prefix = hits * block
    kv_ref[prefix:, :] = part_ref[:, width : 2 * width]
    heads_kv = width // (2 * HD)
    group = model // (heads_kv * HD)
    rows, keys = bias_ref.shape
    stack = rows // tok
    col = lax.broadcasted_iota(jnp.int32, (rows, keys), 1)
    position = lax.rem(lax.broadcasted_iota(jnp.int32, (rows, keys), 0), tok) + rank * tok
    bias_ref[...] = jnp.where(col - prefix <= position, 0.0, MASKED)

    def some_heads(n, squares):
        lane = lambda at: pl.ds(pl.multiple_of(at * HD, HD), HD)
        first = n * stack
        g = lax.div(first, group)
        query = jnp.concatenate([query_ref[:, lane(first + h)] for h in range(stack)], axis=0)
        scores = lax.dot_general(
            query, kv_ref[:, lane(g)], (((1,), (1,)), ((), ())), preferred_element_type=F32
        )
        scores = scores * HD ** (-0.5) + bias_ref[...]
        weights = jnp.exp(scores - jnp.max(scores, axis=-1, keepdims=True))
        row_sum = jnp.sum(weights, axis=-1, keepdims=True)
        mixed = jnp.dot(
            weights.astype(BF16), kv_ref[:, lane(heads_kv + g)], preferred_element_type=F32
        )
        mixed = (mixed / row_sum).astype(BF16)
        for h in range(stack):
            part = mixed[h * tok : (h + 1) * tok]
            attended_ref[:, lane(first + h)] = part
            wide = residual_ref[:, lane(first + h)].astype(F32) + part.astype(F32)
            resid = wide.astype(BF16)
            resid_ref[:, lane(first + h)] = resid
            wide = resid.astype(F32)
            squares = squares + wide * wide
        return squares

    squares = lax.fori_loop(
        0,
        model // (2 * stack * HD),
        lambda n, squares: some_heads(2 * n + 1, some_heads(2 * n, squares)),
        jnp.zeros((tok, HD), F32),
    )
    inv_rms = lax.rsqrt(jnp.sum(squares, axis=-1, keepdims=True) / model + EPSILON)
    normed_ref[...] = (resid_ref[...].astype(F32) * inv_rms * gain_ref[...]).astype(BF16)


def offset_of(piece):
    far = lax.div(piece + 1, 2)
    return jnp.where((lax.rem(piece, 2) == 1) & (piece < 7), -far, far)


def route_kernel(
    rank_ref, meta_ref, take_near_ref, take_far_ref, mix_near_ref, mix_far_ref, named_ref, *, pools, top
):
    tok = meta_ref.shape[0] // pools
    rank = rank_ref[0]
    plane = take_near_ref.shape[0] // NEAR_SLOTS
    before = (
        lax.broadcasted_iota(jnp.int32, (tok, tok), 1)
        < lax.broadcasted_iota(jnp.int32, (tok, tok), 0)
    ).astype(BF16)
    for near, per, take_ref, mix_ref in (
        (True, NEAR_SLOTS, take_near_ref, mix_near_ref),
        (False, FAR_SLOTS, take_far_ref, mix_far_ref),
    ):
        slots, rows = take_ref.shape
        slot = lax.broadcasted_iota(jnp.int32, (1, slots), 1)
        inner = lax.rem(slot, per)
        shared = (per // MOST) * MOST
        expert = (lax.div(slot, per) + rank * plane).astype(F32)
        of_piece = jnp.where(inner < shared, lax.div(inner, MOST) + (1 if near else NEAR), 0)
        own_place = inner - shared if near else MOST - 1
        place = jnp.where(inner < shared, lax.rem(inner, MOST), own_place).astype(F32)

        def one_piece(at, carry):
            piece = at if near else jnp.where(at == 0, 0, at + NEAR - 1)
            row = lax.rem(rank + pools + offset_of(piece), pools) * tok
            meta = meta_ref[pl.ds(pl.multiple_of(row, tok), tok), :].astype(F32)
            named = jnp.zeros((tok, slots), F32)
            high = jnp.zeros((tok, slots), F32)
            low = jnp.zeros((tok, slots), F32)
            for j in range(top):
                same = meta[:, j : j + 1] == expert
                named = jnp.where(same, 1.0, named)
                high = jnp.where(same, meta[:, top + j : top + j + 1], high)
                low = jnp.where(same, meta[:, 2 * top + j : 2 * top + j + 1], low)
            count = jnp.dot(before, named.astype(BF16), preferred_element_type=F32)
            chosen = (named > 0.5) & (count == jnp.where(of_piece == piece, place, -1.0))
            here = pl.ds(pl.multiple_of(at * tok, tok), tok)
            named_ref[here, :slots] = jnp.where(chosen, 1.0, 0.0)
            mix_ref[0, here, :] = jnp.where(chosen, high, 0.0).astype(BF16)
            mix_ref[1, here, :] = jnp.where(chosen, low, 0.0).astype(BF16)
            return carry

        lax.fori_loop(0, rows // tok, one_piece, 0)
        take_ref[...] = named_ref[:rows, :slots].T.astype(BF16)


def by_columns(width, body):
    def step(n, carry):
        body(pl.ds(pl.multiple_of(n * COLS, COLS), COLS))
        return carry

    lax.fori_loop(0, width // COLS, step, 0)


def pack_kernel(take_ref, *refs):
    pieces, (out_ref, rows_ref, packed_ref, sem) = refs[:-4], refs[-4:]
    wide = packed_ref.shape[2]

    def leave(n):
        cols = pl.ds(pl.multiple_of(n * wide, wide), wide)
        return pltpu.make_async_copy(packed_ref.at[n], out_ref.at[:, cols], sem.at[n])

    def step(n, carry):
        cols = pl.ds(pl.multiple_of(n * wide, wide), wide)
        at = 0
        for piece in pieces:
            rows_ref[at : at + piece.shape[0], :] = piece[:, cols]
            at += piece.shape[0]
        packed_ref[n] = jnp.dot(
            take_ref[...], rows_ref[...], preferred_element_type=F32
        ).astype(BF16)
        leave(n).start()
        return carry

    parts = sem.shape[0]
    lax.fori_loop(0, parts, step, 0)
    for n in range(parts):
        leave(n).wait()


def expert_kernel(
    x, g0, g1, u0, u1, d0, d1, out, x_ref, grow_ref, down_ref, sum_ref, hidden_ref, y_ref, x_sem, grow_sem, down_sem, out_sem
):
    half = g0.shape[1]
    parts = x_sem.shape[0]
    deep = x.shape[1] // parts
    ends = out_sem.shape[0]
    wide = out.shape[1] // ends

    def row_copy(n):
        cols = pl.ds(pl.multiple_of(n * deep, deep), deep)
        return pltpu.make_async_copy(x.at[:, cols], x_ref.at[:, cols], x_sem.at[n])

    def grow_copies(slab, n, gate, up):
        rows = pl.ds(pl.multiple_of(n * deep, deep), deep)
        return [
            pltpu.make_async_copy(
                w.at[rows, :],
                grow_ref.at[slab, rows, pl.ds(at * half, half)],
                grow_sem.at[slab, n, at],
            )
            for at, w in enumerate((gate, up))
        ]

    def down_copies(n):
        cols = pl.ds(pl.multiple_of(n * wide, wide), wide)
        return [
            pltpu.make_async_copy(
                w.at[:, cols], down_ref.at[n, pl.ds(at * half, half), :], down_sem.at[n, at]
            )
            for at, w in enumerate((d0, d1))
        ]

    def leave(n):
        cols = pl.ds(pl.multiple_of(n * wide, wide), wide)
        return pltpu.make_async_copy(y_ref.at[n], out.at[:, cols], out_sem.at[n])

    for slab, (gate, up) in enumerate(((g0, u0), (g1, u1))):
        for n in range(parts):
            if slab == 0:
                row_copy(n).start()
            for copy in grow_copies(slab, n, gate, up):
                copy.start()
    for n in range(ends):
        for copy in down_copies(n):
            copy.start()

    def grow(step, carry):
        slab, n = lax.div(step, parts), lax.rem(step, parts)

        @pl.when(slab == 0)
        def _():
            row_copy(n).wait()

        for copy in grow_copies(slab, n, g0, u0):
            copy.wait()
        part = pl.ds(pl.multiple_of(n * deep, deep), deep)
        grown = jnp.dot(x_ref[:, part], grow_ref[slab, part, :], preferred_element_type=F32)
        sum_ref[slab] += grown
        return carry

    sum_ref[...] = jnp.zeros(sum_ref.shape, F32)
    lax.fori_loop(0, 2 * parts, grow, 0)
    for slab in range(2):
        gate, up = sum_ref[slab, :, :half], sum_ref[slab, :, half:]
        hidden = gate / (1.0 + jnp.exp(-gate)) * up
        hidden_ref[:, slab * half : (slab + 1) * half] = hidden.astype(BF16)

    def shrink(n, carry):
        for copy in down_copies(n):
            copy.wait()
        y_ref[n] = jnp.dot(
            hidden_ref[...], down_ref[n], preferred_element_type=F32
        ).astype(BF16)
        leave(n).start()
        return carry

    lax.fori_loop(0, ends, shrink, 0)
    for n in range(ends):
        leave(n).wait()


def weighted(mix_ref, first, last, y):
    return jnp.dot(mix_ref[0, first:last, :], y, preferred_element_type=F32) + jnp.dot(
        mix_ref[1, first:last, :], y, preferred_element_type=F32
    )


def far_kernel(mix_ref, y_ref, own_ref, third_ref, right_ref, left_ref):
    tok = own_ref.shape[0]
    half = tok // 2

    def body(cols):
        mixed = weighted(mix_ref, 0, mix_ref.shape[1], y_ref[:, cols])
        own_ref[:, cols] = mixed[:tok]
        third_ref[:, cols] = mixed[tok : 3 * tok]
        right_ref[:, cols] = mixed[3 * tok : 3 * tok + half].astype(BF16)
        left_ref[:, cols] = mixed[3 * tok + half :].astype(BF16)

    by_columns(y_ref.shape[1], body)


def third_kernel(third_ref, from_left_ref, from_right_ref, right_ref, left_ref):
    tok = right_ref.shape[0]
    half = tok // 2

    def body(cols):
        from_left = from_left_ref[:, cols].astype(F32)
        from_right = from_right_ref[:, cols].astype(F32)
        right_ref[:half, cols] = (third_ref[tok : tok + half, cols] + from_left).astype(BF16)
        right_ref[half:, cols] = third_ref[tok + half :, cols].astype(BF16)
        left_ref[:half, cols] = third_ref[:half, cols].astype(BF16)
        left_ref[half:, cols] = (third_ref[half:tok, cols] + from_right).astype(BF16)

    by_columns(right_ref.shape[1], body)


def second_kernel(
    mix, y_ref, from_left, from_right, right_ref, left_ref, mix_ref, from_left_ref, from_right_ref, sem
):
    tok = right_ref.shape[0]
    copies = [
        pltpu.make_async_copy(
            mix.at[n, pl.ds(3 * tok, 2 * tok), :], mix_ref.at[n], sem.at[n]
        )
        for n in range(2)
    ]
    copies.append(pltpu.make_async_copy(from_left, from_left_ref, sem.at[2]))
    copies.append(pltpu.make_async_copy(from_right, from_right_ref, sem.at[3]))
    for copy in copies:
        copy.start()
    for copy in copies:
        copy.wait()

    def body(cols):
        mixed = weighted(mix_ref, 0, 2 * tok, y_ref[:, cols])
        left_ref[:, cols] = (mixed[:tok] + from_right_ref[:, cols].astype(F32)).astype(BF16)
        right_ref[:, cols] = (mixed[tok:] + from_left_ref[:, cols].astype(F32)).astype(BF16)

    by_columns(y_ref.shape[1], body)


def first_kernel(mix_ref, y_ref, resid_ref, own_ref, base_ref, first_ref):
    tok = resid_ref.shape[0]

    def body(cols):
        mixed = weighted(mix_ref, 0, 3 * tok, y_ref[:, cols])
        base_ref[:, cols] = mixed[:tok] + own_ref[:, cols] + resid_ref[:, cols].astype(F32)
        first_ref[:, cols] = mixed[tok:]

    by_columns(y_ref.shape[1], body)


def add_kernel(first_ref, from_left_ref, from_right_ref, right_ref, left_ref):
    tok = right_ref.shape[0]
    left_ref[...] = (first_ref[:tok] + from_right_ref[...].astype(F32)).astype(BF16)
    right_ref[...] = (first_ref[tok:] + from_left_ref[...].astype(F32)).astype(BF16)


def last_kernel(base_ref, from_left_ref, from_right_ref, out_ref):
    total = base_ref[...] + from_left_ref[...].astype(F32) + from_right_ref[...].astype(F32)
    out_ref[...] = total.astype(BF16)


def ring(block, pools):
    right = [(k, (k + 1) % pools) for k in range(pools)]
    left = [(k, (k - 1) % pools) for k in range(pools)]
    pieces = [block]
    from_left = from_right = block
    for _ in range(1, pools // 2):
        from_left = lax.ppermute(from_left, "pool", right)
        from_right = lax.ppermute(from_right, "pool", left)
        pieces += [from_left, from_right]
    half = block.shape[0] // 2
    pieces += [
        lax.ppermute(from_left[:half], "pool", right),
        lax.ppermute(from_right[half:], "pool", left),
    ]
    return pieces


def shards(
    residual,
    queries,
    fresh_kv,
    pool_cache,
    hit_blocks,
    norm_gain,
    route_ids,
    route_logits,
    w_gate,
    w_up,
    w_down,
):
    pools = lax.axis_size("pool")
    plane = lax.axis_size("xy")
    rank = lax.axis_index("pool").astype(jnp.int32)[None]
    _, tok, model = queries.shape
    held, block, width = pool_cache.shape
    hits = hit_blocks.shape[1]
    top = route_ids.shape[2]
    half = w_gate.shape[2]
    shape = jax.ShapeDtypeStruct

    swap = [(0, 1), (1, 0)]
    own = (w_gate[0], w_up[0], w_down[0])
    peer = tuple(lax.ppermute(w, "core", swap) for w in own)

    (packed,) = held_call(
        gather_kernel,
        "gather_block",
        [shape((tok, 2 * width + META), BF16)],
        [
            rank,
            hit_blocks,
            (pool_cache,),
            Fetched((fresh_kv[0],)),
            Fetched((route_ids[0].T,)),
            Fetched((route_logits[0].T,)),
        ],
        scalars=2,
        near=(0,),
        scratch=[pltpu.SemaphoreType.DMA((HOT,))],
    )
    pieces = ring(packed, pools)

    stack = 4
    keys = hits * block + pools * tok
    attended, resid, normed, meta = held_call(
        lambda *refs: attend_kernel(*refs, pools=pools, held=held),
        "attend",
        [shape((tok, model), BF16)] * 3 + [shape((pools * tok, META), BF16)],
        [
            rank,
            hit_blocks,
            Fetched((norm_gain[None],)),
            Fetched((queries[0],)),
            Fetched((residual[0],)),
            *pieces,
        ],
        scalars=2,
        near=(2, 3),
        scratch=[
            pltpu.VMEM((pools * tok, 2 * width + META), BF16),
            pltpu.VMEM((keys, width), BF16),
            pltpu.VMEM((stack * tok, keys), F32),
        ],
    )

    near_slots, far_slots = plane * NEAR_SLOTS, plane * FAR_SLOTS
    near_rows, far_rows = NEAR * tok, (pools - NEAR + 1) * tok
    take_near, take_far, mix_near, mix_far = held_call(
        lambda *refs: route_kernel(*refs, pools=pools, top=top),
        "route",
        [
            shape((near_slots, near_rows), BF16),
            shape((far_slots, far_rows), BF16),
            shape((2, near_rows, near_slots), BF16),
            shape((2, far_rows, far_slots), BF16),
        ],
        [rank, meta],
        scalars=1,
        near=(0,),
        scratch=[pltpu.VMEM((near_rows, near_slots), F32)],
    )

    def pack(take, parts_in, name):
        slots, rows = (take[0] if isinstance(take, tuple) else take).shape
        parts = model // COLS
        (out,) = held_call(
            pack_kernel,
            name,
            [shape((slots, model), BF16)],
            [take, *parts_in],
            far=(0,),
            scratch=[
                pltpu.VMEM((rows, COLS), BF16),
                pltpu.VMEM((parts, slots, COLS), BF16),
                pltpu.SemaphoreType.DMA((parts,)),
            ],
            limit=32,
        )
        return out

    def exchange(x):
        slots = x.shape[0]
        x = x.reshape(plane, slots // plane, model)
        return lax.all_to_all(x, "xy", split_axis=0, concat_axis=0, tiled=True).reshape(
            slots, model
        )

    def expert(x, name):
        slots = x.shape[0]
        parts, ends = 4, 4
        dma = pltpu.SemaphoreType.DMA
        (out,) = held_call(
            expert_kernel,
            name,
            [shape((slots, model), BF16)],
            [(x,)] + [(w,) for pair in zip(own, peer) for w in pair],
            far=(0,),
            scratch=[
                pltpu.VMEM((slots, model), BF16),
                pltpu.VMEM((2, model, 2 * half), BF16),
                pltpu.VMEM((ends, 2 * half, model // ends), BF16),
                pltpu.VMEM((2, slots, 2 * half), F32),
                pltpu.VMEM((slots, 2 * half), BF16),
                pltpu.VMEM((ends, slots, model // ends), BF16),
                dma((parts,)),
                dma((2, parts, 2)),
                dma((ends, 2)),
                dma((ends,)),
            ],
            limit=48,
        )
        return out

    right = [(k, (k + 1) % pools) for k in range(pools)]
    left = [(k, (k - 1) % pools) for k in range(pools)]
    send = lambda r, l: (lax.ppermute(r, "pool", right), lax.ppermute(l, "pool", left))
    tie = lax.optimization_barrier

    once = send(normed, normed)
    once, take_near, peer = tie((once, take_near, peer))
    twice = send(*once)
    sent_near = pack(take_near, [normed, *once, *twice], "pack_near")
    thrice = send(*twice)
    fourth = send(thrice[0][: tok // 2], thrice[1][tok // 2 :])
    sent_far = pack(Fetched((take_far,)), [Fetched((normed,)), *thrice, *fourth], "pack_far")
    got_near = exchange(sent_near)
    got_near, sent_far = tie((got_near, sent_far))
    got_far = exchange(sent_far)
    out_near = expert(got_near, "expert_near")
    got_far, out_near = tie((got_far, out_near))
    out_far = expert(got_far, "expert_far")
    back_far = exchange(out_far)
    out_near, back_far = tie((out_near, back_far))
    back_near = exchange(out_near)

    row, pair = (tok, model), (2 * tok, model)
    own_far, third, *moving = held_call(
        far_kernel,
        "mix_far",
        [shape(row, F32), shape(pair, F32)] + [shape((tok // 2, model), BF16)] * 2,
        [Fetched((mix_far,)), Fetched((back_far,))],
        near=(1, 2, 3),
    )
    moving = held_call(
        third_kernel,
        "add_third",
        [shape(row, BF16)] * 2,
        [third, *send(*moving)],
        near=(0, 1),
        limit=16,
    )
    moving = held_call(
        second_kernel,
        "mix_second",
        [shape(row, BF16)] * 2,
        [in_hbm(mix_near), back_near, *[in_hbm(m) for m in send(*moving)]],
        near=(0, 1),
        scratch=[
            pltpu.VMEM((2, 2 * tok, near_slots), BF16),
            pltpu.VMEM(row, BF16),
            pltpu.VMEM(row, BF16),
            pltpu.SemaphoreType.DMA((4,)),
        ],
        limit=24,
    )
    moving = send(*moving)
    base, first = held_call(
        first_kernel,
        "mix_first",
        [shape(row, F32), shape(pair, F32)],
        [Fetched((mix_near,)), back_near, Fetched((resid,)), Fetched((own_far,))],
        near=(0, 1),
        limit=24,
    )
    moving = held_call(
        add_kernel, "add_first", [shape(row, BF16)] * 2, [first, *moving], near=(0, 1), limit=16
    )
    (layer_out,) = held_call(
        last_kernel, "add_last", [shape(row, BF16)], [base, *send(*moving)], limit=16
    )
    return (attended[None], layer_out[None])


def solution(mesh):
    pools, experts = mesh.devices.shape
    fine = Mesh(mesh.devices.reshape(pools, experts // 2, 2), ("pool", "xy", "core"))
    ex = ("xy", "core")
    tokens = P(ex, "pool", None)
    slab = P(("pool", "xy", "core"), None, None)
    placed = (
        tokens,
        tokens,
        tokens,
        P("pool", None, None),
        P(ex, None),
        P(),
        tokens,
        tokens,
        slab,
        slab,
        slab,
    )
    return jax.shard_map(
        shards, mesh=fine, in_specs=placed, out_specs=(tokens, tokens), check_vma=False
    )
```

time: 335 us -> 241 us (0.72)
  waiting for transfers between devices: 156 us -> 88.6 us
  blocking collectives: 58 us -> 23.9 us
  starting transfers between devices: 33.4 us -> 66.7 us
  between operations: 14.2 us -> 0.8 us
  Pallas kernels: 62.5 us -> 54.2 us
  local copies, waits for them, and re-layouts: 7.44 us -> 2.56 us
    ppermute x0 -> x16, waiting for transfers between devices: none -> 55.1 us  [the longest x8 53.7 us: shards(): lax.ppermute(r, 'pool', right)]
    reduce_scatter x1 -> x0, waiting for transfers between devices: 52.1 us -> none  [shards(): mix = lax.psum_scatter(mixed, 'pool', scatter_dimension=0, tiled=True)]
    ppermute x6 -> x3, waiting for transfers between devices: 40.8 us -> 0.01 us  [ring(): from_right = lax.ppermute(from_right, 'pool', left)]
    all_to_all x1, blocking collectives: 58 us -> 23.9 us  [exchange(): lax.all_to_all(x, 'xy', split_axis=0, concat_axis=0, tiled=True)]
    ppermute x0 -> x16, starting transfers between devices: none -> 27 us  [the longest x8 15.6 us: shards(): lax.ppermute(l, 'pool', left)]
    all_to_all x1 -> x3, waiting for transfers between devices: 44.3 us -> 20.2 us  [exchange(): lax.all_to_all(x, 'xy', split_axis=0, concat_axis=0, tiled=True)]
    all_to_all x1 -> x3, starting transfers between devices: 7.6 us -> 23.4 us  [exchange(): lax.all_to_all(x, 'xy', split_axis=0, concat_axis=0, tiled=True)]
    ppermute x3, waiting for transfers between devices: 12.2 us -> 0.01 us  [shards(): peer = tuple((lax.ppermute(w, 'core', swap) for w in own))]
  transfers between devices with their start and end apart: 21 -> 30, of which waited for: 14 -> 17; matrix products, arithmetic and copies ran while one was open for 0% -> 0% of each run, Pallas kernels for 2% -> 16%
where the time goes in v2:
time: 241 us; the launch traced here: 237 us
  waiting for transfers between devices  88.6 us (37%)
  starting transfers between devices  66.7 us (28%)
  Pallas kernels  54.2 us (22%)
  blocking collectives  23.9 us (10%)
  local copies, waits for them, and re-layouts  2.56 us (1%)
    pallas_call x13, Pallas kernels, held_call(): pl.pallas_call(kernel, in_specs=specs, out_specs=[ANY if n in far else VM...  54.2 us
    ppermute x8, waiting for transfers between devices, shards(): lax.ppermute(r, 'pool', right)  53.7 us
    all_to_all x1, blocking collectives, exchange(): lax.all_to_all(x, 'xy', split_axis=0, concat_axis=0, tiled=True)  23.9 us
    all_to_all x3, starting transfers between devices, exchange(): lax.all_to_all(x, 'xy', split_axis=0, concat_axis=0, tiled=True)  23.4 us
    all_to_all x3, waiting for transfers between devices, exchange(): lax.all_to_all(x, 'xy', split_axis=0, concat_axis=0, tiled=True)  20.2 us
    ppermute x8, starting transfers between devices, shards(): lax.ppermute(l, 'pool', left)  15.6 us
    ppermute x8, starting transfers between devices, shards(): lax.ppermute(r, 'pool', right)  11.4 us
    ppermute x3, waiting for transfers between devices, ring(): from_left = lax.ppermute(from_left, 'pool', right)  11 us
  transfers between devices with their start and end apart: 30, of which 17 were waited for; matrix products, arithmetic and copies ran while one was open for 0% of the time, Pallas kernels for 16%

profile of v2, /device:TPU:12, one launch (start us, length us, event | category | flops | bytes accessed | tf_op | source)
XLA Modules:
  0.0 236.8 jit_solution(18127102102877098724)
XLA Ops:
  5.2 4.0 %collective-permute-start.1 = (bf16[64,1152]{1,0:T(8,128)(2,1)S(1)}, bf16[64,1152]{1,0:T(8,128)(2,1)S(1)}, u32[]{:S(2)}, u32[]{:S(2)}) collective-permute-start(bf16[64,1152]{1,0:T(8,128)(2,1)S(1)} %gather_block.1.refs_5_), channel_id=1, source_target_pairs={{0,224},{32,0},{64,32},{96,64},{128,96},{160,128},{192,160},{224,1... | collective-permute-start | bytes 442376 | tf_op jit(solution)/shard_map/ppermute | solution.py:430
  9.2 4.3 %collective-permute-done.refs_6_ = bf16[64,1152]{1,0:T(8,128)(2,1)S(1)} collective-permute-done((bf16[64,1152]{1,0:T(8,128)(2,1)S(1)}, bf16[64,1152]{1,0:T(8,128)(2,1)S(1)}, u32[]{:S(2)}, u32[]{:S(2)}) %collective-permute-start) | collective-permute-done | bytes 147488 | tf_op jit(solution)/shard_map/ppermute | solution.py:429
  16.7 3.6 %collective-permute-done.2.refs_8_ = bf16[64,1152]{1,0:T(8,128)(2,1)S(1)} collective-permute-done((bf16[64,1152]{1,0:T(8,128)(2,1)S(1)}, bf16[64,1152]{1,0:T(8,128)(2,1)S(1)}, u32[]{:S(2)}, u32[]{:S(2)}) %collective-permute-start.2) | collective-permute-done | bytes 147488 | tf_op jit(solution)/shard_map/ppermute | solution.py:429
  32.2 6.8 %attend.1 = (bf16[64,4096]{1,0:T(8,128)(2,1)}, bf16[64,4096]{1,0:T(8,128)(2,1)}, bf16[64,4096]{1,0:T(8,128)(2,1)S(1)}, bf16[512,128]{1,0:T(8,128)(2,1)S(1)}) custom-call(s32[1]{0:T(128)} %bitcast.rank_ref.refs_0_, s32[1,16]{1,0:T(1,128)} %refs_1_.1, f32[1,4096]{1,0:T(1,128)} %bitcast.43, bf16[64,4096]{1,0:T(8,128)(2,1)} %bitcast.40, ...), custom_call_target="tpu_custom_call" | custom-call | tf_op jit(solution)/shard_map/attend/pallas_call | solution.py:44
  39.0 3.3 %collective-permute-start.9 = (bf16[64,4096]{1,0:T(8,128)(2,1)S(1)}, bf16[64,4096]{1,0:T(8,128)(2,1)S(1)}, u32[]{:S(2)}, u32[]{:S(2)}) collective-permute-start(bf16[64,4096]{1,0:T(8,128)(2,1)S(1)} %get-tuple-element.37.refs_0_), channel_id=1, source_target_pairs={{0,224},{32,0},{64,32},{96,64},{128,96},{160,128},{192,160},{224,1... | collective-permute-start | bytes 1572872 | tf_op jit(solution)/shard_map/ppermute | solution.py:578
  42.3 4.0 %route.1 = (bf16[384,320]{1,0:T(8,128)(2,1)S(1)}, bf16[256,256]{1,0:T(8,128)(2,1)}, bf16[2,320,384]{2,1,0:T(8,128)(2,1)}, bf16[2,256,256]{2,1,0:T(8,128)(2,1)}) custom-call(s32[1]{0:T(128)} %bitcast.rank_ref.refs_0_, bf16[512,128]{1,0:T(8,128)(2,1)S(1)} %get-tuple-element.35.refs_1_), custom_call_target="tpu_custom_call" | custom-call | tf_op jit(solution)/shard_map/route/pallas_call | solution.py:44
  46.4 4.5 %collective-permute-done.8.refs_1_ = bf16[64,4096]{1,0:T(8,128)(2,1)S(1)} collective-permute-done((bf16[64,4096]{1,0:T(8,128)(2,1)S(1)}, bf16[64,4096]{1,0:T(8,128)(2,1)S(1)}, u32[]{:S(2)}, u32[]{:S(2)}) %collective-permute-start.8) | collective-permute-done | bytes 524320 | tf_op jit(solution)/shard_map/ppermute | solution.py:578
  54.4 7.6 %collective-permute-done.13.refs_3_ = bf16[64,4096]{1,0:T(8,128)(2,1)S(1)} collective-permute-done((bf16[64,4096]{1,0:T(8,128)(2,1)S(1)}, bf16[64,4096]{1,0:T(8,128)(2,1)S(1)}, u32[]{:S(2)}, u32[]{:S(2)}) %collective-permute-start.13) | collective-permute-done | bytes 524320 | tf_op jit(solution)/shard_map/ppermute | solution.py:578
  66.3 7.3 %all-to-all-start = ((bf16[16,24,4096]{2,1,0:T(8,128)(2,1)}), bf16[16,24,4096]{2,1,0:T(8,128)(2,1)}, u32[]{:S(2)}, u32[]{:S(2)}) async-start(bf16[16,24,4096]{2,1,0:T(8,128)(2,1)} %bitcast.13), calls=%async_computation | async-start | bytes 6291456 | tf_op jit(solution)/shard_map/all_to_all | solution.py:546
  76.9 10.0 %collective-permute-done.15.refs_1_ = bf16[64,4096]{1,0:T(8,128)(2,1)S(1)} collective-permute-done((bf16[64,4096]{1,0:T(8,128)(2,1)S(1)}, bf16[64,4096]{1,0:T(8,128)(2,1)S(1)}, u32[]{:S(2)}, u32[]{:S(2)}) %collective-permute-start.15) | collective-permute-done | bytes 524320 | tf_op jit(solution)/shard_map/ppermute | solution.py:578
  90.3 4.2 %collective-permute-done.17.refs_3_ = bf16[32,4096]{1,0:T(8,128)(2,1)S(1)} collective-permute-done((bf16[32,4096]{1,0:T(8,128)(2,1)S(1)}, bf16[32,4096]{1,0:T(8,128)(2,1)S(1)}, u32[]{:S(2)}, u32[]{:S(2)}) %collective-permute-start.17) | collective-permute-done | bytes 262176 | tf_op jit(solution)/shard_map/ppermute | solution.py:578
  96.6 11.9 %all-to-all-done = bf16[16,24,4096]{2,1,0:T(8,128)(2,1)} async-done(((bf16[16,24,4096]{2,1,0:T(8,128)(2,1)}), bf16[16,24,4096]{2,1,0:T(8,128)(2,1)}, u32[]{:S(2)}, u32[]{:S(2)}) %all-to-all-start) | async-done | bytes 3145760 | tf_op jit(solution)/shard_map/all_to_all | solution.py:546
  108.5 8.9 %all-to-all-start.1 = ((bf16[16,16,4096]{2,1,0:T(8,128)(2,1)}), bf16[16,16,4096]{2,1,0:T(8,128)(2,1)S(1)}, u32[]{:S(2)}, u32[]{:S(2)}) async-start(bf16[16,16,4096]{2,1,0:T(8,128)(2,1)} %bitcast.15), calls=%async_computation.1 | async-start | bytes 4194304 | tf_op jit(solution)/shard_map/all_to_all | solution.py:546
  117.4 15.1 %expert_near.1 = bf16[384,4096]{1,0:T(8,128)(2,1)S(1)} custom-call(bf16[384,4096]{1,0:T(8,128)(2,1)} %bitcast.14.x, bf16[4096,384]{1,0:T(8,128)(2,1)} %bitcast.30, bf16[4096,384]{1,0:T(8,128)(2,1)} %collective-permute-done.10.g1, bf16[4096,384]{1,0:T(8,128)(2,1)} %bitcast.33, bf16[4096,384]{1,0:T(8,128)(2,1)} %collective-permute-done.11.u1, ...), custom_call_target="tpu_custom_call" | custom-call | tf_op jit(solution)/shard_map/expert_near/pallas_call | solution.py:44
  134.2 3.3 %all-to-all-done.1 = bf16[16,16,4096]{2,1,0:T(8,128)(2,1)S(1)} async-done(((bf16[16,16,4096]{2,1,0:T(8,128)(2,1)}), bf16[16,16,4096]{2,1,0:T(8,128)(2,1)S(1)}, u32[]{:S(2)}, u32[]{:S(2)}) %all-to-all-start.1) | async-done | bytes 2097184 | tf_op jit(solution)/shard_map/all_to_all | solution.py:546
  137.5 9.8 %expert_far.1 = bf16[256,4096]{1,0:T(8,128)(2,1)S(1)} custom-call(bf16[256,4096]{1,0:T(8,128)(2,1)S(1)} %bitcast.27, bf16[4096,384]{1,0:T(8,128)(2,1)} %bitcast.31, bf16[4096,384]{1,0:T(8,128)(2,1)} %collective-permute-done.10.g1, bf16[4096,384]{1,0:T(8,128)(2,1)} %bitcast.34, bf16[4096,384]{1,0:T(8,128)(2,1)} %collective-permute-done.11.u1, ...), custom_call_target="tpu_custom_call" | custom-call | tf_op jit(solution)/shard_map/expert_far/pallas_call | solution.py:44
  147.4 23.9 %all_to_all.20 = bf16[16,16,4096]{2,1,0:T(8,128)(2,1)} all-to-all(bf16[16,16,4096]{2,1,0:T(8,128)(2,1)S(1)} %bitcast.28), channel_id=1, replica_groups=mesh['pool'=8,'xy'=16,'core'=2] {'xy'}, dimensions={0} | all-to-all | bytes 4194304 | tf_op jit(solution)/shard_map/all_to_all | solution.py:546
  171.2 7.1 %all-to-all-start.3 = ((bf16[16,24,4096]{2,1,0:T(8,128)(2,1)}), bf16[16,24,4096]{2,1,0:T(8,128)(2,1)S(1)}, u32[]{:S(2)}, u32[]{:S(2)}) async-start(bf16[16,24,4096]{2,1,0:T(8,128)(2,1)} %bitcast.26), calls=%async_computation.3 | async-start | bytes 6291456 | tf_op jit(solution)/shard_map/all_to_all | solution.py:546
  178.4 4.4 %mix_far.1 = (f32[64,4096]{1,0:T(8,128)}, f32[128,4096]{1,0:T(8,128)S(1)}, bf16[32,4096]{1,0:T(8,128)(2,1)S(1)}, bf16[32,4096]{1,0:T(8,128)(2,1)S(1)}) custom-call(bf16[2,256,256]{2,1,0:T(8,128)(2,1)} %get-tuple-element.52.mix_ref, bf16[256,4096]{1,0:T(8,128)(2,1)} %bitcast.38), custom_call_target="tpu_custom_call" | custom-call | tf_op jit(solution)/shard_map/mix_far/pallas_call | solution.py:44
  186.0 5.4 %collective-permute-done.19.from_left_ref = bf16[32,4096]{1,0:T(8,128)(2,1)S(1)} collective-permute-done((bf16[32,4096]{1,0:T(8,128)(2,1)S(1)}, bf16[32,4096]{1,0:T(8,128)(2,1)S(1)}, u32[]{:S(2)}, u32[]{:S(2)}) %collective-permute-start.19) | collective-permute-done | bytes 262176 | tf_op jit(solution)/shard_map/ppermute | solution.py:578
  195.2 6.8 %collective-permute-done.21.from_left = bf16[64,4096]{1,0:T(8,128)(2,1)S(1)} collective-permute-done((bf16[64,4096]{1,0:T(8,128)(2,1)S(1)}, bf16[64,4096]{1,0:T(8,128)(2,1)S(1)}, u32[]{:S(2)}, u32[]{:S(2)}) %collective-permute-start.21) | collective-permute-done | bytes 524320 | tf_op jit(solution)/shard_map/ppermute | solution.py:578
  202.8 5.0 %all-to-all-done.3 = bf16[16,24,4096]{2,1,0:T(8,128)(2,1)S(1)} async-done(((bf16[16,24,4096]{2,1,0:T(8,128)(2,1)}), bf16[16,24,4096]{2,1,0:T(8,128)(2,1)S(1)}, u32[]{:S(2)}, u32[]{:S(2)}) %all-to-all-start.3) | async-done | bytes 3145760 | tf_op jit(solution)/shard_map/all_to_all | solution.py:546
  216.8 8.0 %collective-permute-done.23.from_left_ref = bf16[64,4096]{1,0:T(8,128)(2,1)S(1)} collective-permute-done((bf16[64,4096]{1,0:T(8,128)(2,1)S(1)}, bf16[64,4096]{1,0:T(8,128)(2,1)S(1)}, u32[]{:S(2)}, u32[]{:S(2)}) %collective-permute-start.23) | collective-permute-done | bytes 524320 | tf_op jit(solution)/shard_map/ppermute | solution.py:578
  228.2 7.2 %collective-permute-done.25.from_left_ref = bf16[64,4096]{1,0:T(8,128)(2,1)S(1)} collective-permute-done((bf16[64,4096]{1,0:T(8,128)(2,1)S(1)}, bf16[64,4096]{1,0:T(8,128)(2,1)S(1)}, u32[]{:S(2)}, u32[]{:S(2)}) %collective-permute-start.25) | collective-permute-done | bytes 524320 | tf_op jit(solution)/shard_map/ppermute | solution.py:578
  (66 shorter events, 59.5 us)
Async XLA Ops:
  0.6 50.3 %collective-permute-start.10 = (bf16[4096,384]{1,0:T(8,128)(2,1)}, bf16[4096,384]{1,0:T(8,128)(2,1)}, u32[]{:S(2)}, u32[]{:S(2)}) collective-permute-start(bf16[4096,384]{1,0:T(8,128)(2,1)} %bitcast.29), channel_id=1, source_target_pairs={{0,1},{1,0},{2,3},{3,2},{4,5},{5,4},{6,7},{7,6},{8,9},{9,8},{10,11... | collective-permute-start | bytes 9437192 | tf_op jit(solution)/shard_map/ppermute | solution.py:465
  0.7 50.2 %collective-permute-start.11 = (bf16[4096,384]{1,0:T(8,128)(2,1)}, bf16[4096,384]{1,0:T(8,128)(2,1)}, u32[]{:S(2)}, u32[]{:S(2)}) collective-permute-start(bf16[4096,384]{1,0:T(8,128)(2,1)} %bitcast.32), channel_id=1, source_target_pairs={{0,1},{1,0},{2,3},{3,2},{4,5},{5,4},{6,7},{7,6},{8,9},{9,8},{10,11... | collective-permute-start | bytes 9437192 | tf_op jit(solution)/shard_map/ppermute | solution.py:465
  1.2 49.7 %collective-permute-start.12 = (bf16[384,4096]{1,0:T(8,128)(2,1)}, bf16[384,4096]{1,0:T(8,128)(2,1)}, u32[]{:S(2)}, u32[]{:S(2)}) collective-permute-start(bf16[384,4096]{1,0:T(8,128)(2,1)} %bitcast.35), channel_id=1, source_target_pairs={{0,1},{1,0},{2,3},{3,2},{4,5},{5,4},{6,7},{7,6},{8,9},{9,8},{10,11... | collective-permute-start | bytes 9437192 | tf_op jit(solution)/shard_map/ppermute | solution.py:465
  3.2 10.3 %collective-permute-start = (bf16[64,1152]{1,0:T(8,128)(2,1)S(1)}, bf16[64,1152]{1,0:T(8,128)(2,1)S(1)}, u32[]{:S(2)}, u32[]{:S(2)}) collective-permute-start(bf16[64,1152]{1,0:T(8,128)(2,1)S(1)} %gather_block.1.refs_5_), channel_id=1, source_target_pairs={{0,32},{32,64},{64,96},{96,128},{128,160},{160,192},{192,224},{224... | collective-permute-start | bytes 442376 | tf_op jit(solution)/shard_map/ppermute | solution.py:429
  5.2 8.3 %collective-permute-start.1 = (bf16[64,1152]{1,0:T(8,128)(2,1)S(1)}, bf16[64,1152]{1,0:T(8,128)(2,1)S(1)}, u32[]{:S(2)}, u32[]{:S(2)}) collective-permute-start(bf16[64,1152]{1,0:T(8,128)(2,1)S(1)} %gather_block.1.refs_5_), channel_id=1, source_target_pairs={{0,224},{32,0},{64,32},{96,64},{128,96},{160,128},{192,160},{224,1... | collective-permute-start | bytes 442376 | tf_op jit(solution)/shard_map/ppermute | solution.py:430
  39.0 11.9 %collective-permute-start.8 = (bf16[64,4096]{1,0:T(8,128)(2,1)S(1)}, bf16[64,4096]{1,0:T(8,128)(2,1)S(1)}, u32[]{:S(2)}, u32[]{:S(2)}) collective-permute-start(bf16[64,4096]{1,0:T(8,128)(2,1)S(1)} %get-tuple-element.37.refs_0_), channel_id=1, source_target_pairs={{0,32},{32,64},{64,96},{96,128},{128,160},{160,192},{192,224},{224... | collective-permute-start | bytes 1572872 | tf_op jit(solution)/shard_map/ppermute | solution.py:578
  39.0 11.9 %collective-permute-start.9 = (bf16[64,4096]{1,0:T(8,128)(2,1)S(1)}, bf16[64,4096]{1,0:T(8,128)(2,1)S(1)}, u32[]{:S(2)}, u32[]{:S(2)}) collective-permute-start(bf16[64,4096]{1,0:T(8,128)(2,1)S(1)} %get-tuple-element.37.refs_0_), channel_id=1, source_target_pairs={{0,224},{32,0},{64,32},{96,64},{128,96},{160,128},{192,160},{224,1... | collective-permute-start | bytes 1572872 | tf_op jit(solution)/shard_map/ppermute | solution.py:578
  50.9 11.1 %collective-permute-start.13 = (bf16[64,4096]{1,0:T(8,128)(2,1)S(1)}, bf16[64,4096]{1,0:T(8,128)(2,1)S(1)}, u32[]{:S(2)}, u32[]{:S(2)}) collective-permute-start(bf16[64,4096]{1,0:T(8,128)(2,1)S(1)} %collective-permute-done.8.refs_1_), channel_id=1, source_target_pairs={{0,32},{32,64},{64,96},{96,128},{128,160},{160,192},{192,224},{224... | collective-permute-start | bytes 1572872 | tf_op jit(solution)/shard_map/ppermute | solution.py:578
  53.8 9.2 %collective-permute-start.14 = (bf16[64,4096]{1,0:T(8,128)(2,1)S(1)}, bf16[64,4096]{1,0:T(8,128)(2,1)S(1)}, u32[]{:S(2)}, u32[]{:S(2)}) collective-permute-start(bf16[64,4096]{1,0:T(8,128)(2,1)S(1)} %collective-permute-done.9.refs_2_), channel_id=1, source_target_pairs={{0,224},{32,0},{64,32},{96,64},{128,96},{160,128},{192,160},{224,1... | collective-permute-start | bytes 1572872 | tf_op jit(solution)/shard_map/ppermute | solution.py:578
  66.3 42.2 %all-to-all-start = ((bf16[16,24,4096]{2,1,0:T(8,128)(2,1)}), bf16[16,24,4096]{2,1,0:T(8,128)(2,1)}, u32[]{:S(2)}, u32[]{:S(2)}) async-start(bf16[16,24,4096]{2,1,0:T(8,128)(2,1)} %bitcast.13), calls=%async_computation | async-start | bytes 6291456 | tf_op jit(solution)/shard_map/all_to_all | solution.py:546
  73.6 13.2 %collective-permute-start.15 = (bf16[64,4096]{1,0:T(8,128)(2,1)S(1)}, bf16[64,4096]{1,0:T(8,128)(2,1)S(1)}, u32[]{:S(2)}, u32[]{:S(2)}) collective-permute-start(bf16[64,4096]{1,0:T(8,128)(2,1)S(1)} %collective-permute-done.13.refs_3_), channel_id=1, source_target_pairs={{0,32},{32,64},{64,96},{96,128},{128,160},{160,192},{192,224},{224... | collective-permute-start | bytes 1572872 | tf_op jit(solution)/shard_map/ppermute | solution.py:578
  75.4 12.1 %collective-permute-start.16 = (bf16[64,4096]{1,0:T(8,128)(2,1)S(1)}, bf16[64,4096]{1,0:T(8,128)(2,1)S(1)}, u32[]{:S(2)}, u32[]{:S(2)}) collective-permute-start(bf16[64,4096]{1,0:T(8,128)(2,1)S(1)} %collective-permute-done.14.refs_4_), channel_id=1, source_target_pairs={{0,224},{32,0},{64,32},{96,64},{128,96},{160,128},{192,160},{224,1... | collective-permute-start | bytes 1572872 | tf_op jit(solution)/shard_map/ppermute | solution.py:578
  86.8 7.7 %collective-permute-start.17 = (bf16[32,4096]{1,0:T(8,128)(2,1)S(1)}, bf16[32,4096]{1,0:T(8,128)(2,1)S(1)}, u32[]{:S(2)}, u32[]{:S(2)}) collective-permute-start(bf16[32,4096]{1,0:T(8,128)(2,1)S(1)} %slice.18), channel_id=1, source_target_pairs={{0,32},{32,64},{64,96},{96,128},{128,160},{160,192},{192,224},{224... | collective-permute-start | bytes 786440 | tf_op jit(solution)/shard_map/ppermute | solution.py:578
  87.5 7.0 %collective-permute-start.18 = (bf16[32,4096]{1,0:T(8,128)(2,1)S(1)}, bf16[32,4096]{1,0:T(8,128)(2,1)S(1)}, u32[]{:S(2)}, u32[]{:S(2)}) collective-permute-start(bf16[32,4096]{1,0:T(8,128)(2,1)S(1)} %slice.19), channel_id=1, source_target_pairs={{0,224},{32,0},{64,32},{96,64},{128,96},{160,128},{192,160},{224,1... | collective-permute-start | bytes 786440 | tf_op jit(solution)/shard_map/ppermute | solution.py:578
  108.5 29.0 %all-to-all-start.1 = ((bf16[16,16,4096]{2,1,0:T(8,128)(2,1)}), bf16[16,16,4096]{2,1,0:T(8,128)(2,1)S(1)}, u32[]{:S(2)}, u32[]{:S(2)}) async-start(bf16[16,16,4096]{2,1,0:T(8,128)(2,1)} %bitcast.15), calls=%async_computation.1 | async-start | bytes 4194304 | tf_op jit(solution)/shard_map/all_to_all | solution.py:546
  171.2 36.6 %all-to-all-start.3 = ((bf16[16,24,4096]{2,1,0:T(8,128)(2,1)}), bf16[16,24,4096]{2,1,0:T(8,128)(2,1)S(1)}, u32[]{:S(2)}, u32[]{:S(2)}) async-start(bf16[16,24,4096]{2,1,0:T(8,128)(2,1)} %bitcast.26), calls=%async_computation.3 | async-start | bytes 6291456 | tf_op jit(solution)/shard_map/all_to_all | solution.py:546
  182.8 8.6 %collective-permute-start.19 = (bf16[32,4096]{1,0:T(8,128)(2,1)S(1)}, bf16[32,4096]{1,0:T(8,128)(2,1)S(1)}, u32[]{:S(2)}, u32[]{:S(2)}) collective-permute-start(bf16[32,4096]{1,0:T(8,128)(2,1)S(1)} %get-tuple-element.58), channel_id=1, source_target_pairs={{0,32},{32,64},{64,96},{96,128},{128,160},{160,192},{192,224},{224... | collective-permute-start | bytes 786440 | tf_op jit(solution)/shard_map/ppermute | solution.py:578
  184.1 7.3 %collective-permute-start.20 = (bf16[32,4096]{1,0:T(8,128)(2,1)S(1)}, bf16[32,4096]{1,0:T(8,128)(2,1)S(1)}, u32[]{:S(2)}, u32[]{:S(2)}) collective-permute-start(bf16[32,4096]{1,0:T(8,128)(2,1)S(1)} %get-tuple-element.59), channel_id=1, source_target_pairs={{0,224},{32,0},{64,32},{96,64},{128,96},{160,128},{192,160},{224,1... | collective-permute-start | bytes 786440 | tf_op jit(solution)/shard_map/ppermute | solution.py:578
  191.5 10.5 %collective-permute-start.21 = (bf16[64,4096]{1,0:T(8,128)(2,1)S(1)}, bf16[64,4096]{1,0:T(8,128)(2,1)S(1)}, u32[]{:S(2)}, u32[]{:S(2)}) collective-permute-start(bf16[64,4096]{1,0:T(8,128)(2,1)S(1)} %get-tuple-element.60), channel_id=1, source_target_pairs={{0,32},{32,64},{64,96},{96,128},{128,160},{160,192},{192,224},{224... | collective-permute-start | bytes 1572872 | tf_op jit(solution)/shard_map/ppermute | solution.py:578
  193.2 9.6 %collective-permute-start.22 = (bf16[64,4096]{1,0:T(8,128)(2,1)S(1)}, bf16[64,4096]{1,0:T(8,128)(2,1)}, u32[]{:S(2)}, u32[]{:S(2)}) collective-permute-start(bf16[64,4096]{1,0:T(8,128)(2,1)S(1)} %get-tuple-element.61), channel_id=1, source_target_pairs={{0,224},{32,0},{64,32},{96,64},{128,96},{160,128},{192,160},{224,1... | collective-permute-start | bytes 1572872 | tf_op jit(solution)/shard_map/ppermute | solution.py:578
  211.1 13.6 %collective-permute-start.23 = (bf16[64,4096]{1,0:T(8,128)(2,1)S(1)}, bf16[64,4096]{1,0:T(8,128)(2,1)S(1)}, u32[]{:S(2)}, u32[]{:S(2)}) collective-permute-start(bf16[64,4096]{1,0:T(8,128)(2,1)S(1)} %get-tuple-element.62), channel_id=1, source_target_pairs={{0,32},{32,64},{64,96},{96,128},{128,160},{160,192},{192,224},{224... | collective-permute-start | bytes 1572872 | tf_op jit(solution)/shard_map/ppermute | solution.py:578
  212.5 12.2 %collective-permute-start.24 = (bf16[64,4096]{1,0:T(8,128)(2,1)S(1)}, bf16[64,4096]{1,0:T(8,128)(2,1)S(1)}, u32[]{:S(2)}, u32[]{:S(2)}) collective-permute-start(bf16[64,4096]{1,0:T(8,128)(2,1)S(1)} %get-tuple-element.63), channel_id=1, source_target_pairs={{0,224},{32,0},{64,32},{96,64},{128,96},{160,128},{192,160},{224,1... | collective-permute-start | bytes 1572872 | tf_op jit(solution)/shard_map/ppermute | solution.py:578
  224.9 10.5 %collective-permute-start.25 = (bf16[64,4096]{1,0:T(8,128)(2,1)S(1)}, bf16[64,4096]{1,0:T(8,128)(2,1)S(1)}, u32[]{:S(2)}, u32[]{:S(2)}) collective-permute-start(bf16[64,4096]{1,0:T(8,128)(2,1)S(1)} %get-tuple-element.64), channel_id=1, source_target_pairs={{0,32},{32,64},{64,96},{96,128},{128,160},{160,192},{192,224},{224... | collective-permute-start | bytes 1572872 | tf_op jit(solution)/shard_map/ppermute | solution.py:578
  226.6 9.2 %collective-permute-start.26 = (bf16[64,4096]{1,0:T(8,128)(2,1)S(1)}, bf16[64,4096]{1,0:T(8,128)(2,1)S(1)}, u32[]{:S(2)}, u32[]{:S(2)}) collective-permute-start(bf16[64,4096]{1,0:T(8,128)(2,1)S(1)} %get-tuple-element.65), channel_id=1, source_target_pairs={{0,224},{32,0},{64,32},{96,64},{128,96},{160,128},{192,160},{224,1... | collective-permute-start | bytes 1572872 | tf_op jit(solution)/shard_map/ppermute | solution.py:578
  (12 other events, 88.0 us)

commit v3 on v2

--- a/solution.py
+++ b/solution.py
@@ -9,9 +9,11 @@
 HOT = 4
 MOST = 5
 META = 128
-NEAR = 5
-NEAR_SLOTS = 24
-FAR_SLOTS = 16
+FIRST = [(0, 0), (0, 1), (0, 2), (0, 3), (1, 0), (1, 1), (2, 0), (2, 1)]
+MID = [(p, k) for p in (1, 2) for k in (2, 3, 4)] + [(p, k) for p in (3, 4) for k in range(MOST)]
+FAR = [(0, 4)] + [(p, k) for p in (5, 6, 7) for k in range(MOST)]
+TAKE_NEAR, TAKE_FAR = (FIRST + MID, 0, 5), (FAR, 4, 4)
+MIX_FIRST, MIX_MID, MIX_FAR = (FIRST, 0, 3), (MID, 1, 4), (FAR, 4, 4)
 MASKED = -1e30
 EPSILON = 1e-06
 F32 = jnp.float32
@@ -175,31 +177,33 @@
     return jnp.where((lax.rem(piece, 2) == 1) & (piece < 7), -far, far)
 
 
-def route_kernel(
-    rank_ref, meta_ref, take_near_ref, take_far_ref, mix_near_ref, mix_far_ref, named_ref, *, pools, top
-):
+def route_kernel(rank_ref, meta_ref, *refs, pools, top):
+    takes, mixes, named_ref = refs[:2], refs[2:5], refs[5]
     tok = meta_ref.shape[0] // pools
     rank = rank_ref[0]
-    plane = take_near_ref.shape[0] // NEAR_SLOTS
+    plane = takes[0].shape[0] // len(TAKE_NEAR[0])
     before = (
         lax.broadcasted_iota(jnp.int32, (tok, tok), 1)
         < lax.broadcasted_iota(jnp.int32, (tok, tok), 0)
     ).astype(BF16)
-    for near, per, take_ref, mix_ref in (
-        (True, NEAR_SLOTS, take_near_ref, mix_near_ref),
-        (False, FAR_SLOTS, take_far_ref, mix_far_ref),
-    ):
-        slots, rows = take_ref.shape
+
+    def fill(table, take_ref, mix_ref):
+        part, first, count = table
+        per = len(part)
+        slots = plane * per
         slot = lax.broadcasted_iota(jnp.int32, (1, slots), 1)
         inner = lax.rem(slot, per)
-        shared = (per // MOST) * MOST
         expert = (lax.div(slot, per) + rank * plane).astype(F32)
-        of_piece = jnp.where(inner < shared, lax.div(inner, MOST) + (1 if near else NEAR), 0)
-        own_place = inner - shared if near else MOST - 1
-        place = jnp.where(inner < shared, lax.rem(inner, MOST), own_place).astype(F32)
+        of_piece = jnp.zeros((1, slots), jnp.int32)
+        place = jnp.zeros((1, slots), F32)
+        for n, (p, k) in enumerate(part):
+            of_piece = jnp.where(inner == n, p, of_piece)
+            place = jnp.where(inner == n, float(k), place)
 
         def one_piece(at, carry):
-            piece = at if near else jnp.where(at == 0, 0, at + NEAR - 1)
+            piece = at + first
+            if table in (TAKE_FAR, MIX_FAR):
+                piece = jnp.where(at == 0, 0, piece)
             row = lax.rem(rank + pools + offset_of(piece), pools) * tok
             meta = meta_ref[pl.ds(pl.multiple_of(row, tok), tok), :].astype(F32)
             named = jnp.zeros((tok, slots), F32)
@@ -208,18 +212,27 @@
             for j in range(top):
                 same = meta[:, j : j + 1] == expert
                 named = jnp.where(same, 1.0, named)
-                high = jnp.where(same, meta[:, top + j : top + j + 1], high)
-                low = jnp.where(same, meta[:, 2 * top + j : 2 * top + j + 1], low)
-            count = jnp.dot(before, named.astype(BF16), preferred_element_type=F32)
-            chosen = (named > 0.5) & (count == jnp.where(of_piece == piece, place, -1.0))
+                if mix_ref is not None:
+                    high = jnp.where(same, meta[:, top + j : top + j + 1], high)
+                    low = jnp.where(same, meta[:, 2 * top + j : 2 * top + j + 1], low)
+            ahead = jnp.dot(before, named.astype(BF16), preferred_element_type=F32)
+            chosen = (named > 0.5) & (ahead == jnp.where(of_piece == piece, place, -1.0))
             here = pl.ds(pl.multiple_of(at * tok, tok), tok)
-            named_ref[here, :slots] = jnp.where(chosen, 1.0, 0.0)
-            mix_ref[0, here, :] = jnp.where(chosen, high, 0.0).astype(BF16)
-            mix_ref[1, here, :] = jnp.where(chosen, low, 0.0).astype(BF16)
+            if take_ref is not None:
+                named_ref[here, :slots] = jnp.where(chosen, 1.0, 0.0)
+            if mix_ref is not None:
+                mix_ref[0, here, :] = jnp.where(chosen, high, 0.0).astype(BF16)
+                mix_ref[1, here, :] = jnp.where(chosen, low, 0.0).astype(BF16)
             return carry
 
-        lax.fori_loop(0, rows // tok, one_piece, 0)
-        take_ref[...] = named_ref[:rows, :slots].T.astype(BF16)
+        lax.fori_loop(0, count, one_piece, 0)
+        if take_ref is not None:
+            take_ref[...] = named_ref[: count * tok, :slots].T.astype(BF16)
+
+    fill(TAKE_NEAR, takes[0], None)
+    fill(TAKE_FAR, takes[1], mixes[2])
+    fill(MIX_FIRST, None, mixes[0])
+    fill(MIX_MID, None, mixes[1])
 
 
 def by_columns(width, body):
@@ -256,14 +269,16 @@
         leave(n).wait()
 
 
-def expert_kernel(
-    x, g0, g1, u0, u1, d0, d1, out, x_ref, grow_ref, down_ref, sum_ref, hidden_ref, y_ref, x_sem, grow_sem, down_sem, out_sem
-):
+def expert_kernel(x, g0, g1, u0, u1, d0, d1, *refs):
+    outs = refs[:-10]
+    x_ref, grow_ref, down_ref, sum_ref, hidden_ref, y_ref, x_sem, grow_sem, down_sem, out_sem = (
+        refs[-10:]
+    )
     half = g0.shape[1]
     parts = x_sem.shape[0]
     deep = x.shape[1] // parts
     ends = out_sem.shape[0]
-    wide = out.shape[1] // ends
+    wide = x.shape[1] // ends
 
     def row_copy(n):
         cols = pl.ds(pl.multiple_of(n * deep, deep), deep)
@@ -291,7 +306,16 @@
 
     def leave(n):
         cols = pl.ds(pl.multiple_of(n * wide, wide), wide)
-        return pltpu.make_async_copy(y_ref.at[n], out.at[:, cols], out_sem.at[n])
+        copies, at = [], 0
+        for c, out in enumerate(outs):
+            rows = out.shape[1]
+            copies.append(
+                pltpu.make_async_copy(
+                    y_ref.at[n, :, pl.ds(at, rows), :], out.at[:, :, cols], out_sem.at[n, c]
+                )
+            )
+            at += rows
+        return copies
 
     for slab, (gate, up) in enumerate(((g0, u0), (g1, u1))):
         for n in range(parts):
@@ -327,15 +351,16 @@
     def shrink(n, carry):
         for copy in down_copies(n):
             copy.wait()
-        y_ref[n] = jnp.dot(
-            hidden_ref[...], down_ref[n], preferred_element_type=F32
-        ).astype(BF16)
-        leave(n).start()
+        y = jnp.dot(hidden_ref[...], down_ref[n], preferred_element_type=F32)
+        y_ref[n] = y.reshape(y_ref.shape[1:]).astype(BF16)
+        for copy in leave(n):
+            copy.start()
         return carry
 
     lax.fori_loop(0, ends, shrink, 0)
     for n in range(ends):
-        leave(n).wait()
+        for copy in leave(n):
+            copy.wait()
 
 
 def weighted(mix_ref, first, last, y):
@@ -379,7 +404,7 @@
     tok = right_ref.shape[0]
     copies = [
         pltpu.make_async_copy(
-            mix.at[n, pl.ds(3 * tok, 2 * tok), :], mix_ref.at[n], sem.at[n]
+            mix.at[n, pl.ds(2 * tok, 2 * tok), :], mix_ref.at[n], sem.at[n]
         )
         for n in range(2)
     ]
@@ -387,24 +412,33 @@
     copies.append(pltpu.make_async_copy(from_right, from_right_ref, sem.at[3]))
     for copy in copies:
         copy.start()
-    for copy in copies:
+    for copy in copies[:2]:
         copy.wait()
 
     def body(cols):
         mixed = weighted(mix_ref, 0, 2 * tok, y_ref[:, cols])
+
+        @pl.when(cols.start == 0)
+        def _():
+            for copy in copies[2:]:
+                copy.wait()
+
         left_ref[:, cols] = (mixed[:tok] + from_right_ref[:, cols].astype(F32)).astype(BF16)
         right_ref[:, cols] = (mixed[tok:] + from_left_ref[:, cols].astype(F32)).astype(BF16)
 
     by_columns(y_ref.shape[1], body)
 
 
-def first_kernel(mix_ref, y_ref, resid_ref, own_ref, base_ref, first_ref):
+def first_kernel(
+    near_ref, near_y_ref, mix_ref, y_ref, resid_ref, own_ref, base_ref, first_ref
+):
     tok = resid_ref.shape[0]
 
     def body(cols):
-        mixed = weighted(mix_ref, 0, 3 * tok, y_ref[:, cols])
-        base_ref[:, cols] = mixed[:tok] + own_ref[:, cols] + resid_ref[:, cols].astype(F32)
-        first_ref[:, cols] = mixed[tok:]
+        near = weighted(near_ref, 0, 3 * tok, near_y_ref[:, cols])
+        mixed = weighted(mix_ref, 0, 2 * tok, y_ref[:, cols])
+        base_ref[:, cols] = near[:tok] + own_ref[:, cols] + resid_ref[:, cols].astype(F32)
+        first_ref[:, cols] = near[tok:] + mixed
 
     by_columns(y_ref.shape[1], body)
 
@@ -505,21 +539,19 @@
         ],
     )
 
-    near_slots, far_slots = plane * NEAR_SLOTS, plane * FAR_SLOTS
-    near_rows, far_rows = NEAR * tok, (pools - NEAR + 1) * tok
-    take_near, take_far, mix_near, mix_far = held_call(
+    def size(table):
+        return plane * len(table[0]), table[2] * tok
+
+    mixing = (MIX_FIRST, MIX_MID, MIX_FAR)
+    take_near, take_far, mix_first, mix_mid, mix_far = held_call(
         lambda *refs: route_kernel(*refs, pools=pools, top=top),
         "route",
-        [
-            shape((near_slots, near_rows), BF16),
-            shape((far_slots, far_rows), BF16),
-            shape((2, near_rows, near_slots), BF16),
-            shape((2, far_rows, far_slots), BF16),
-        ],
+        [shape(size(t), BF16) for t in (TAKE_NEAR, TAKE_FAR)]
+        + [shape((2,) + size(t)[::-1], BF16) for t in mixing],
         [rank, meta],
         scalars=1,
         near=(0,),
-        scratch=[pltpu.VMEM((near_rows, near_slots), F32)],
+        scratch=[pltpu.VMEM(size(TAKE_NEAR)[::-1], F32)],
     )
 
     def pack(take, parts_in, name):
@@ -541,37 +573,35 @@
         return out
 
     def exchange(x):
-        slots = x.shape[0]
-        x = x.reshape(plane, slots // plane, model)
+        x = x.reshape(plane, -1, model)
         return lax.all_to_all(x, "xy", split_axis=0, concat_axis=0, tiled=True).reshape(
-            slots, model
+            -1, model
         )
 
-    def expert(x, name):
+    def expert(x, splits, name):
         slots = x.shape[0]
         parts, ends = 4, 4
         dma = pltpu.SemaphoreType.DMA
-        (out,) = held_call(
+        return held_call(
             expert_kernel,
             name,
-            [shape((slots, model), BF16)],
+            [shape((plane, rows, model), BF16) for rows in splits],
             [(x,)] + [(w,) for pair in zip(own, peer) for w in pair],
-            far=(0,),
+            far=range(len(splits)),
             scratch=[
                 pltpu.VMEM((slots, model), BF16),
                 pltpu.VMEM((2, model, 2 * half), BF16),
                 pltpu.VMEM((ends, 2 * half, model // ends), BF16),
                 pltpu.VMEM((2, slots, 2 * half), F32),
                 pltpu.VMEM((slots, 2 * half), BF16),
-                pltpu.VMEM((ends, slots, model // ends), BF16),
+                pltpu.VMEM((ends, plane, slots // plane, model // ends), BF16),
                 dma((parts,)),
                 dma((2, parts, 2)),
                 dma((ends, 2)),
-                dma((ends,)),
+                dma((ends, len(splits))),
             ],
             limit=48,
         )
-        return out
 
     right = [(k, (k + 1) % pools) for k in range(pools)]
     left = [(k, (k - 1) % pools) for k in range(pools)]
@@ -588,12 +618,14 @@
     got_near = exchange(sent_near)
     got_near, sent_far = tie((got_near, sent_far))
     got_far = exchange(sent_far)
-    out_near = expert(got_near, "expert_near")
-    got_far, out_near = tie((got_far, out_near))
-    out_far = expert(got_far, "expert_far")
+    out_first, out_mid = expert(got_near, (len(FIRST), len(MID)), "expert_near")
+    got_far, out_first, out_mid = tie((got_far, out_first, out_mid))
+    (out_far,) = expert(got_far, (len(FAR),), "expert_far")
     back_far = exchange(out_far)
-    out_near, back_far = tie((out_near, back_far))
-    back_near = exchange(out_near)
+    out_mid, back_far = tie((out_mid, back_far))
+    back_mid = exchange(out_mid)
+    out_first, back_mid = tie((out_first, back_mid))
+    back_first = exchange(out_first)
 
     row, pair = (tok, model), (2 * tok, model)
     own_far, third, *moving = held_call(
@@ -615,10 +647,10 @@
         second_kernel,
         "mix_second",
         [shape(row, BF16)] * 2,
-        [in_hbm(mix_near), back_near, *[in_hbm(m) for m in send(*moving)]],
+        [in_hbm(mix_mid), back_mid, *[in_hbm(m) for m in send(*moving)]],
         near=(0, 1),
         scratch=[
-            pltpu.VMEM((2, 2 * tok, near_slots), BF16),
+            pltpu.VMEM((2, 2 * tok, plane * len(MID)), BF16),
             pltpu.VMEM(row, BF16),
             pltpu.VMEM(row, BF16),
             pltpu.SemaphoreType.DMA((4,)),
@@ -630,7 +662,14 @@
         first_kernel,
         "mix_first",
         [shape(row, F32), shape(pair, F32)],
-        [Fetched((mix_near,)), back_near, Fetched((resid,)), Fetched((own_far,))],
+        [
+            Fetched((mix_first,)),
+            Fetched((back_first,)),
+            Fetched((mix_mid,)),
+            back_mid,
+            Fetched((resid,)),
+            Fetched((own_far,)),
+        ],
         near=(0, 1),
         limit=24,
     )

time: 241 us -> 241 us (level); the launches traced: 237 us -> 240 us
  waiting for transfers between devices: 88.6 us -> 79.3 us
  starting transfers between devices: 66.7 us -> 73.6 us
  Pallas kernels: 54.2 us -> 58.1 us
    all_to_all x3 -> x4, starting transfers between devices: 23.4 us -> 30.7 us  [exchange(): lax.all_to_all(x, 'xy', split_axis=0, concat_axis=0, tiled=True)]
    all_to_all x3 -> x4, waiting for transfers between devices: 20.2 us -> 14.6 us  [exchange(): lax.all_to_all(x, 'xy', split_axis=0, concat_axis=0, tiled=True)]
    ppermute x8, waiting for transfers between devices: 53.7 us -> 49.4 us  [shards(): lax.ppermute(r, 'pool', right)]
    pallas_call x13, Pallas kernels: 54.2 us -> 58.1 us  [held_call(): pl.pallas_call(kernel, in_specs=specs, out_specs=[ANY if n in far else VM...]
  transfers between devices with their start and end apart: 30 -> 31, of which waited for: 17 -> 18; matrix products, arithmetic and copies ran while one was open for 0% -> 0% of each run, Pallas kernels for 16% -> 18%
where the time goes in v3:
time: 241 us; the launch traced here: 240 us
  waiting for transfers between devices  79.3 us (33%)
  starting transfers between devices  73.6 us (31%)
  Pallas kernels  58.1 us (24%)
  blocking collectives  23.8 us (10%)
  local copies, waits for them, and re-layouts  4.65 us (2%)
    pallas_call x13, Pallas kernels, held_call(): pl.pallas_call(kernel, in_specs=specs, out_specs=[ANY if n in far else VM...  58.1 us
    ppermute x8, waiting for transfers between devices, shards(): lax.ppermute(r, 'pool', right)  49.4 us
    all_to_all x4, starting transfers between devices, exchange(): lax.all_to_all(x, 'xy', split_axis=0, concat_axis=0, tiled=True)  30.7 us
    all_to_all x1, blocking collectives, exchange(): lax.all_to_all(x, 'xy', split_axis=0, concat_axis=0, tiled=True)  23.8 us
    ppermute x8, starting transfers between devices, shards(): lax.ppermute(l, 'pool', left)  14.9 us
    all_to_all x4, waiting for transfers between devices, exchange(): lax.all_to_all(x, 'xy', split_axis=0, concat_axis=0, tiled=True)  14.6 us
    ppermute x8, starting transfers between devices, shards(): lax.ppermute(r, 'pool', right)  11.4 us
    ppermute x3, waiting for transfers between devices, ring(): from_left = lax.ppermute(from_left, 'pool', right)  11 us
  transfers between devices with their start and end apart: 31, of which 18 were waited for; matrix products, arithmetic and copies ran while one was open for 0% of the time, Pallas kernels for 18%

profile of v3, /device:TPU:12, one launch (start us, length us, event | category | flops | bytes accessed | tf_op | source)
XLA Modules:
  0.0 240.2 jit_solution(6465906488275647242)
XLA Ops:
  5.2 4.0 %collective-permute-start.1 = (bf16[64,1152]{1,0:T(8,128)(2,1)S(1)}, bf16[64,1152]{1,0:T(8,128)(2,1)S(1)}, u32[]{:S(2)}, u32[]{:S(2)}) collective-permute-start(bf16[64,1152]{1,0:T(8,128)(2,1)S(1)} %gather_block.1.refs_5_), channel_id=1, source_target_pairs={{0,224},{32,0},{64,32},{96,64},{128,96},{160,128},{192,160},{224,1... | collective-permute-start | bytes 442376 | tf_op jit(solution)/shard_map/ppermute | solution.py:464
  9.2 4.3 %collective-permute-done.refs_6_ = bf16[64,1152]{1,0:T(8,128)(2,1)S(1)} collective-permute-done((bf16[64,1152]{1,0:T(8,128)(2,1)S(1)}, bf16[64,1152]{1,0:T(8,128)(2,1)S(1)}, u32[]{:S(2)}, u32[]{:S(2)}) %collective-permute-start) | collective-permute-done | bytes 147488 | tf_op jit(solution)/shard_map/ppermute | solution.py:463
  16.8 3.6 %collective-permute-done.2.refs_8_ = bf16[64,1152]{1,0:T(8,128)(2,1)S(1)} collective-permute-done((bf16[64,1152]{1,0:T(8,128)(2,1)S(1)}, bf16[64,1152]{1,0:T(8,128)(2,1)S(1)}, u32[]{:S(2)}, u32[]{:S(2)}) %collective-permute-start.2) | collective-permute-done | bytes 147488 | tf_op jit(solution)/shard_map/ppermute | solution.py:463
  26.7 3.3 %collective-permute-start.7 = (bf16[32,1152]{1,0:T(8,128)(2,1)S(1)}, bf16[32,1152]{1,0:T(8,128)(2,1)S(1)}, u32[]{:S(2)}, u32[]{:S(2)}) collective-permute-start(bf16[32,1152]{1,0:T(8,128)(2,1)S(1)} %slice.17), channel_id=1, source_target_pairs={{0,224},{32,0},{64,32},{96,64},{128,96},{160,128},{192,160},{224,1... | collective-permute-start | bytes 221192 | tf_op jit(solution)/shard_map/ppermute | solution.py:469
  32.3 6.8 %attend.1 = (bf16[64,4096]{1,0:T(8,128)(2,1)}, bf16[64,4096]{1,0:T(8,128)(2,1)}, bf16[64,4096]{1,0:T(8,128)(2,1)S(1)}, bf16[512,128]{1,0:T(8,128)(2,1)S(1)}) custom-call(s32[1]{0:T(128)} %bitcast.rank_ref.refs_0_, s32[1,16]{1,0:T(1,128)} %refs_1_.1, f32[1,4096]{1,0:T(1,128)} %bitcast.41, bf16[64,4096]{1,0:T(8,128)(2,1)} %bitcast.38, ...), custom_call_target="tpu_custom_call" | custom-call | tf_op jit(solution)/shard_map/attend/pallas_call | solution.py:46
  39.1 3.3 %collective-permute-start.9 = (bf16[64,4096]{1,0:T(8,128)(2,1)S(1)}, bf16[64,4096]{1,0:T(8,128)(2,1)S(1)}, u32[]{:S(2)}, u32[]{:S(2)}) collective-permute-start(bf16[64,4096]{1,0:T(8,128)(2,1)S(1)} %get-tuple-element.43.refs_0_), channel_id=1, source_target_pairs={{0,224},{32,0},{64,32},{96,64},{128,96},{160,128},{192,160},{224,1... | collective-permute-start | bytes 1572872 | tf_op jit(solution)/shard_map/ppermute | solution.py:608
  42.4 6.0 %route.1 = (bf16[384,320]{1,0:T(8,128)(2,1)S(1)}, bf16[256,256]{1,0:T(8,128)(2,1)}, bf16[2,192,128]{2,1,0:T(8,128)(2,1)}, bf16[2,256,256]{2,1,0:T(8,128)(2,1)}, bf16[2,256,256]{2,1,0:T(8,128)(2,1)}) custom-call(s32[1]{0:T(128)} %bitcast.rank_ref.refs_0_, bf16[512,128]{1,0:T(8,128)(2,1)S(1)} %get-tuple-element.41.refs_1_), custom_call_target="tpu_custom_call" | custom-call | tf_op jit(solution)/shard_map/route/pallas_call | solution.py:46
  54.5 7.6 %collective-permute-done.13.refs_3_ = bf16[64,4096]{1,0:T(8,128)(2,1)S(1)} collective-permute-done((bf16[64,4096]{1,0:T(8,128)(2,1)S(1)}, bf16[64,4096]{1,0:T(8,128)(2,1)S(1)}, u32[]{:S(2)}, u32[]{:S(2)}) %collective-permute-start.13) | collective-permute-done | bytes 524320 | tf_op jit(solution)/shard_map/ppermute | solution.py:608
  66.3 7.3 %all-to-all-start = ((bf16[16,24,4096]{2,1,0:T(8,128)(2,1)}), bf16[16,24,4096]{2,1,0:T(8,128)(2,1)}, u32[]{:S(2)}, u32[]{:S(2)}) async-start(bf16[16,24,4096]{2,1,0:T(8,128)(2,1)} %bitcast.13), calls=%async_computation | async-start | bytes 6291456 | tf_op jit(solution)/shard_map/all_to_all | solution.py:577
  76.9 10.0 %collective-permute-done.15.refs_1_ = bf16[64,4096]{1,0:T(8,128)(2,1)S(1)} collective-permute-done((bf16[64,4096]{1,0:T(8,128)(2,1)S(1)}, bf16[64,4096]{1,0:T(8,128)(2,1)S(1)}, u32[]{:S(2)}, u32[]{:S(2)}) %collective-permute-start.15) | collective-permute-done | bytes 524320 | tf_op jit(solution)/shard_map/ppermute | solution.py:608
  90.3 4.2 %collective-permute-done.17.refs_3_ = bf16[32,4096]{1,0:T(8,128)(2,1)S(1)} collective-permute-done((bf16[32,4096]{1,0:T(8,128)(2,1)S(1)}, bf16[32,4096]{1,0:T(8,128)(2,1)S(1)}, u32[]{:S(2)}, u32[]{:S(2)}) %collective-permute-start.17) | collective-permute-done | bytes 262176 | tf_op jit(solution)/shard_map/ppermute | solution.py:608
  96.6 11.9 %all-to-all-done = bf16[16,24,4096]{2,1,0:T(8,128)(2,1)} async-done(((bf16[16,24,4096]{2,1,0:T(8,128)(2,1)}), bf16[16,24,4096]{2,1,0:T(8,128)(2,1)}, u32[]{:S(2)}, u32[]{:S(2)}) %all-to-all-start) | async-done | bytes 3145760 | tf_op jit(solution)/shard_map/all_to_all | solution.py:577
  108.5 9.0 %all-to-all-start.1 = ((bf16[16,16,4096]{2,1,0:T(8,128)(2,1)}), bf16[16,16,4096]{2,1,0:T(8,128)(2,1)S(1)}, u32[]{:S(2)}, u32[]{:S(2)}) async-start(bf16[16,16,4096]{2,1,0:T(8,128)(2,1)} %bitcast.15), calls=%async_computation.1 | async-start | bytes 4194304 | tf_op jit(solution)/shard_map/all_to_all | solution.py:577
  117.6 15.1 %expert_near.1 = (bf16[16,8,4096]{2,1,0:T(8,128)(2,1)S(1)}, bf16[16,16,4096]{2,1,0:T(8,128)(2,1)S(1)}) custom-call(bf16[384,4096]{1,0:T(8,128)(2,1)} %bitcast.14.x, bf16[4096,384]{1,0:T(8,128)(2,1)} %bitcast.28, bf16[4096,384]{1,0:T(8,128)(2,1)} %collective-permute-done.10.g1, bf16[4096,384]{1,0:T(8,128)(2,1)} %bitcast.31, ...), custom_call_target="tpu_custom_call" | custom-call | tf_op jit(solution)/shard_map/expert_near/pallas_call | solution.py:46
  137.7 9.8 %expert_far.1 = bf16[16,16,4096]{2,1,0:T(8,128)(2,1)S(1)} custom-call(bf16[256,4096]{1,0:T(8,128)(2,1)S(1)} %bitcast.25, bf16[4096,384]{1,0:T(8,128)(2,1)} %bitcast.29, bf16[4096,384]{1,0:T(8,128)(2,1)} %collective-permute-done.10.g1, bf16[4096,384]{1,0:T(8,128)(2,1)} %bitcast.32, bf16[4096,384]{1,0:T(8,128)(2,1)} %collective-permute-done.11.u1, ...), custom_call_target="tpu_custom_call" | custom-call | tf_op jit(solution)/shard_map/expert_far/pallas_call | solution.py:46
  147.5 23.8 %all_to_all.25 = bf16[16,16,4096]{2,1,0:T(8,128)(2,1)} all-to-all(bf16[16,16,4096]{2,1,0:T(8,128)(2,1)S(1)} %expert_far.1), channel_id=1, replica_groups=mesh['pool'=8,'xy'=16,'core'=2] {'xy'}, dimensions={0} | all-to-all | bytes 4194304 | tf_op jit(solution)/shard_map/all_to_all | solution.py:577
  171.4 7.1 %all-to-all-start.3 = ((bf16[16,16,4096]{2,1,0:T(8,128)(2,1)}), bf16[16,16,4096]{2,1,0:T(8,128)(2,1)S(1)}, u32[]{:S(2)}, u32[]{:S(2)}) async-start(bf16[16,16,4096]{2,1,0:T(8,128)(2,1)} %copy-done), calls=%async_computation.3 | async-start | bytes 4194304 | tf_op jit(solution)/shard_map/all_to_all | solution.py:577
  178.5 4.4 %mix_far.1 = (f32[64,4096]{1,0:T(8,128)}, f32[128,4096]{1,0:T(8,128)S(1)}, bf16[32,4096]{1,0:T(8,128)(2,1)S(1)}, bf16[32,4096]{1,0:T(8,128)(2,1)S(1)}) custom-call(bf16[2,256,256]{2,1,0:T(8,128)(2,1)} %get-tuple-element.64.mix_ref, bf16[256,4096]{1,0:T(8,128)(2,1)} %bitcast.36), custom_call_target="tpu_custom_call" | custom-call | tf_op jit(solution)/shard_map/mix_far/pallas_call | solution.py:46
  186.1 6.5 %collective-permute-done.19.from_left_ref = bf16[32,4096]{1,0:T(8,128)(2,1)S(1)} collective-permute-done((bf16[32,4096]{1,0:T(8,128)(2,1)S(1)}, bf16[32,4096]{1,0:T(8,128)(2,1)S(1)}, u32[]{:S(2)}, u32[]{:S(2)}) %collective-permute-start.19) | collective-permute-done | bytes 262176 | tf_op jit(solution)/shard_map/ppermute | solution.py:608
  197.0 7.2 %all-to-all-start.4 = ((bf16[16,8,4096]{2,1,0:T(8,128)(2,1)}), bf16[16,8,4096]{2,1,0:T(8,128)(2,1)S(1)}, u32[]{:S(2)}, u32[]{:S(2)}) async-start(bf16[16,8,4096]{2,1,0:T(8,128)(2,1)} %copy-done.2), calls=%async_computation.4 | async-start | bytes 2097152 | tf_op jit(solution)/shard_map/all_to_all | solution.py:577
  204.2 3.3 %collective-permute-done.21.from_left = bf16[64,4096]{1,0:T(8,128)(2,1)} collective-permute-done((bf16[64,4096]{1,0:T(8,128)(2,1)}, bf16[64,4096]{1,0:T(8,128)(2,1)}, u32[]{:S(2)}, u32[]{:S(2)}) %collective-permute-start.21) | collective-permute-done | bytes 524320 | tf_op jit(solution)/shard_map/ppermute | solution.py:608
  208.2 3.4 %mix_second.1 = (bf16[64,4096]{1,0:T(8,128)(2,1)}, bf16[64,4096]{1,0:T(8,128)(2,1)}) custom-call(bf16[2,256,256]{2,1,0:T(8,128)(2,1)} %get-tuple-element.61.mix_ref.mix, bf16[256,4096]{1,0:T(8,128)(2,1)S(1)} %bitcast.23, bf16[64,4096]{1,0:T(8,128)(2,1)} %collective-permute-done.21.from_left, bf16[64,4096]{1,0:T(8,128)(2,1)} %collective-permute-done.22.from_right), custom_call_target="tpu_custom_call" | custom-call | tf_op jit(solution)/shard_map/mix_second/pallas_call | solution.py:46
  219.1 7.8 %collective-permute-done.23.from_left_ref = bf16[64,4096]{1,0:T(8,128)(2,1)} collective-permute-done((bf16[64,4096]{1,0:T(8,128)(2,1)}, bf16[64,4096]{1,0:T(8,128)(2,1)}, u32[]{:S(2)}, u32[]{:S(2)}) %collective-permute-start.23) | collective-permute-done | bytes 524320 | tf_op jit(solution)/shard_map/ppermute | solution.py:608
  231.8 7.2 %collective-permute-done.25.from_left_ref = bf16[64,4096]{1,0:T(8,128)(2,1)S(1)} collective-permute-done((bf16[64,4096]{1,0:T(8,128)(2,1)S(1)}, bf16[64,4096]{1,0:T(8,128)(2,1)S(1)}, u32[]{:S(2)}, u32[]{:S(2)}) %collective-permute-start.25) | collective-permute-done | bytes 524320 | tf_op jit(solution)/shard_map/ppermute | solution.py:608
  (70 shorter events, 62.3 us)
Async XLA Ops:
  0.6 50.5 %collective-permute-start.10 = (bf16[4096,384]{1,0:T(8,128)(2,1)}, bf16[4096,384]{1,0:T(8,128)(2,1)}, u32[]{:S(2)}, u32[]{:S(2)}) collective-permute-start(bf16[4096,384]{1,0:T(8,128)(2,1)} %bitcast.27), channel_id=1, source_target_pairs={{0,1},{1,0},{2,3},{3,2},{4,5},{5,4},{6,7},{7,6},{8,9},{9,8},{10,11... | collective-permute-start | bytes 9437192 | tf_op jit(solution)/shard_map/ppermute | solution.py:499
  0.7 50.4 %collective-permute-start.11 = (bf16[4096,384]{1,0:T(8,128)(2,1)}, bf16[4096,384]{1,0:T(8,128)(2,1)}, u32[]{:S(2)}, u32[]{:S(2)}) collective-permute-start(bf16[4096,384]{1,0:T(8,128)(2,1)} %bitcast.30), channel_id=1, source_target_pairs={{0,1},{1,0},{2,3},{3,2},{4,5},{5,4},{6,7},{7,6},{8,9},{9,8},{10,11... | collective-permute-start | bytes 9437192 | tf_op jit(solution)/shard_map/ppermute | solution.py:499
  1.2 50.0 %collective-permute-start.12 = (bf16[384,4096]{1,0:T(8,128)(2,1)}, bf16[384,4096]{1,0:T(8,128)(2,1)}, u32[]{:S(2)}, u32[]{:S(2)}) collective-permute-start(bf16[384,4096]{1,0:T(8,128)(2,1)} %bitcast.33), channel_id=1, source_target_pairs={{0,1},{1,0},{2,3},{3,2},{4,5},{5,4},{6,7},{7,6},{8,9},{9,8},{10,11... | collective-permute-start | bytes 9437192 | tf_op jit(solution)/shard_map/ppermute | solution.py:499
  3.1 10.4 %collective-permute-start = (bf16[64,1152]{1,0:T(8,128)(2,1)S(1)}, bf16[64,1152]{1,0:T(8,128)(2,1)S(1)}, u32[]{:S(2)}, u32[]{:S(2)}) collective-permute-start(bf16[64,1152]{1,0:T(8,128)(2,1)S(1)} %gather_block.1.refs_5_), channel_id=1, source_target_pairs={{0,32},{32,64},{64,96},{96,128},{128,160},{160,192},{192,224},{224... | collective-permute-start | bytes 442376 | tf_op jit(solution)/shard_map/ppermute | solution.py:463
  5.2 8.4 %collective-permute-start.1 = (bf16[64,1152]{1,0:T(8,128)(2,1)S(1)}, bf16[64,1152]{1,0:T(8,128)(2,1)S(1)}, u32[]{:S(2)}, u32[]{:S(2)}) collective-permute-start(bf16[64,1152]{1,0:T(8,128)(2,1)S(1)} %gather_block.1.refs_5_), channel_id=1, source_target_pairs={{0,224},{32,0},{64,32},{96,64},{128,96},{160,128},{192,160},{224,1... | collective-permute-start | bytes 442376 | tf_op jit(solution)/shard_map/ppermute | solution.py:464
  39.1 12.1 %collective-permute-start.8 = (bf16[64,4096]{1,0:T(8,128)(2,1)S(1)}, bf16[64,4096]{1,0:T(8,128)(2,1)S(1)}, u32[]{:S(2)}, u32[]{:S(2)}) collective-permute-start(bf16[64,4096]{1,0:T(8,128)(2,1)S(1)} %get-tuple-element.43.refs_0_), channel_id=1, source_target_pairs={{0,32},{32,64},{64,96},{96,128},{128,160},{160,192},{192,224},{224... | collective-permute-start | bytes 1572872 | tf_op jit(solution)/shard_map/ppermute | solution.py:608
  39.1 12.1 %collective-permute-start.9 = (bf16[64,4096]{1,0:T(8,128)(2,1)S(1)}, bf16[64,4096]{1,0:T(8,128)(2,1)S(1)}, u32[]{:S(2)}, u32[]{:S(2)}) collective-permute-start(bf16[64,4096]{1,0:T(8,128)(2,1)S(1)} %get-tuple-element.43.refs_0_), channel_id=1, source_target_pairs={{0,224},{32,0},{64,32},{96,64},{128,96},{160,128},{192,160},{224,1... | collective-permute-start | bytes 1572872 | tf_op jit(solution)/shard_map/ppermute | solution.py:608
  51.2 10.9 %collective-permute-start.13 = (bf16[64,4096]{1,0:T(8,128)(2,1)S(1)}, bf16[64,4096]{1,0:T(8,128)(2,1)S(1)}, u32[]{:S(2)}, u32[]{:S(2)}) collective-permute-start(bf16[64,4096]{1,0:T(8,128)(2,1)S(1)} %collective-permute-done.8.refs_1_), channel_id=1, source_target_pairs={{0,32},{32,64},{64,96},{96,128},{128,160},{160,192},{192,224},{224... | collective-permute-start | bytes 1572872 | tf_op jit(solution)/shard_map/ppermute | solution.py:608
  53.8 9.2 %collective-permute-start.14 = (bf16[64,4096]{1,0:T(8,128)(2,1)S(1)}, bf16[64,4096]{1,0:T(8,128)(2,1)S(1)}, u32[]{:S(2)}, u32[]{:S(2)}) collective-permute-start(bf16[64,4096]{1,0:T(8,128)(2,1)S(1)} %collective-permute-done.9.refs_2_), channel_id=1, source_target_pairs={{0,224},{32,0},{64,32},{96,64},{128,96},{160,128},{192,160},{224,1... | collective-permute-start | bytes 1572872 | tf_op jit(solution)/shard_map/ppermute | solution.py:608
  66.3 42.2 %all-to-all-start = ((bf16[16,24,4096]{2,1,0:T(8,128)(2,1)}), bf16[16,24,4096]{2,1,0:T(8,128)(2,1)}, u32[]{:S(2)}, u32[]{:S(2)}) async-start(bf16[16,24,4096]{2,1,0:T(8,128)(2,1)} %bitcast.13), calls=%async_computation | async-start | bytes 6291456 | tf_op jit(solution)/shard_map/all_to_all | solution.py:577
  73.6 13.2 %collective-permute-start.15 = (bf16[64,4096]{1,0:T(8,128)(2,1)S(1)}, bf16[64,4096]{1,0:T(8,128)(2,1)S(1)}, u32[]{:S(2)}, u32[]{:S(2)}) collective-permute-start(bf16[64,4096]{1,0:T(8,128)(2,1)S(1)} %collective-permute-done.13.refs_3_), channel_id=1, source_target_pairs={{0,32},{32,64},{64,96},{96,128},{128,160},{160,192},{192,224},{224... | collective-permute-start | bytes 1572872 | tf_op jit(solution)/shard_map/ppermute | solution.py:608
  75.4 12.1 %collective-permute-start.16 = (bf16[64,4096]{1,0:T(8,128)(2,1)S(1)}, bf16[64,4096]{1,0:T(8,128)(2,1)S(1)}, u32[]{:S(2)}, u32[]{:S(2)}) collective-permute-start(bf16[64,4096]{1,0:T(8,128)(2,1)S(1)} %collective-permute-done.14.refs_4_), channel_id=1, source_target_pairs={{0,224},{32,0},{64,32},{96,64},{128,96},{160,128},{192,160},{224,1... | collective-permute-start | bytes 1572872 | tf_op jit(solution)/shard_map/ppermute | solution.py:608
  86.8 7.7 %collective-permute-start.17 = (bf16[32,4096]{1,0:T(8,128)(2,1)S(1)}, bf16[32,4096]{1,0:T(8,128)(2,1)S(1)}, u32[]{:S(2)}, u32[]{:S(2)}) collective-permute-start(bf16[32,4096]{1,0:T(8,128)(2,1)S(1)} %slice.18), channel_id=1, source_target_pairs={{0,32},{32,64},{64,96},{96,128},{128,160},{160,192},{192,224},{224... | collective-permute-start | bytes 786440 | tf_op jit(solution)/shard_map/ppermute | solution.py:608
  108.5 29.2 %all-to-all-start.1 = ((bf16[16,16,4096]{2,1,0:T(8,128)(2,1)}), bf16[16,16,4096]{2,1,0:T(8,128)(2,1)S(1)}, u32[]{:S(2)}, u32[]{:S(2)}) async-start(bf16[16,16,4096]{2,1,0:T(8,128)(2,1)} %bitcast.15), calls=%async_computation.1 | async-start | bytes 4194304 | tf_op jit(solution)/shard_map/all_to_all | solution.py:577
  171.4 25.6 %all-to-all-start.3 = ((bf16[16,16,4096]{2,1,0:T(8,128)(2,1)}), bf16[16,16,4096]{2,1,0:T(8,128)(2,1)S(1)}, u32[]{:S(2)}, u32[]{:S(2)}) async-start(bf16[16,16,4096]{2,1,0:T(8,128)(2,1)} %copy-done), calls=%async_computation.3 | async-start | bytes 4194304 | tf_op jit(solution)/shard_map/all_to_all | solution.py:577
  182.8 9.7 %collective-permute-start.19 = (bf16[32,4096]{1,0:T(8,128)(2,1)S(1)}, bf16[32,4096]{1,0:T(8,128)(2,1)S(1)}, u32[]{:S(2)}, u32[]{:S(2)}) collective-permute-start(bf16[32,4096]{1,0:T(8,128)(2,1)S(1)} %get-tuple-element.70), channel_id=1, source_target_pairs={{0,32},{32,64},{64,96},{96,128},{128,160},{160,192},{192,224},{224... | collective-permute-start | bytes 786440 | tf_op jit(solution)/shard_map/ppermute | solution.py:608
  184.0 8.6 %collective-permute-start.20 = (bf16[32,4096]{1,0:T(8,128)(2,1)S(1)}, bf16[32,4096]{1,0:T(8,128)(2,1)S(1)}, u32[]{:S(2)}, u32[]{:S(2)}) collective-permute-start(bf16[32,4096]{1,0:T(8,128)(2,1)S(1)} %get-tuple-element.71), channel_id=1, source_target_pairs={{0,224},{32,0},{64,32},{96,64},{128,96},{160,128},{192,160},{224,1... | collective-permute-start | bytes 786440 | tf_op jit(solution)/shard_map/ppermute | solution.py:608
  193.7 13.8 %collective-permute-start.21 = (bf16[64,4096]{1,0:T(8,128)(2,1)}, bf16[64,4096]{1,0:T(8,128)(2,1)}, u32[]{:S(2)}, u32[]{:S(2)}) collective-permute-start(bf16[64,4096]{1,0:T(8,128)(2,1)} %get-tuple-element.72), channel_id=1, source_target_pairs={{0,32},{32,64},{64,96},{96,128},{128,160},{160,192},{192,224},{224... | collective-permute-start | bytes 1572872 | tf_op jit(solution)/shard_map/ppermute | solution.py:608
  195.1 13.1 %collective-permute-start.22 = (bf16[64,4096]{1,0:T(8,128)(2,1)}, bf16[64,4096]{1,0:T(8,128)(2,1)}, u32[]{:S(2)}, u32[]{:S(2)}) collective-permute-start(bf16[64,4096]{1,0:T(8,128)(2,1)} %get-tuple-element.73), channel_id=1, source_target_pairs={{0,224},{32,0},{64,32},{96,64},{128,96},{160,128},{192,160},{224,1... | collective-permute-start | bytes 1572872 | tf_op jit(solution)/shard_map/ppermute | solution.py:608
  197.0 17.9 %all-to-all-start.4 = ((bf16[16,8,4096]{2,1,0:T(8,128)(2,1)}), bf16[16,8,4096]{2,1,0:T(8,128)(2,1)S(1)}, u32[]{:S(2)}, u32[]{:S(2)}) async-start(bf16[16,8,4096]{2,1,0:T(8,128)(2,1)} %copy-done.2), calls=%async_computation.4 | async-start | bytes 2097152 | tf_op jit(solution)/shard_map/all_to_all | solution.py:577
  211.6 15.4 %collective-permute-start.23 = (bf16[64,4096]{1,0:T(8,128)(2,1)}, bf16[64,4096]{1,0:T(8,128)(2,1)}, u32[]{:S(2)}, u32[]{:S(2)}) collective-permute-start(bf16[64,4096]{1,0:T(8,128)(2,1)} %get-tuple-element.74), channel_id=1, source_target_pairs={{0,32},{32,64},{64,96},{96,128},{128,160},{160,192},{192,224},{224... | collective-permute-start | bytes 1572872 | tf_op jit(solution)/shard_map/ppermute | solution.py:608
  213.8 13.3 %collective-permute-start.24 = (bf16[64,4096]{1,0:T(8,128)(2,1)}, bf16[64,4096]{1,0:T(8,128)(2,1)}, u32[]{:S(2)}, u32[]{:S(2)}) collective-permute-start(bf16[64,4096]{1,0:T(8,128)(2,1)} %get-tuple-element.75), channel_id=1, source_target_pairs={{0,224},{32,0},{64,32},{96,64},{128,96},{160,128},{192,160},{224,1... | collective-permute-start | bytes 1572872 | tf_op jit(solution)/shard_map/ppermute | solution.py:608
  228.5 10.5 %collective-permute-start.25 = (bf16[64,4096]{1,0:T(8,128)(2,1)S(1)}, bf16[64,4096]{1,0:T(8,128)(2,1)S(1)}, u32[]{:S(2)}, u32[]{:S(2)}) collective-permute-start(bf16[64,4096]{1,0:T(8,128)(2,1)S(1)} %get-tuple-element.76), channel_id=1, source_target_pairs={{0,32},{32,64},{64,96},{96,128},{128,160},{160,192},{192,224},{224... | collective-permute-start | bytes 1572872 | tf_op jit(solution)/shard_map/ppermute | solution.py:608
  230.1 9.2 %collective-permute-start.26 = (bf16[64,4096]{1,0:T(8,128)(2,1)S(1)}, bf16[64,4096]{1,0:T(8,128)(2,1)S(1)}, u32[]{:S(2)}, u32[]{:S(2)}) collective-permute-start(bf16[64,4096]{1,0:T(8,128)(2,1)S(1)} %get-tuple-element.77), channel_id=1, source_target_pairs={{0,224},{32,0},{64,32},{96,64},{128,96},{160,128},{192,160},{224,1... | collective-permute-start | bytes 1572872 | tf_op jit(solution)/shard_map/ppermute | solution.py:608
  (14 other events, 119.6 us)

commit v4 on v3

--- a/solution.py
+++ b/solution.py
@@ -15,6 +15,7 @@
 TAKE_NEAR, TAKE_FAR = (FIRST + MID, 0, 5), (FAR, 4, 4)
 MIX_FIRST, MIX_MID, MIX_FAR = (FIRST, 0, 3), (MID, 1, 4), (FAR, 4, 4)
 MASKED = -1e30
+LOG2E = 1.4426950408889634
 EPSILON = 1e-06
 F32 = jnp.float32
 BF16 = jnp.bfloat16
@@ -135,22 +136,31 @@
     stack = rows // tok
     col = lax.broadcasted_iota(jnp.int32, (rows, keys), 1)
     position = lax.rem(lax.broadcasted_iota(jnp.int32, (rows, keys), 0), tok) + rank * tok
-    bias_ref[...] = jnp.where(col - prefix <= position, 0.0, MASKED)
+    bias_ref[...] = jnp.where(col <= position, 0.0, MASKED)
 
     def some_heads(n, squares):
         lane = lambda at: pl.ds(pl.multiple_of(at * HD, HD), HD)
         first = n * stack
         g = lax.div(first, group)
         query = jnp.concatenate([query_ref[:, lane(first + h)] for h in range(stack)], axis=0)
-        scores = lax.dot_general(
-            query, kv_ref[:, lane(g)], (((1,), (1,)), ((), ())), preferred_element_type=F32
+        held_keys, new_keys = kv_ref[:prefix, lane(g)], kv_ref[prefix:, lane(g)]
+        across = (((1,), (1,)), ((), ()))
+        held_scores = lax.dot_general(query, held_keys, across, preferred_element_type=F32)
+        new_scores = lax.dot_general(query, new_keys, across, preferred_element_type=F32)
+        new_scores = new_scores + bias_ref[...]
+        peak = jnp.maximum(
+            jnp.max(held_scores, axis=-1, keepdims=True),
+            jnp.max(new_scores, axis=-1, keepdims=True),
         )
-        scores = scores * HD ** (-0.5) + bias_ref[...]
-        weights = jnp.exp(scores - jnp.max(scores, axis=-1, keepdims=True))
-        row_sum = jnp.sum(weights, axis=-1, keepdims=True)
+        held_weights = jnp.exp2((held_scores - peak) * (HD ** (-0.5) * LOG2E))
+        new_weights = jnp.exp2((new_scores - peak) * (HD ** (-0.5) * LOG2E))
+        row_sum = jnp.sum(held_weights, axis=-1, keepdims=True) + jnp.sum(
+            new_weights, axis=-1, keepdims=True
+        )
+        at = lane(heads_kv + g)
         mixed = jnp.dot(
-            weights.astype(BF16), kv_ref[:, lane(heads_kv + g)], preferred_element_type=F32
-        )
+            held_weights.astype(BF16), kv_ref[:prefix, at], preferred_element_type=F32
+        ) + jnp.dot(new_weights.astype(BF16), kv_ref[prefix:, at], preferred_element_type=F32)
         mixed = (mixed / row_sum).astype(BF16)
         for h in range(stack):
             part = mixed[h * tok : (h + 1) * tok]
@@ -535,7 +545,7 @@
         scratch=[
             pltpu.VMEM((pools * tok, 2 * width + META), BF16),
             pltpu.VMEM((keys, width), BF16),
-            pltpu.VMEM((stack * tok, keys), F32),
+            pltpu.VMEM((stack * tok, pools * tok), F32),
         ],
     )
 

time: 241 us -> 241 us (level)
  no operation moved by 1% of the time
where the time goes in v4:
time: 241 us; the launch traced here: 240 us
  waiting for transfers between devices  79.1 us (33%)
  starting transfers between devices  73.7 us (31%)
  Pallas kernels  57.9 us (24%)
  blocking collectives  23.9 us (10%)
  local copies, waits for them, and re-layouts  4.65 us (2%)
    pallas_call x13, Pallas kernels, held_call(): pl.pallas_call(kernel, in_specs=specs, out_specs=[ANY if n in far else VM...  57.9 us
    ppermute x8, waiting for transfers between devices, shards(): lax.ppermute(r, 'pool', right)  49.9 us
    all_to_all x4, starting transfers between devices, exchange(): lax.all_to_all(x, 'xy', split_axis=0, concat_axis=0, tiled=True)  30.9 us
    all_to_all x1, blocking collectives, exchange(): lax.all_to_all(x, 'xy', split_axis=0, concat_axis=0, tiled=True)  23.9 us
    ppermute x8, starting transfers between devices, shards(): lax.ppermute(l, 'pool', left)  14.1 us
    all_to_all x4, waiting for transfers between devices, exchange(): lax.all_to_all(x, 'xy', split_axis=0, concat_axis=0, tiled=True)  14 us
    ppermute x8, starting transfers between devices, shards(): lax.ppermute(r, 'pool', right)  12.2 us
    ppermute x3, waiting for transfers between devices, ring(): from_left = lax.ppermute(from_left, 'pool', right)  11 us
  transfers between devices with their start and end apart: 31, of which 18 were waited for; matrix products, arithmetic and copies ran while one was open for 0% of the time, Pallas kernels for 18%

profile of v4, /device:TPU:12, one launch (start us, length us, event | category | flops | bytes accessed | tf_op | source)
XLA Modules:
  0.0 240.1 jit_solution(4558409046043622094)
XLA Ops:
  5.2 4.0 %collective-permute-start.1 = (bf16[64,1152]{1,0:T(8,128)(2,1)S(1)}, bf16[64,1152]{1,0:T(8,128)(2,1)S(1)}, u32[]{:S(2)}, u32[]{:S(2)}) collective-permute-start(bf16[64,1152]{1,0:T(8,128)(2,1)S(1)} %gather_block.1.refs_5_), channel_id=1, source_target_pairs={{0,224},{32,0},{64,32},{96,64},{128,96},{160,128},{192,160},{224,1... | collective-permute-start | bytes 442376 | tf_op jit(solution)/shard_map/ppermute | solution.py:474
  9.2 4.3 %collective-permute-done.refs_6_ = bf16[64,1152]{1,0:T(8,128)(2,1)S(1)} collective-permute-done((bf16[64,1152]{1,0:T(8,128)(2,1)S(1)}, bf16[64,1152]{1,0:T(8,128)(2,1)S(1)}, u32[]{:S(2)}, u32[]{:S(2)}) %collective-permute-start) | collective-permute-done | bytes 147488 | tf_op jit(solution)/shard_map/ppermute | solution.py:473
  16.8 3.6 %collective-permute-done.2.refs_8_ = bf16[64,1152]{1,0:T(8,128)(2,1)S(1)} collective-permute-done((bf16[64,1152]{1,0:T(8,128)(2,1)S(1)}, bf16[64,1152]{1,0:T(8,128)(2,1)S(1)}, u32[]{:S(2)}, u32[]{:S(2)}) %collective-permute-start.2) | collective-permute-done | bytes 147488 | tf_op jit(solution)/shard_map/ppermute | solution.py:473
  26.7 3.3 %collective-permute-start.7 = (bf16[32,1152]{1,0:T(8,128)(2,1)S(1)}, bf16[32,1152]{1,0:T(8,128)(2,1)S(1)}, u32[]{:S(2)}, u32[]{:S(2)}) collective-permute-start(bf16[32,1152]{1,0:T(8,128)(2,1)S(1)} %slice.17), channel_id=1, source_target_pairs={{0,224},{32,0},{64,32},{96,64},{128,96},{160,128},{192,160},{224,1... | collective-permute-start | bytes 221192 | tf_op jit(solution)/shard_map/ppermute | solution.py:479
  32.3 6.6 %attend.1 = (bf16[64,4096]{1,0:T(8,128)(2,1)}, bf16[64,4096]{1,0:T(8,128)(2,1)}, bf16[64,4096]{1,0:T(8,128)(2,1)S(1)}, bf16[512,128]{1,0:T(8,128)(2,1)S(1)}) custom-call(s32[1]{0:T(128)} %bitcast.rank_ref.refs_0_, s32[1,16]{1,0:T(1,128)} %refs_1_.1, f32[1,4096]{1,0:T(1,128)} %bitcast.41, bf16[64,4096]{1,0:T(8,128)(2,1)} %bitcast.38, ...), custom_call_target="tpu_custom_call" | custom-call | tf_op jit(solution)/shard_map/attend/pallas_call | solution.py:47
  38.8 3.3 %collective-permute-start.9 = (bf16[64,4096]{1,0:T(8,128)(2,1)S(1)}, bf16[64,4096]{1,0:T(8,128)(2,1)S(1)}, u32[]{:S(2)}, u32[]{:S(2)}) collective-permute-start(bf16[64,4096]{1,0:T(8,128)(2,1)S(1)} %get-tuple-element.43.refs_0_), channel_id=1, source_target_pairs={{0,224},{32,0},{64,32},{96,64},{128,96},{160,128},{192,160},{224,1... | collective-permute-start | bytes 1572872 | tf_op jit(solution)/shard_map/ppermute | solution.py:618
  42.2 6.0 %route.1 = (bf16[384,320]{1,0:T(8,128)(2,1)S(1)}, bf16[256,256]{1,0:T(8,128)(2,1)}, bf16[2,192,128]{2,1,0:T(8,128)(2,1)}, bf16[2,256,256]{2,1,0:T(8,128)(2,1)}, bf16[2,256,256]{2,1,0:T(8,128)(2,1)}) custom-call(s32[1]{0:T(128)} %bitcast.rank_ref.refs_0_, bf16[512,128]{1,0:T(8,128)(2,1)S(1)} %get-tuple-element.41.refs_1_), custom_call_target="tpu_custom_call" | custom-call | tf_op jit(solution)/shard_map/route/pallas_call | solution.py:47
  54.3 7.6 %collective-permute-done.13.refs_3_ = bf16[64,4096]{1,0:T(8,128)(2,1)S(1)} collective-permute-done((bf16[64,4096]{1,0:T(8,128)(2,1)S(1)}, bf16[64,4096]{1,0:T(8,128)(2,1)S(1)}, u32[]{:S(2)}, u32[]{:S(2)}) %collective-permute-start.13) | collective-permute-done | bytes 524320 | tf_op jit(solution)/shard_map/ppermute | solution.py:618
  66.1 7.5 %all-to-all-start = ((bf16[16,24,4096]{2,1,0:T(8,128)(2,1)}), bf16[16,24,4096]{2,1,0:T(8,128)(2,1)}, u32[]{:S(2)}, u32[]{:S(2)}) async-start(bf16[16,24,4096]{2,1,0:T(8,128)(2,1)} %bitcast.13), calls=%async_computation | async-start | bytes 6291456 | tf_op jit(solution)/shard_map/all_to_all | solution.py:587
  76.8 10.0 %collective-permute-done.15.refs_1_ = bf16[64,4096]{1,0:T(8,128)(2,1)S(1)} collective-permute-done((bf16[64,4096]{1,0:T(8,128)(2,1)S(1)}, bf16[64,4096]{1,0:T(8,128)(2,1)S(1)}, u32[]{:S(2)}, u32[]{:S(2)}) %collective-permute-start.15) | collective-permute-done | bytes 524320 | tf_op jit(solution)/shard_map/ppermute | solution.py:618
  90.2 4.2 %collective-permute-done.17.refs_3_ = bf16[32,4096]{1,0:T(8,128)(2,1)S(1)} collective-permute-done((bf16[32,4096]{1,0:T(8,128)(2,1)S(1)}, bf16[32,4096]{1,0:T(8,128)(2,1)S(1)}, u32[]{:S(2)}, u32[]{:S(2)}) %collective-permute-start.17) | collective-permute-done | bytes 262176 | tf_op jit(solution)/shard_map/ppermute | solution.py:618
  96.5 11.9 %all-to-all-done = bf16[16,24,4096]{2,1,0:T(8,128)(2,1)} async-done(((bf16[16,24,4096]{2,1,0:T(8,128)(2,1)}), bf16[16,24,4096]{2,1,0:T(8,128)(2,1)}, u32[]{:S(2)}, u32[]{:S(2)}) %all-to-all-start) | async-done | bytes 3145760 | tf_op jit(solution)/shard_map/all_to_all | solution.py:587
  108.4 9.0 %all-to-all-start.1 = ((bf16[16,16,4096]{2,1,0:T(8,128)(2,1)}), bf16[16,16,4096]{2,1,0:T(8,128)(2,1)S(1)}, u32[]{:S(2)}, u32[]{:S(2)}) async-start(bf16[16,16,4096]{2,1,0:T(8,128)(2,1)} %bitcast.15), calls=%async_computation.1 | async-start | bytes 4194304 | tf_op jit(solution)/shard_map/all_to_all | solution.py:587
  117.5 15.1 %expert_near.1 = (bf16[16,8,4096]{2,1,0:T(8,128)(2,1)S(1)}, bf16[16,16,4096]{2,1,0:T(8,128)(2,1)S(1)}) custom-call(bf16[384,4096]{1,0:T(8,128)(2,1)} %bitcast.14.x, bf16[4096,384]{1,0:T(8,128)(2,1)} %bitcast.28, bf16[4096,384]{1,0:T(8,128)(2,1)} %collective-permute-done.10.g1, bf16[4096,384]{1,0:T(8,128)(2,1)} %bitcast.31, ...), custom_call_target="tpu_custom_call" | custom-call | tf_op jit(solution)/shard_map/expert_near/pallas_call | solution.py:47
  137.0 9.8 %expert_far.1 = bf16[16,16,4096]{2,1,0:T(8,128)(2,1)S(1)} custom-call(bf16[256,4096]{1,0:T(8,128)(2,1)S(1)} %bitcast.25, bf16[4096,384]{1,0:T(8,128)(2,1)} %bitcast.29, bf16[4096,384]{1,0:T(8,128)(2,1)} %collective-permute-done.10.g1, bf16[4096,384]{1,0:T(8,128)(2,1)} %bitcast.32, bf16[4096,384]{1,0:T(8,128)(2,1)} %collective-permute-done.11.u1, ...), custom_call_target="tpu_custom_call" | custom-call | tf_op jit(solution)/shard_map/expert_far/pallas_call | solution.py:47
  146.8 23.9 %all_to_all.25 = bf16[16,16,4096]{2,1,0:T(8,128)(2,1)} all-to-all(bf16[16,16,4096]{2,1,0:T(8,128)(2,1)S(1)} %expert_far.1), channel_id=1, replica_groups=mesh['pool'=8,'xy'=16,'core'=2] {'xy'}, dimensions={0} | all-to-all | bytes 4194304 | tf_op jit(solution)/shard_map/all_to_all | solution.py:587
  170.7 7.1 %all-to-all-start.3 = ((bf16[16,16,4096]{2,1,0:T(8,128)(2,1)}), bf16[16,16,4096]{2,1,0:T(8,128)(2,1)S(1)}, u32[]{:S(2)}, u32[]{:S(2)}) async-start(bf16[16,16,4096]{2,1,0:T(8,128)(2,1)} %copy-done), calls=%async_computation.3 | async-start | bytes 4194304 | tf_op jit(solution)/shard_map/all_to_all | solution.py:587
  177.9 4.4 %mix_far.1 = (f32[64,4096]{1,0:T(8,128)}, f32[128,4096]{1,0:T(8,128)S(1)}, bf16[32,4096]{1,0:T(8,128)(2,1)S(1)}, bf16[32,4096]{1,0:T(8,128)(2,1)S(1)}) custom-call(bf16[2,256,256]{2,1,0:T(8,128)(2,1)} %get-tuple-element.64.mix_ref, bf16[256,4096]{1,0:T(8,128)(2,1)} %bitcast.36), custom_call_target="tpu_custom_call" | custom-call | tf_op jit(solution)/shard_map/mix_far/pallas_call | solution.py:47
  185.5 6.8 %collective-permute-done.19.from_left_ref = bf16[32,4096]{1,0:T(8,128)(2,1)S(1)} collective-permute-done((bf16[32,4096]{1,0:T(8,128)(2,1)S(1)}, bf16[32,4096]{1,0:T(8,128)(2,1)S(1)}, u32[]{:S(2)}, u32[]{:S(2)}) %collective-permute-start.19) | collective-permute-done | bytes 262176 | tf_op jit(solution)/shard_map/ppermute | solution.py:618
  196.6 7.2 %all-to-all-start.4 = ((bf16[16,8,4096]{2,1,0:T(8,128)(2,1)}), bf16[16,8,4096]{2,1,0:T(8,128)(2,1)S(1)}, u32[]{:S(2)}, u32[]{:S(2)}) async-start(bf16[16,8,4096]{2,1,0:T(8,128)(2,1)} %copy-done.2), calls=%async_computation.4 | async-start | bytes 2097152 | tf_op jit(solution)/shard_map/all_to_all | solution.py:587
  203.9 3.6 %collective-permute-done.21.from_left = bf16[64,4096]{1,0:T(8,128)(2,1)} collective-permute-done((bf16[64,4096]{1,0:T(8,128)(2,1)}, bf16[64,4096]{1,0:T(8,128)(2,1)}, u32[]{:S(2)}, u32[]{:S(2)}) %collective-permute-start.21) | collective-permute-done | bytes 524320 | tf_op jit(solution)/shard_map/ppermute | solution.py:618
  208.0 3.4 %mix_second.1 = (bf16[64,4096]{1,0:T(8,128)(2,1)}, bf16[64,4096]{1,0:T(8,128)(2,1)}) custom-call(bf16[2,256,256]{2,1,0:T(8,128)(2,1)} %get-tuple-element.61.mix_ref.mix, bf16[256,4096]{1,0:T(8,128)(2,1)S(1)} %bitcast.23, bf16[64,4096]{1,0:T(8,128)(2,1)} %collective-permute-done.21.from_left, bf16[64,4096]{1,0:T(8,128)(2,1)} %collective-permute-done.22.from_right), custom_call_target="tpu_custom_call" | custom-call | tf_op jit(solution)/shard_map/mix_second/pallas_call | solution.py:47
  218.9 7.8 %collective-permute-done.23.from_left_ref = bf16[64,4096]{1,0:T(8,128)(2,1)} collective-permute-done((bf16[64,4096]{1,0:T(8,128)(2,1)}, bf16[64,4096]{1,0:T(8,128)(2,1)}, u32[]{:S(2)}, u32[]{:S(2)}) %collective-permute-start.23) | collective-permute-done | bytes 524320 | tf_op jit(solution)/shard_map/ppermute | solution.py:618
  231.7 7.2 %collective-permute-done.25.from_left_ref = bf16[64,4096]{1,0:T(8,128)(2,1)S(1)} collective-permute-done((bf16[64,4096]{1,0:T(8,128)(2,1)S(1)}, bf16[64,4096]{1,0:T(8,128)(2,1)S(1)}, u32[]{:S(2)}, u32[]{:S(2)}) %collective-permute-start.25) | collective-permute-done | bytes 524320 | tf_op jit(solution)/shard_map/ppermute | solution.py:618
  (70 shorter events, 61.8 us)
Async XLA Ops:
  0.6 50.3 %collective-permute-start.10 = (bf16[4096,384]{1,0:T(8,128)(2,1)}, bf16[4096,384]{1,0:T(8,128)(2,1)}, u32[]{:S(2)}, u32[]{:S(2)}) collective-permute-start(bf16[4096,384]{1,0:T(8,128)(2,1)} %bitcast.27), channel_id=1, source_target_pairs={{0,1},{1,0},{2,3},{3,2},{4,5},{5,4},{6,7},{7,6},{8,9},{9,8},{10,11... | collective-permute-start | bytes 9437192 | tf_op jit(solution)/shard_map/ppermute | solution.py:509
  0.7 50.2 %collective-permute-start.11 = (bf16[4096,384]{1,0:T(8,128)(2,1)}, bf16[4096,384]{1,0:T(8,128)(2,1)}, u32[]{:S(2)}, u32[]{:S(2)}) collective-permute-start(bf16[4096,384]{1,0:T(8,128)(2,1)} %bitcast.30), channel_id=1, source_target_pairs={{0,1},{1,0},{2,3},{3,2},{4,5},{5,4},{6,7},{7,6},{8,9},{9,8},{10,11... | collective-permute-start | bytes 9437192 | tf_op jit(solution)/shard_map/ppermute | solution.py:509
  1.2 49.7 %collective-permute-start.12 = (bf16[384,4096]{1,0:T(8,128)(2,1)}, bf16[384,4096]{1,0:T(8,128)(2,1)}, u32[]{:S(2)}, u32[]{:S(2)}) collective-permute-start(bf16[384,4096]{1,0:T(8,128)(2,1)} %bitcast.33), channel_id=1, source_target_pairs={{0,1},{1,0},{2,3},{3,2},{4,5},{5,4},{6,7},{7,6},{8,9},{9,8},{10,11... | collective-permute-start | bytes 9437192 | tf_op jit(solution)/shard_map/ppermute | solution.py:509
  3.2 10.4 %collective-permute-start = (bf16[64,1152]{1,0:T(8,128)(2,1)S(1)}, bf16[64,1152]{1,0:T(8,128)(2,1)S(1)}, u32[]{:S(2)}, u32[]{:S(2)}) collective-permute-start(bf16[64,1152]{1,0:T(8,128)(2,1)S(1)} %gather_block.1.refs_5_), channel_id=1, source_target_pairs={{0,32},{32,64},{64,96},{96,128},{128,160},{160,192},{192,224},{224... | collective-permute-start | bytes 442376 | tf_op jit(solution)/shard_map/ppermute | solution.py:473
  5.2 8.4 %collective-permute-start.1 = (bf16[64,1152]{1,0:T(8,128)(2,1)S(1)}, bf16[64,1152]{1,0:T(8,128)(2,1)S(1)}, u32[]{:S(2)}, u32[]{:S(2)}) collective-permute-start(bf16[64,1152]{1,0:T(8,128)(2,1)S(1)} %gather_block.1.refs_5_), channel_id=1, source_target_pairs={{0,224},{32,0},{64,32},{96,64},{128,96},{160,128},{192,160},{224,1... | collective-permute-start | bytes 442376 | tf_op jit(solution)/shard_map/ppermute | solution.py:474
  38.8 12.1 %collective-permute-start.8 = (bf16[64,4096]{1,0:T(8,128)(2,1)S(1)}, bf16[64,4096]{1,0:T(8,128)(2,1)S(1)}, u32[]{:S(2)}, u32[]{:S(2)}) collective-permute-start(bf16[64,4096]{1,0:T(8,128)(2,1)S(1)} %get-tuple-element.43.refs_0_), channel_id=1, source_target_pairs={{0,32},{32,64},{64,96},{96,128},{128,160},{160,192},{192,224},{224... | collective-permute-start | bytes 1572872 | tf_op jit(solution)/shard_map/ppermute | solution.py:618
  38.8 12.1 %collective-permute-start.9 = (bf16[64,4096]{1,0:T(8,128)(2,1)S(1)}, bf16[64,4096]{1,0:T(8,128)(2,1)S(1)}, u32[]{:S(2)}, u32[]{:S(2)}) collective-permute-start(bf16[64,4096]{1,0:T(8,128)(2,1)S(1)} %get-tuple-element.43.refs_0_), channel_id=1, source_target_pairs={{0,224},{32,0},{64,32},{96,64},{128,96},{160,128},{192,160},{224,1... | collective-permute-start | bytes 1572872 | tf_op jit(solution)/shard_map/ppermute | solution.py:618
  50.9 10.9 %collective-permute-start.13 = (bf16[64,4096]{1,0:T(8,128)(2,1)S(1)}, bf16[64,4096]{1,0:T(8,128)(2,1)S(1)}, u32[]{:S(2)}, u32[]{:S(2)}) collective-permute-start(bf16[64,4096]{1,0:T(8,128)(2,1)S(1)} %collective-permute-done.8.refs_1_), channel_id=1, source_target_pairs={{0,32},{32,64},{64,96},{96,128},{128,160},{160,192},{192,224},{224... | collective-permute-start | bytes 1572872 | tf_op jit(solution)/shard_map/ppermute | solution.py:618
  53.6 9.2 %collective-permute-start.14 = (bf16[64,4096]{1,0:T(8,128)(2,1)S(1)}, bf16[64,4096]{1,0:T(8,128)(2,1)S(1)}, u32[]{:S(2)}, u32[]{:S(2)}) collective-permute-start(bf16[64,4096]{1,0:T(8,128)(2,1)S(1)} %collective-permute-done.9.refs_2_), channel_id=1, source_target_pairs={{0,224},{32,0},{64,32},{96,64},{128,96},{160,128},{192,160},{224,1... | collective-permute-start | bytes 1572872 | tf_op jit(solution)/shard_map/ppermute | solution.py:618
  66.1 42.4 %all-to-all-start = ((bf16[16,24,4096]{2,1,0:T(8,128)(2,1)}), bf16[16,24,4096]{2,1,0:T(8,128)(2,1)}, u32[]{:S(2)}, u32[]{:S(2)}) async-start(bf16[16,24,4096]{2,1,0:T(8,128)(2,1)} %bitcast.13), calls=%async_computation | async-start | bytes 6291456 | tf_op jit(solution)/shard_map/all_to_all | solution.py:587
  73.6 13.2 %collective-permute-start.15 = (bf16[64,4096]{1,0:T(8,128)(2,1)S(1)}, bf16[64,4096]{1,0:T(8,128)(2,1)S(1)}, u32[]{:S(2)}, u32[]{:S(2)}) collective-permute-start(bf16[64,4096]{1,0:T(8,128)(2,1)S(1)} %collective-permute-done.13.refs_3_), channel_id=1, source_target_pairs={{0,32},{32,64},{64,96},{96,128},{128,160},{160,192},{192,224},{224... | collective-permute-start | bytes 1572872 | tf_op jit(solution)/shard_map/ppermute | solution.py:618
  75.3 12.1 %collective-permute-start.16 = (bf16[64,4096]{1,0:T(8,128)(2,1)S(1)}, bf16[64,4096]{1,0:T(8,128)(2,1)S(1)}, u32[]{:S(2)}, u32[]{:S(2)}) collective-permute-start(bf16[64,4096]{1,0:T(8,128)(2,1)S(1)} %collective-permute-done.14.refs_4_), channel_id=1, source_target_pairs={{0,224},{32,0},{64,32},{96,64},{128,96},{160,128},{192,160},{224,1... | collective-permute-start | bytes 1572872 | tf_op jit(solution)/shard_map/ppermute | solution.py:618
  86.8 7.7 %collective-permute-start.17 = (bf16[32,4096]{1,0:T(8,128)(2,1)S(1)}, bf16[32,4096]{1,0:T(8,128)(2,1)S(1)}, u32[]{:S(2)}, u32[]{:S(2)}) collective-permute-start(bf16[32,4096]{1,0:T(8,128)(2,1)S(1)} %slice.18), channel_id=1, source_target_pairs={{0,32},{32,64},{64,96},{96,128},{128,160},{160,192},{192,224},{224... | collective-permute-start | bytes 786440 | tf_op jit(solution)/shard_map/ppermute | solution.py:618
  108.4 28.6 %all-to-all-start.1 = ((bf16[16,16,4096]{2,1,0:T(8,128)(2,1)}), bf16[16,16,4096]{2,1,0:T(8,128)(2,1)S(1)}, u32[]{:S(2)}, u32[]{:S(2)}) async-start(bf16[16,16,4096]{2,1,0:T(8,128)(2,1)} %bitcast.15), calls=%async_computation.1 | async-start | bytes 4194304 | tf_op jit(solution)/shard_map/all_to_all | solution.py:587
  170.7 25.9 %all-to-all-start.3 = ((bf16[16,16,4096]{2,1,0:T(8,128)(2,1)}), bf16[16,16,4096]{2,1,0:T(8,128)(2,1)S(1)}, u32[]{:S(2)}, u32[]{:S(2)}) async-start(bf16[16,16,4096]{2,1,0:T(8,128)(2,1)} %copy-done), calls=%async_computation.3 | async-start | bytes 4194304 | tf_op jit(solution)/shard_map/all_to_all | solution.py:587
  182.2 10.0 %collective-permute-start.19 = (bf16[32,4096]{1,0:T(8,128)(2,1)S(1)}, bf16[32,4096]{1,0:T(8,128)(2,1)S(1)}, u32[]{:S(2)}, u32[]{:S(2)}) collective-permute-start(bf16[32,4096]{1,0:T(8,128)(2,1)S(1)} %get-tuple-element.70), channel_id=1, source_target_pairs={{0,32},{32,64},{64,96},{96,128},{128,160},{160,192},{192,224},{224... | collective-permute-start | bytes 786440 | tf_op jit(solution)/shard_map/ppermute | solution.py:618
  184.0 8.3 %collective-permute-start.20 = (bf16[32,4096]{1,0:T(8,128)(2,1)S(1)}, bf16[32,4096]{1,0:T(8,128)(2,1)S(1)}, u32[]{:S(2)}, u32[]{:S(2)}) collective-permute-start(bf16[32,4096]{1,0:T(8,128)(2,1)S(1)} %get-tuple-element.71), channel_id=1, source_target_pairs={{0,224},{32,0},{64,32},{96,64},{128,96},{160,128},{192,160},{224,1... | collective-permute-start | bytes 786440 | tf_op jit(solution)/shard_map/ppermute | solution.py:618
  193.4 14.0 %collective-permute-start.21 = (bf16[64,4096]{1,0:T(8,128)(2,1)}, bf16[64,4096]{1,0:T(8,128)(2,1)}, u32[]{:S(2)}, u32[]{:S(2)}) collective-permute-start(bf16[64,4096]{1,0:T(8,128)(2,1)} %get-tuple-element.72), channel_id=1, source_target_pairs={{0,32},{32,64},{64,96},{96,128},{128,160},{160,192},{192,224},{224... | collective-permute-start | bytes 1572872 | tf_op jit(solution)/shard_map/ppermute | solution.py:618
  195.0 13.0 %collective-permute-start.22 = (bf16[64,4096]{1,0:T(8,128)(2,1)}, bf16[64,4096]{1,0:T(8,128)(2,1)}, u32[]{:S(2)}, u32[]{:S(2)}) collective-permute-start(bf16[64,4096]{1,0:T(8,128)(2,1)} %get-tuple-element.73), channel_id=1, source_target_pairs={{0,224},{32,0},{64,32},{96,64},{128,96},{160,128},{192,160},{224,1... | collective-permute-start | bytes 1572872 | tf_op jit(solution)/shard_map/ppermute | solution.py:618
  196.6 18.1 %all-to-all-start.4 = ((bf16[16,8,4096]{2,1,0:T(8,128)(2,1)}), bf16[16,8,4096]{2,1,0:T(8,128)(2,1)S(1)}, u32[]{:S(2)}, u32[]{:S(2)}) async-start(bf16[16,8,4096]{2,1,0:T(8,128)(2,1)} %copy-done.2), calls=%async_computation.4 | async-start | bytes 2097152 | tf_op jit(solution)/shard_map/all_to_all | solution.py:587
  211.4 15.3 %collective-permute-start.23 = (bf16[64,4096]{1,0:T(8,128)(2,1)}, bf16[64,4096]{1,0:T(8,128)(2,1)}, u32[]{:S(2)}, u32[]{:S(2)}) collective-permute-start(bf16[64,4096]{1,0:T(8,128)(2,1)} %get-tuple-element.74), channel_id=1, source_target_pairs={{0,32},{32,64},{64,96},{96,128},{128,160},{160,192},{192,224},{224... | collective-permute-start | bytes 1572872 | tf_op jit(solution)/shard_map/ppermute | solution.py:618
  213.6 13.3 %collective-permute-start.24 = (bf16[64,4096]{1,0:T(8,128)(2,1)}, bf16[64,4096]{1,0:T(8,128)(2,1)}, u32[]{:S(2)}, u32[]{:S(2)}) collective-permute-start(bf16[64,4096]{1,0:T(8,128)(2,1)} %get-tuple-element.75), channel_id=1, source_target_pairs={{0,224},{32,0},{64,32},{96,64},{128,96},{160,128},{192,160},{224,1... | collective-permute-start | bytes 1572872 | tf_op jit(solution)/shard_map/ppermute | solution.py:618
  228.3 10.5 %collective-permute-start.25 = (bf16[64,4096]{1,0:T(8,128)(2,1)S(1)}, bf16[64,4096]{1,0:T(8,128)(2,1)S(1)}, u32[]{:S(2)}, u32[]{:S(2)}) collective-permute-start(bf16[64,4096]{1,0:T(8,128)(2,1)S(1)} %get-tuple-element.76), channel_id=1, source_target_pairs={{0,32},{32,64},{64,96},{96,128},{128,160},{160,192},{192,224},{224... | collective-permute-start | bytes 1572872 | tf_op jit(solution)/shard_map/ppermute | solution.py:618
  230.0 9.2 %collective-permute-start.26 = (bf16[64,4096]{1,0:T(8,128)(2,1)S(1)}, bf16[64,4096]{1,0:T(8,128)(2,1)S(1)}, u32[]{:S(2)}, u32[]{:S(2)}) collective-permute-start(bf16[64,4096]{1,0:T(8,128)(2,1)S(1)} %get-tuple-element.77), channel_id=1, source_target_pairs={{0,224},{32,0},{64,32},{96,64},{128,96},{160,128},{192,160},{224,1... | collective-permute-start | bytes 1572872 | tf_op jit(solution)/shard_map/ppermute | solution.py:618
  (14 other events, 120.1 us)
